TPU v7x, 128 devices: a whole 4x4x4 slice. The times are simulated.
128 devices in a mesh: ctx: 128 (over x, y, z, core).
Axes of the slice: x: 4, y: 4, z: 4, core: 2. Of those that a mesh axis runs over, the one named last changes fastest.
Arguments:
- queries: bfloat16 [32768, 2048], P('ctx')
- keys: bfloat16 [32768, 512], P('ctx')
- values: bfloat16 [32768, 512], P('ctx'), may hold values from -6 to 6
- cotangent: bfloat16 [32768, 2048], P('ctx'), may hold values from -180 to 180
- summary_positions: int32 [256], replicated, may hold values from 0 to 32767, as said below
Outputs:
- query_grad: bfloat16 [32768, 2048], P('ctx')
- key_grad: bfloat16 [32768, 512], P('ctx')
- value_gradient: bfloat16 [32768, 512], P('ctx')
Inputs may be any that keep to these rules, and one draw needn't show every extreme that they name: `summary_positions`: entry m lies in [m * 128, (m + 1) * 128); the first entry is 0 and the last is 32767.
All inputs are finite; a program needn't handle non-finite values.
Results may differ from a plain program's by a relative error of at most 0.012.
The roundings to bfloat16 on the way count: a program that leaves them out, or rounds other values in their place, can miss the bound.
Values may be sent and summed in bfloat16 or wider, within the bound.
No kernel may reach another device: no remote copies, remote signals or barrier semaphores. Data moves between devices by JAX's collectives and lax.ppermute only.
A program may use at most 128 MiB of HBM per device.

v0:
```python
import jax
import jax.numpy as jnp
from jax import lax
from jax.sharding import PartitionSpec as P

HEAD = 128
BAND_LENGTH = 1024


NEGATIVE = -1e30


def passed_along(block, axis, distance):
    devices = range(lax.axis_size(axis))
    route = [(i - distance, i) for i in devices if i - distance in devices]
    return lax.ppermute(block, axis, route)


def group_pass(
    group_query, group_cot, band_keys, band_vals, summ_keys, summ_vals, band_mask, summ_mask, scale
):
    band_score = (
        jnp.einsum("tgd,kd->gtk", group_query, band_keys, preferred_element_type=jnp.float32)
        * scale
    )
    band_score = jnp.where(band_mask[None], band_score, NEGATIVE)
    summ_score = (
        jnp.einsum("tgd,kd->gtk", group_query, summ_keys, preferred_element_type=jnp.float32)
        * scale
    )
    summ_score = jnp.where(summ_mask[None], summ_score, NEGATIVE)
    highest = jnp.maximum(jnp.max(band_score, -1), jnp.max(summ_score, -1))
    total = jnp.sum(jnp.exp(band_score - highest[..., None]), -1) + jnp.sum(
        jnp.exp(summ_score - highest[..., None]), -1
    )
    log_total = highest + jnp.log(total)
    band_prob = jnp.exp(band_score - log_total[..., None])
    summ_prob = jnp.exp(summ_score - log_total[..., None])
    band_half = band_prob.astype(jnp.bfloat16)
    summ_half = summ_prob.astype(jnp.bfloat16)
    attended = jnp.einsum("gtk,kd->tgd", band_half, band_vals, preferred_element_type=jnp.float32)
    attended = attended + jnp.einsum(
        "gtk,kd->tgd", summ_half, summ_vals, preferred_element_type=jnp.float32
    )
    attended = lax.optimization_barrier(attended.astype(jnp.bfloat16)).astype(jnp.float32)
    delta = jnp.sum(group_cot.astype(jnp.float32) * attended, -1).T
    band_dprob = jnp.einsum("tgd,kd->gtk", group_cot, band_vals, preferred_element_type=jnp.float32)
    summ_dprob = jnp.einsum("tgd,kd->gtk", group_cot, summ_vals, preferred_element_type=jnp.float32)
    band_dscore = (band_prob * (band_dprob - delta[..., None])).astype(jnp.bfloat16)
    summ_dscore = (summ_prob * (summ_dprob - delta[..., None])).astype(jnp.bfloat16)
    query_part = jnp.einsum(
        "gtk,kd->tgd", band_dscore, band_keys, preferred_element_type=jnp.float32
    )
    query_part = (
        query_part
        + jnp.einsum("gtk,kd->tgd", summ_dscore, summ_keys, preferred_element_type=jnp.float32)
    ) * scale
    key_part = (
        jnp.einsum("gtk,tgd->kd", band_dscore, group_query, preferred_element_type=jnp.float32)
        * scale
    )
    value_part = jnp.einsum("gtk,tgd->kd", band_half, group_cot, preferred_element_type=jnp.float32)
    summ_key_part = (
        jnp.einsum("gtk,tgd->kd", summ_dscore, group_query, preferred_element_type=jnp.float32)
        * scale
    )
    summ_value_part = jnp.einsum(
        "gtk,tgd->kd", summ_half, group_cot, preferred_element_type=jnp.float32
    )
    return (query_part, key_part, value_part, summ_key_part, summ_value_part, log_total, delta)


def body(queries, keys, values, cotangent, summary_positions):
    row_count = queries.shape[0]
    key_cols = keys.shape[1]
    kv_heads = key_cols // HEAD
    group = queries.shape[1] // key_cols
    scale = HEAD ** (-0.5)
    reach = BAND_LENGTH // row_count
    device_count = lax.axis_size("ctx")
    shard_index = lax.axis_index("ctx")
    first_row = shard_index * row_count
    per_device = summary_positions.shape[0] // device_count
    earlier_keys, earlier_vals = ([], [])
    for turn in range(reach):
        prev_keys, prev_vals = passed_along((keys, values), "ctx", reach - turn)
        earlier_keys.append(prev_keys)
        earlier_vals.append(prev_vals)
    band_keys = jnp.concatenate(earlier_keys + [keys], 0)
    band_vals = jnp.concatenate(earlier_vals + [values], 0)
    local_rows = (
        lax.dynamic_slice_in_dim(summary_positions, shard_index * per_device, per_device, 0)
        - first_row
    )
    local_keys = jnp.take(keys, local_rows, axis=0)
    local_vals = jnp.take(values, local_rows, axis=0)
    summ_keys, summ_vals = (
        lax.all_gather(local_keys, "ctx", axis=0, tiled=True),
        lax.all_gather(local_vals, "ctx", axis=0, tiled=True),
    )
    query_pos = first_row + jnp.arange(row_count, dtype=jnp.int32)
    band_pos = first_row - BAND_LENGTH + jnp.arange(BAND_LENGTH + row_count, dtype=jnp.int32)
    distance = query_pos[:, None] - band_pos[None, :]
    band_mask = (distance >= 0) & (distance < BAND_LENGTH) & (band_pos[None, :] >= 0)
    summ_mask = summary_positions[None, :] <= query_pos[:, None]
    query_parts, key_parts, value_parts, summ_kparts, summ_vparts, lse_parts, delta_parts = (
        [],
        [],
        [],
        [],
        [],
        [],
        [],
    )
    for head_group in range(kv_heads):
        query_cols = slice(head_group * group * HEAD, (head_group + 1) * group * HEAD)
        head_cols = slice(head_group * HEAD, (head_group + 1) * HEAD)
        group_query = queries[:, query_cols].reshape(row_count, group, HEAD)
        group_cot = cotangent[:, query_cols].reshape(row_count, group, HEAD)
        outcome = group_pass(
            group_query,
            group_cot,
            band_keys[:, head_cols],
            band_vals[:, head_cols],
            summ_keys[:, head_cols],
            summ_vals[:, head_cols],
            band_mask,
            summ_mask,
            scale,
        )
        query_parts.append(outcome[0].reshape(row_count, group * HEAD))
        key_parts.append(outcome[1])
        value_parts.append(outcome[2])
        summ_kparts.append(outcome[3])
        summ_vparts.append(outcome[4])
        lse_parts.append(outcome[5])
        delta_parts.append(outcome[6])
    query_grad = jnp.concatenate(query_parts, 1).astype(jnp.bfloat16)
    band_kgrad = jnp.concatenate(key_parts, 1)
    band_vgrad = jnp.concatenate(value_parts, 1)
    key_grad = band_kgrad[BAND_LENGTH:]
    value_gradient = band_vgrad[BAND_LENGTH:]
    for turn in range(reach):
        lower = turn * row_count
        back_keys, back_vals = (
            passed_along(
                band_kgrad[lower : lower + row_count].astype(jnp.bfloat16), "ctx", turn - reach
            ).astype(jnp.float32),
            passed_along(
                band_vgrad[lower : lower + row_count].astype(jnp.bfloat16), "ctx", turn - reach
            ).astype(jnp.float32),
        )
        key_grad = key_grad + back_keys
        value_gradient = value_gradient + back_vals
    summ_kterm = jnp.concatenate(summ_kparts, 1)
    summ_vterm = jnp.concatenate(summ_vparts, 1)
    share_keys, share_vals = (
        lax.psum_scatter(summ_kterm, "ctx", scatter_dimension=0, tiled=True),
        lax.psum_scatter(summ_vterm, "ctx", scatter_dimension=0, tiled=True),
    )
    key_grad = key_grad.at[local_rows].add(share_keys)
    value_gradient = value_gradient.at[local_rows].add(share_vals)
    return (query_grad, key_grad.astype(jnp.bfloat16), value_gradient.astype(jnp.bfloat16))


def solution(mesh):
    return jax.shard_map(
        body,
        mesh=mesh,
        in_specs=(P("ctx", None), P("ctx", None), P("ctx", None), P("ctx", None), P()),
        out_specs=(P("ctx", None), P("ctx", None), P("ctx", None)),
        check_vma=False,
    )
```

profile of v0, /device:TPU:1, one launch (start us, length us, event | category | flops | bytes accessed | tf_op | source)
XLA Modules:
  0.0 388.8 jit_solution(9783124111173024778)
XLA Ops:
  7.2 4.9 %collective-permute-start.3 = (bf16[256,512]{1,0:T(8,128)(2,1)}, bf16[256,512]{1,0:T(8,128)(2,1)}, u32[]{:S(2)}, u32[]{:S(2)}) collective-permute-start(bf16[256,512]{1,0:T(8,128)(2,1)} %param.8), channel_id=1, source_target_pairs={{0,1},{1,2},{2,3},{3,4},{4,5},{5,6},{6,7},{7,8},{8,9},{9,10},{10,1... | collective-permute-start | bytes 786440 | tf_op jit(solution)/shard_map/ppermute | solution.py:16
  12.2 4.2 %collective-permute-start.2 = (bf16[256,512]{1,0:T(8,128)(2,1)}, bf16[256,512]{1,0:T(8,128)(2,1)}, u32[]{:S(2)}, u32[]{:S(2)}) collective-permute-start(bf16[256,512]{1,0:T(8,128)(2,1)} %param.8), channel_id=1, source_target_pairs={{0,2},{1,3},{2,4},{3,5},{4,6},{5,7},{6,8},{7,9},{8,10},{9,11},{10,... | collective-permute-start | bytes 786440 | tf_op jit(solution)/shard_map/ppermute | solution.py:16
  16.4 3.3 collective-permute-start.6
  19.7 2.7 collective-permute-start.5
  22.4 4.3 %collective-permute-start.4 = (bf16[256,512]{1,0:T(8,128)(2,1)}, bf16[256,512]{1,0:T(8,128)(2,1)}, u32[]{:S(2)}, u32[]{:S(2)}) collective-permute-start(bf16[256,512]{1,0:T(8,128)(2,1)} %param.9), channel_id=1, source_target_pairs={{0,4},{1,5},{2,6},{3,7},{4,8},{5,9},{6,10},{7,11},{8,12},{9,13},{1... | collective-permute-start | bytes 786440 | tf_op jit(solution)/shard_map/ppermute | solution.py:16
  27.5 1.5 gather_fusion.1
  29.0 1.5 gather_fusion
  31.5 41.0 %all-gather = bf16[128,2,512]{2,1,0:T(2,128)(2,1)S(1)} all-gather(bf16[1,2,512]{2,1,0:T(2,128)(2,1)S(1)} %get-tuple-element.28), channel_id=1, replica_groups=mesh['ctx'=128] {'ctx'}, dimensions={0}, use_global_device_ids=true | all-gather | bytes 264192 | tf_op jit(solution)/shard_map/all_gather | solution.py:98
  72.6 1.4 fusion.98
  75.6 1.3 fusion.103
  76.9 1.4 fusion.107
  78.3 1.6 fusion.33
  80.7 33.2 %all-gather.1 = bf16[128,2,512]{2,1,0:T(2,128)(2,1)S(1)} all-gather(bf16[1,2,512]{2,1,0:T(2,128)(2,1)S(1)} %get-tuple-element.27), channel_id=1, replica_groups=mesh['ctx'=128] {'ctx'}, dimensions={0}, use_global_device_ids=true | all-gather | bytes 264192 | tf_op jit(solution)/shard_map/all_gather | solution.py:99
  114.3 1.1 copy.343
  115.4 1.1 copy.349
  116.6 3.0 collective-permute-start.7
  120.6 2.6 collective-permute-start.1
  124.1 4.5 %collective-permute-start = (bf16[256,512]{1,0:T(8,128)(2,1)}, bf16[256,512]{1,0:T(8,128)(2,1)S(1)}, u32[]{:S(2)}, u32[]{:S(2)}) collective-permute-start(bf16[256,512]{1,0:T(8,128)(2,1)} %param.8), channel_id=1, source_target_pairs={{0,4},{1,5},{2,6},{3,7},{4,8},{5,9},{6,10},{7,11},{8,12},{9,13},{1... | collective-permute-start | bytes 786440 | tf_op jit(solution)/shard_map/ppermute | solution.py:16
  130.6 3.3 collective-permute-done
  139.2 1.0 fusion.50
  141.4 1.0 convolution_bitcast_fusion
  142.4 1.1 fusion.1
  146.7 1.0 fusion.52
  149.1 1.1 fusion.89
  150.2 1.0 convolution_bitcast_fusion.2
  151.2 1.1 fusion.5
  152.3 1.2 fusion.102
  155.9 1.0 fusion.51
  158.4 1.0 fusion.90
  159.4 1.0 convolution_bitcast_fusion.1
  160.4 1.1 fusion.3
  162.5 1.0 copy-done.3
  164.8 1.0 convolution_bitcast_fusion.15
  165.8 1.0 fusion.53
  168.1 1.1 fusion.88
  169.2 1.0 convolution_bitcast_fusion.3
  170.2 1.1 fusion.7
  173.3 1.2 fusion.13
  175.5 1.2 fusion.95
  176.7 1.7 pad_maximum_fusion
  178.3 1.2 fusion.94
  179.6 1.7 pad_maximum_fusion.1
  182.7 1.5 fusion.43
  185.1 2.6 fusion.44
  188.6 1.5 fusion.42
  190.3 2.3 fusion.97
  192.6 1.3 collective-permute-start.8
  193.9 3.5 collective-permute-start.11
  197.4 1.3 collective-permute-start.10
  198.7 1.4 collective-permute-start.9
  200.2 1.0 fusion.96
  201.2 1.4 collective-permute-start.12
  202.7 2.0 pad_maximum_fusion.3
  204.7 1.1 pad_maximum_fusion.2
  206.2 2.7 collective-permute-start.15
  208.9 5.6 %collective-permute-done.11 = bf16[256,512]{0,1:T(8,128)(2,1)} collective-permute-done((bf16[256,512]{0,1:T(8,128)(2,1)}, bf16[256,512]{0,1:T(8,128)(2,1)}, u32[]{:S(2)}, u32[]{:S(2)}) %collective-permute-start.11) | collective-permute-done | bytes 262176 | tf_op jit(solution)/shard_map/ppermute | solution.py:16
  214.5 1.3 collective-permute-start.14
  215.8 1.3 collective-permute-start.13
  217.1 1.5 fusion.75
  218.8 15.7 %collective-permute-done.15 = bf16[256,512]{0,1:T(8,128)(2,1)S(1)} collective-permute-done((bf16[256,512]{0,1:T(8,128)(2,1)}, bf16[256,512]{0,1:T(8,128)(2,1)S(1)}, u32[]{:S(2)}, u32[]{:S(2)}) %collective-permute-start.15) | collective-permute-done | bytes 262176 | tf_op jit(solution)/shard_map/ppermute | solution.py:16
  235.0 1.2 fusion.72
  236.4 140.0 %all-reduce.5.cloned.1.call-done = (f32[256,512]{0,1:T(8,128)}, f32[256,512]{0,1:T(8,128)}) async-done(((f32[256,512]{0,1:T(8,128)}, f32[256,512]{0,1:T(8,128)}), (f32[256,512]{0,1:T(8,128)}, f32[256,512]{0,1:T(8,128)})) %all-reduce.5.cloned.1.call-update) | async-done | bytes 1048592
  376.4 1.1 constant_dynamic-slice_fusion.1
  377.5 1.1 constant_dynamic-slice_fusion
  (165 shorter events, 37.4 us)
Async XLA Ops:
  7.2 369.2 %all-reduce.5.cloned.1.call-start = ((), (), s32[]{:S(2)}) async-start(), calls=%async_computation | async-start | bytes 2097152
  7.2 127.8 %collective-permute-start.3 = (bf16[256,512]{1,0:T(8,128)(2,1)}, bf16[256,512]{1,0:T(8,128)(2,1)}, u32[]{:S(2)}, u32[]{:S(2)}) collective-permute-start(bf16[256,512]{1,0:T(8,128)(2,1)} %param.8), channel_id=1, source_target_pairs={{0,1},{1,2},{2,3},{3,4},{4,5},{5,6},{6,7},{7,8},{8,9},{9,10},{10,1... | collective-permute-start | bytes 786440 | tf_op jit(solution)/shard_map/ppermute | solution.py:16
  12.2 121.8 %collective-permute-start.2 = (bf16[256,512]{1,0:T(8,128)(2,1)}, bf16[256,512]{1,0:T(8,128)(2,1)}, u32[]{:S(2)}, u32[]{:S(2)}) collective-permute-start(bf16[256,512]{1,0:T(8,128)(2,1)} %param.8), channel_id=1, source_target_pairs={{0,2},{1,3},{2,4},{3,5},{4,6},{5,7},{6,8},{7,9},{8,10},{9,11},{10,... | collective-permute-start | bytes 786440 | tf_op jit(solution)/shard_map/ppermute | solution.py:16
  16.4 107.7 %collective-permute-start.6 = (bf16[256,512]{1,0:T(8,128)(2,1)}, bf16[256,512]{1,0:T(8,128)(2,1)}, u32[]{:S(2)}, u32[]{:S(2)}) collective-permute-start(bf16[256,512]{1,0:T(8,128)(2,1)} %param.9), channel_id=1, source_target_pairs={{0,2},{1,3},{2,4},{3,5},{4,6},{5,7},{6,8},{7,9},{8,10},{9,11},{10,... | collective-permute-start | bytes 786440 | tf_op jit(solution)/shard_map/ppermute | solution.py:16
  19.7 100.9 %collective-permute-start.5 = (bf16[256,512]{1,0:T(8,128)(2,1)}, bf16[256,512]{1,0:T(8,128)(2,1)}, u32[]{:S(2)}, u32[]{:S(2)}) collective-permute-start(bf16[256,512]{1,0:T(8,128)(2,1)} %param.9), channel_id=1, source_target_pairs={{0,3},{1,4},{2,5},{3,6},{4,7},{5,8},{6,9},{7,10},{8,11},{9,12},{10... | collective-permute-start | bytes 786440 | tf_op jit(solution)/shard_map/ppermute | solution.py:16
  22.4 94.2 %collective-permute-start.4 = (bf16[256,512]{1,0:T(8,128)(2,1)}, bf16[256,512]{1,0:T(8,128)(2,1)}, u32[]{:S(2)}, u32[]{:S(2)}) collective-permute-start(bf16[256,512]{1,0:T(8,128)(2,1)} %param.9), channel_id=1, source_target_pairs={{0,4},{1,5},{2,6},{3,7},{4,8},{5,9},{6,10},{7,11},{8,12},{9,13},{1... | collective-permute-start | bytes 786440 | tf_op jit(solution)/shard_map/ppermute | solution.py:16
  72.6 4.3 %copy-start.16 = (bf16[256,512]{1,0:T(8,128)(2,1)}, bf16[256,512]{1,0:T(8,128)(2,1)S(1)}, u32[]{:S(2)}) copy-start(bf16[256,512]{1,0:T(8,128)(2,1)S(1)} %reshape.253) | copy-start | bytes 786436
  74.1 2.7 copy-start.6
  74.3 2.6 copy-start.8
  74.4 3.8 copy-start.10
  74.6 0.7 copy-start.12
  75.3 4.6 %copy-start.22 = (bf16[256,2048]{1,0:T(8,128)(2,1)S(1)}, bf16[256,2048]{1,0:T(8,128)(2,1)}, u32[]{:S(2)}) copy-start(bf16[256,2048]{1,0:T(8,128)(2,1)} %param.10) | copy-start | bytes 3145732
  114.1 33.8 %copy-start.18 = (bf16[256,512]{1,0:T(8,128)(2,1)}, bf16[256,512]{1,0:T(8,128)(2,1)S(1)}, u32[]{:S(2)}) copy-start(bf16[256,512]{1,0:T(8,128)(2,1)S(1)} %reshape.255) | copy-start | bytes 786436
  116.5 19.4 %copy-start.32 = (bf16[256,512]{1,0:T(8,128)(2,1)S(1)}, bf16[256,512]{1,0:T(8,128)(2,1)}, u32[]{:S(2)}) copy-start(bf16[256,512]{1,0:T(8,128)(2,1)} %param.8) | copy-start | bytes 786436
  116.5 19.4 %copy-start.5 = (pred[256,1280]{0,1:T(8,128)(4,1)S(1)}, pred[256,1280]{0,1:T(8,128)(4,1)}, u32[]{:S(2)}) copy-start(pred[256,1280]{0,1:T(8,128)(4,1)} %fusion.33) | copy-start | bytes 983044
  116.6 19.4 %copy-start.13 = (bf16[256,512]{0,1:T(8,128)(2,1)S(1)}, bf16[256,512]{0,1:T(8,128)(2,1)}, u32[]{:S(2)}) copy-start(bf16[256,512]{0,1:T(8,128)(2,1)} %copy-done.12) | copy-start | bytes 786436
  116.6 13.0 %collective-permute-start.7 = (bf16[256,512]{1,0:T(8,128)(2,1)}, bf16[256,512]{1,0:T(8,128)(2,1)S(1)}, u32[]{:S(2)}, u32[]{:S(2)}) collective-permute-start(bf16[256,512]{1,0:T(8,128)(2,1)} %param.9), channel_id=1, source_target_pairs={{0,1},{1,2},{2,3},{3,4},{4,5},{5,6},{6,7},{7,8},{8,9},{9,10},{10,1... | collective-permute-start | bytes 786440 | tf_op jit(solution)/shard_map/ppermute | solution.py:16
  120.6 13.4 %collective-permute-start.1 = (bf16[256,512]{1,0:T(8,128)(2,1)}, bf16[256,512]{1,0:T(8,128)(2,1)S(1)}, u32[]{:S(2)}, u32[]{:S(2)}) collective-permute-start(bf16[256,512]{1,0:T(8,128)(2,1)} %param.8), channel_id=1, source_target_pairs={{0,3},{1,4},{2,5},{3,6},{4,7},{5,8},{6,9},{7,10},{8,11},{9,12},{10... | collective-permute-start | bytes 786440 | tf_op jit(solution)/shard_map/ppermute | solution.py:16
  124.1 9.8 %collective-permute-start = (bf16[256,512]{1,0:T(8,128)(2,1)}, bf16[256,512]{1,0:T(8,128)(2,1)S(1)}, u32[]{:S(2)}, u32[]{:S(2)}) collective-permute-start(bf16[256,512]{1,0:T(8,128)(2,1)} %param.8), channel_id=1, source_target_pairs={{0,4},{1,5},{2,6},{3,7},{4,8},{5,9},{6,10},{7,11},{8,12},{9,13},{1... | collective-permute-start | bytes 786440 | tf_op jit(solution)/shard_map/ppermute | solution.py:16
  136.0 45.3 %copy-start.14 = (bf16[1280,512]{1,0:T(8,128)(2,1)}, bf16[1280,512]{1,0:T(8,128)(2,1)S(1)}, u32[]{:S(2)}) copy-start(bf16[1280,512]{1,0:T(8,128)(2,1)S(1)} %constant_dynamic-update-slice_fusion) | copy-start | bytes 3932164
  140.2 1.0 copy-start.17
  142.4 1.1 copy-start.11
  151.2 1.1 copy-start.9
  152.3 1.2 copy-start.4
  153.7 1.0 copy-start.19
  160.4 1.1 copy-start.7
  161.5 11.7 %copy-start = (bf16[4,256,1280]{1,2,0:T(8,128)(2,1)}, bf16[4,256,1280]{1,2,0:T(8,128)(2,1)S(1)}, u32[]{:S(2)}) copy-start(bf16[4,256,1280]{1,2,0:T(8,128)(2,1)S(1)} %fusion.3) | copy-start | bytes 7864324
  161.5 2.0 copy-start.3
  171.3 3.2 copy-start.1
  181.3 1.4 copy-start.20
  184.2 4.4 %copy-start.2 = (bf16[4,256,1280]{1,2,0:T(8,128)(2,1)S(1)}, bf16[4,256,1280]{1,2,0:T(8,128)(2,1)}, u32[]{:S(2)}) copy-start(bf16[4,256,1280]{1,2,0:T(8,128)(2,1)} %copy-done.1) | copy-start | bytes 7864324
  184.2 4.4 %copy-start.21 = (f32[128,4,256]{2,0,1:T(8,128)S(1)}, f32[128,4,256]{2,0,1:T(8,128)}, u32[]{:S(2)}) copy-start(f32[128,4,256]{2,0,1:T(8,128)} %fusion.88) | copy-start | bytes 1572868
  190.1 10.1 %copy-start.15 = (bf16[1280,512]{0,1:T(8,128)(2,1)S(1)}, bf16[1280,512]{0,1:T(8,128)(2,1)}, u32[]{:S(2)}) copy-start(bf16[1280,512]{0,1:T(8,128)(2,1)} %fusion.94) | copy-start | bytes 3932164
  190.1 12.5 %copy-start.26 = (f32[256,128]{0,1:T(8,128)S(1)}, f32[256,128]{0,1:T(8,128)}, u32[]{:S(2)}) copy-start(f32[256,128]{0,1:T(8,128)} %fusion.55) | copy-start | bytes 393220
  190.1 12.5 %copy-start.27 = (f32[256,128]{0,1:T(8,128)S(1)}, f32[256,128]{0,1:T(8,128)}, u32[]{:S(2)}) copy-start(f32[256,128]{0,1:T(8,128)} %fusion.56) | copy-start | bytes 393220
  190.1 12.5 %copy-start.28 = (f32[256,128]{0,1:T(8,128)S(1)}, f32[256,128]{0,1:T(8,128)}, u32[]{:S(2)}) copy-start(f32[256,128]{0,1:T(8,128)} %fusion.54) | copy-start | bytes 393220
  190.1 12.5 %copy-start.29 = (f32[256,128]{0,1:T(8,128)S(1)}, f32[256,128]{0,1:T(8,128)}, u32[]{:S(2)}) copy-start(f32[256,128]{0,1:T(8,128)} %convolution_bitcast_fusion.12) | copy-start | bytes 393220
  190.1 12.5 %copy-start.30 = (f32[256,128]{0,1:T(8,128)S(1)}, f32[256,128]{0,1:T(8,128)}, u32[]{:S(2)}) copy-start(f32[256,128]{0,1:T(8,128)} %convolution_bitcast_fusion.14) | copy-start | bytes 393220
  190.2 12.5 %copy-start.31 = (f32[256,128]{0,1:T(8,128)S(1)}, f32[256,128]{0,1:T(8,128)}, u32[]{:S(2)}) copy-start(f32[256,128]{0,1:T(8,128)} %convolution_bitcast_fusion.13) | copy-start | bytes 393220
  192.6 13.6 %collective-permute-start.8 = (bf16[256,512]{0,1:T(8,128)(2,1)}, bf16[256,512]{0,1:T(8,128)(2,1)}, u32[]{:S(2)}, u32[]{:S(2)}) collective-permute-start(bf16[256,512]{0,1:T(8,128)(2,1)} %get-tuple-element.15), channel_id=1, source_target_pairs={{4,0},{5,1},{6,2},{7,3},{8,4},{9,5},{10,6},{11,7},{12,8},{13,9},{1... | collective-permute-start | bytes 786440 | tf_op jit(solution)/shard_map/ppermute | solution.py:16
  193.9 20.6 %collective-permute-start.11 = (bf16[256,512]{0,1:T(8,128)(2,1)}, bf16[256,512]{0,1:T(8,128)(2,1)}, u32[]{:S(2)}, u32[]{:S(2)}) collective-permute-start(bf16[256,512]{0,1:T(8,128)(2,1)} %get-tuple-element.16), channel_id=1, source_target_pairs={{1,0},{2,1},{3,2},{4,3},{5,4},{6,5},{7,6},{8,7},{9,8},{10,9},{11,1... | collective-permute-start | bytes 786440 | tf_op jit(solution)/shard_map/ppermute | solution.py:16
  197.4 18.4 %collective-permute-start.10 = (bf16[256,512]{0,1:T(8,128)(2,1)}, bf16[256,512]{0,1:T(8,128)(2,1)}, u32[]{:S(2)}, u32[]{:S(2)}) collective-permute-start(bf16[256,512]{0,1:T(8,128)(2,1)} %get-tuple-element.17), channel_id=1, source_target_pairs={{2,0},{3,1},{4,2},{5,3},{6,4},{7,5},{8,6},{9,7},{10,8},{11,9},{12,... | collective-permute-start | bytes 786440 | tf_op jit(solution)/shard_map/ppermute | solution.py:16
  198.7 6.0 %copy-start.23 = (bf16[256,512]{1,0:T(8,128)(2,1)S(1)}, bf16[256,512]{1,0:T(8,128)(2,1)}, u32[]{:S(2)}) copy-start(bf16[256,512]{1,0:T(8,128)(2,1)} %copy.234) | copy-start | bytes 786436
  198.7 6.0 %copy-start.24 = (bf16[256,512]{1,0:T(8,128)(2,1)S(1)}, bf16[256,512]{1,0:T(8,128)(2,1)}, u32[]{:S(2)}) copy-start(bf16[256,512]{1,0:T(8,128)(2,1)} %copy.232) | copy-start | bytes 786436
  198.7 6.0 %copy-start.25 = (bf16[256,512]{1,0:T(8,128)(2,1)S(1)}, bf16[256,512]{1,0:T(8,128)(2,1)}, u32[]{:S(2)}) copy-start(bf16[256,512]{1,0:T(8,128)(2,1)} %copy.233) | copy-start | bytes 786436
  198.7 18.4 %collective-permute-start.9 = (bf16[256,512]{0,1:T(8,128)(2,1)}, bf16[256,512]{0,1:T(8,128)(2,1)}, u32[]{:S(2)}, u32[]{:S(2)}) collective-permute-start(bf16[256,512]{0,1:T(8,128)(2,1)} %get-tuple-element.18), channel_id=1, source_target_pairs={{3,0},{4,1},{5,2},{6,3},{7,4},{8,5},{9,6},{10,7},{11,8},{12,9},{13... | collective-permute-start | bytes 786440 | tf_op jit(solution)/shard_map/ppermute | solution.py:16
  201.2 14.6 %copy-start.33 = (bf16[256,512]{0,1:T(8,128)(2,1)S(1)}, bf16[256,512]{0,1:T(8,128)(2,1)}, u32[]{:S(2)}) copy-start(bf16[256,512]{0,1:T(8,128)(2,1)} %get-tuple-element.14) | copy-start | bytes 786436
  201.2 17.6 %collective-permute-start.12 = (bf16[256,512]{0,1:T(8,128)(2,1)}, bf16[256,512]{0,1:T(8,128)(2,1)S(1)}, u32[]{:S(2)}, u32[]{:S(2)}) collective-permute-start(bf16[256,512]{0,1:T(8,128)(2,1)} %get-tuple-element.11), channel_id=1, source_target_pairs={{4,0},{5,1},{6,2},{7,3},{8,4},{9,5},{10,6},{11,7},{12,8},{13,9},{1... | collective-permute-start | bytes 786440 | tf_op jit(solution)/shard_map/ppermute | solution.py:16
  206.2 28.4 %collective-permute-start.15 = (bf16[256,512]{0,1:T(8,128)(2,1)}, bf16[256,512]{0,1:T(8,128)(2,1)S(1)}, u32[]{:S(2)}, u32[]{:S(2)}) collective-permute-start(bf16[256,512]{0,1:T(8,128)(2,1)} %get-tuple-element.12), channel_id=1, source_target_pairs={{1,0},{2,1},{3,2},{4,3},{5,4},{6,5},{7,6},{8,7},{9,8},{10,9},{11,1... | collective-permute-start | bytes 786440 | tf_op jit(solution)/shard_map/ppermute | solution.py:16
  214.5 20.5 %collective-permute-start.14 = (bf16[256,512]{0,1:T(8,128)(2,1)}, bf16[256,512]{0,1:T(8,128)(2,1)S(1)}, u32[]{:S(2)}, u32[]{:S(2)}) collective-permute-start(bf16[256,512]{0,1:T(8,128)(2,1)} %get-tuple-element.13), channel_id=1, source_target_pairs={{2,0},{3,1},{4,2},{5,3},{6,4},{7,5},{8,6},{9,7},{10,8},{11,9},{12,... | collective-permute-start | bytes 786440 | tf_op jit(solution)/shard_map/ppermute | solution.py:16
  215.8 19.2 %collective-permute-start.13 = (bf16[256,512]{0,1:T(8,128)(2,1)S(1)}, bf16[256,512]{0,1:T(8,128)(2,1)S(1)}, u32[]{:S(2)}, u32[]{:S(2)}) collective-permute-start(bf16[256,512]{0,1:T(8,128)(2,1)S(1)} %copy-done.33), channel_id=1, source_target_pairs={{3,0},{4,1},{5,2},{6,3},{7,4},{8,5},{9,6},{10,7},{11,8},{12,9},{13... | collective-permute-start | bytes 786440 | tf_op jit(solution)/shard_map/ppermute | solution.py:16
Sparse Core Ops, SparseCore 0:
  204.8 171.5 all-reduce.4
where the time goes:
time: 390 us; the launch traced here: 389 us
  waiting for transfers between devices  165 us (42%)
  blocking collectives  74.2 us (19%)
  starting transfers between devices  43.8 us (11%)
  matrix products  43.2 us (11%)
  local copies, waits for them, and re-layouts  25.2 us (6%)
  other arithmetic  21.8 us (6%)
  between operations  15.2 us (4%)
    unnamed x2, waiting for transfers between devices  140 us
    ppermute x16, starting transfers between devices, passed_along(): return lax.ppermute(block, axis, route)  43.7 us
    all_gather x1, blocking collectives, body(): lax.all_gather(local_keys, 'ctx', axis=0, tiled=True)  41 us
    all_gather x1, blocking collectives, body(): lax.all_gather(local_vals, 'ctx', axis=0, tiled=True)  33.2 us
    ppermute x16, waiting for transfers between devices, passed_along(): return lax.ppermute(block, axis, route)  25.5 us
    unnamed x88, local copies, waits for them, and re-layouts  12.2 us
  transfers between devices with their start and end apart: 17, of which 6 were waited for; matrix products, arithmetic and copies ran while one was open for 7% of the time, Pallas kernels for 0%

commit v1 on v0

v1 whole, which is shorter than its diff:
```python
import functools

import jax
import jax.numpy as jnp
from jax import lax
from jax.experimental import pallas as pl
from jax.experimental.pallas import tpu as pltpu
from jax.sharding import PartitionSpec as P

HEAD = 128
ROWS = 256
SPAN = 1792
GATHER_FLOPS = 6_000_000_000
UNPACK_FLOPS = 40_000_000_000
BIG = 3e38
NEG = -1e30
SCALE = HEAD**-0.5
LOG2E = 1.4426950408889634
F32 = jnp.float32
BF = jnp.bfloat16
VM = pl.BlockSpec(memory_space=pltpu.VMEM)
SM = pl.BlockSpec(memory_space=pltpu.SMEM)
ANY = pl.BlockSpec(memory_space=pltpu.HBM)


def dot(a, b):
    return jnp.dot(a, b, preferred_element_type=F32)


def place():
    index = lax.axis_index("ctx")
    return index, index // 2, index % 2


def window(start, size):
    return pl.ds(pl.multiple_of(start, size), size)


def run(copies):
    for copy in copies:
        copy.start()
    for copy in copies:
        copy.wait()


def pack_kernel(pos_ref, k_ref, v_ref, q_hbm, d_hbm, own_ref, send_ref, block_ref, qd_ref, sem):
    index, _, core = place()
    copies = []
    for i, ref in enumerate((q_hbm, d_hbm)):
        src = ref.at[:, window((1 - core) * 1024, 1024)]
        copies.append(pltpu.make_async_copy(src, qd_ref.at[:, i * 1024 : (i + 1) * 1024], sem.at[i]))
        copies[-1].start()
    for out, which in ((own_ref, core), (send_ref, 1 - core)):
        for g in range(2):
            cols = window((2 * which + g) * HEAD, HEAD)
            out[g, :, :HEAD] = k_ref[:, cols]
            out[g, :, HEAD:] = v_ref[:, cols]
    slot = lax.broadcasted_iota(jnp.int32, (8, ROWS), 0)
    row = lax.broadcasted_iota(jnp.int32, (8, ROWS), 1)
    first = pos_ref[2 * index] - index * ROWS
    second = pos_ref[2 * index + 1] - index * ROWS
    wanted = jnp.where(slot % 2 == 0, first, second)
    tiles = []
    for which in range(2):
        tile = jnp.zeros((8, HEAD), F32)
        for g in range(2):
            for i, ref in enumerate((k_ref, v_ref)):
                pick = ((row == wanted) & (slot // 2 == 2 * g + i)).astype(F32).astype(BF)
                head = 2 * which + g
                tile = tile + dot(pick, ref[:, head * HEAD : (head + 1) * HEAD])
        tiles.append(tile.astype(BF))
    for device in range(block_ref.shape[0]):
        block_ref[device] = tiles[device % 2]
    for copy in copies:
        copy.wait()


def pack(pos, keys, values, queries, cotangent):
    shape = jax.ShapeDtypeStruct
    return pl.pallas_call(
        pack_kernel,
        in_specs=[SM, VM, VM, ANY, ANY],
        out_specs=[VM] * 4,
        out_shape=[
            shape((2, ROWS, 2 * HEAD), BF),
            shape((2, ROWS, 2 * HEAD), BF),
            shape((128, 8, HEAD), BF),
            shape((ROWS, 2048), BF),
        ],
        scratch_shapes=[pltpu.SemaphoreType.DMA((2,))],
        compiler_params=pltpu.CompilerParams(vmem_limit_bytes=60 << 20),
        name="pack",
    )(pos, keys, values, queries, cotangent)


def unpack_kernel(pos_ref, summ_ref, sk0_ref, sk1_ref, posb_ref, f_sc, t_sc):
    f_sc[...] = summ_ref[...].astype(F32)
    for g, out in enumerate((sk0_ref, sk1_ref)):
        for i in range(2):
            for r in range(2):
                slots = pl.ds(4 * g + 2 * i + r, 128, stride=8)
                t_sc[pl.ds(r, 128, stride=2), :] = f_sc[slots, :]
            out[:, i * HEAD : (i + 1) * HEAD] = t_sc[...].astype(BF)
    for i in range(2):
        row = jnp.broadcast_to(pos_ref[i : i + 1, :].astype(F32), (HEAD, HEAD))
        posb_ref[i * HEAD : (i + 1) * HEAD, :] = row.T


def unpack(pos, summ):
    shape = jax.ShapeDtypeStruct
    return pl.pallas_call(
        unpack_kernel,
        in_specs=[VM, VM],
        out_specs=[VM] * 3,
        out_shape=[shape((ROWS, 256), BF), shape((ROWS, 256), BF), shape((ROWS, HEAD), F32)],
        scratch_shapes=[pltpu.VMEM((1024, HEAD), F32), pltpu.VMEM((ROWS, HEAD), F32)],
        compiler_params=pltpu.CompilerParams(vmem_limit_bytes=60 << 20),
        cost_estimate=pl.CostEstimate(flops=UNPACK_FLOPS, bytes_accessed=1_000_000, transcendentals=0),
        name="unpack",
    )(pos, summ)


def fold(x, op):
    return op(x.reshape(x.shape[0] // 8, 8, x.shape[1]), axis=0)


def attend_kernel(g, pos_ref, q_hbm, d_hbm, qd_hbm, kv2, kv1, kv0, summ, *rest):
    before, rest = (rest[0], rest[1:]) if g else (None, rest)
    dqo_hbm, dqs_hbm, gs_hbm, grad_hbm = rest[0], rest[1], rest[2], rest[3:6]
    (k_sc, v_sc, kt_sc, vt_sc, s_sc, q_sc, d_sc, dq_sc, dk_sc, dv_sc, lim_sc, lims_sc) = rest[6:18]
    own_sc, bf_sc, gs_sc, sem, out_sem = rest[18:]
    _, chip, core = place()
    mine = window(core * ROWS, ROWS)
    theirs = window((1 - core) * ROWS, ROWS)
    copies = []

    def copy(src, dst):
        copies.append(pltpu.make_async_copy(src, dst, sem.at[len(copies)]))
        copies[-1].start()

    if g:
        copy(before, gs_sc)
    copy(q_hbm.at[:, window(core * 1024 + g * 512, 512)], q_sc.at[mine])
    copy(d_hbm.at[:, window(core * 1024 + g * 512, 512)], d_sc.at[mine])
    copy(qd_hbm.at[:, g * 512 : (g + 1) * 512], q_sc.at[theirs])
    copy(qd_hbm.at[:, 1024 + g * 512 : 1536 + g * 512], d_sc.at[theirs])
    for i, kv in enumerate((kv2, kv1, kv0)):
        for part in range(2):
            at = window(i * 512 + (core if part == 0 else 1 - core) * ROWS, ROWS)
            rows = slice(part * ROWS, (part + 1) * ROWS)
            copy(kv.at[rows, :HEAD], k_sc.at[at])
            copy(kv.at[rows, HEAD:], v_sc.at[at])
    copy(summ.at[:, :HEAD], k_sc.at[1536:])
    copy(summ.at[:, HEAD:], v_sc.at[1536:])
    ki = lax.broadcasted_iota(jnp.int32, (ROWS, ROWS), 0)
    qi = lax.broadcasted_iota(jnp.int32, (ROWS, ROWS), 1)
    pos = jnp.concatenate([pos_ref[...], pos_ref[...]], 1)
    for b in range(2):
        lim_sc[b] = jnp.where((ki > qi) & (chip * 2 + b >= 4), BIG, NEG)
        lims_sc[b] = jnp.where(pos <= ((chip * 2 + b) * ROWS + qi).astype(F32), BIG, NEG)
    lim_sc[2] = jnp.where(ki <= qi, BIG, NEG)
    dk_sc[...] = jnp.zeros_like(dk_sc)
    dv_sc[...] = jnp.zeros_like(dv_sc)
    for done in copies:
        done.wait()
    for i in range(7):
        at = slice(i * ROWS, (i + 1) * ROWS)
        kt_sc[:, at] = k_sc[at, :].T
        vt_sc[:, at] = v_sc[at, :].T
    outs = []

    def send(src, dst):
        outs.append(pltpu.make_async_copy(src, dst, out_sem.at[len(outs)]))
        outs[-1].start()

    def emit():
        send(dq_sc.at[mine], dqo_hbm)
        send(dq_sc.at[theirs], dqs_hbm)
        dk_sc[1536:, :] = dk_sc[1536:, :] * SCALE
        for i, acc in enumerate((dk_sc, dv_sc)):
            for r in range(2):
                slots = pl.ds(4 * g + 2 * i + r, 128, stride=8)
                gs_sc[slots, :] = acc[pl.ds(1536 + r, 128, stride=2), :]
        send(gs_sc, gs_hbm)
        for i, hbm in enumerate(grad_hbm):
            for part in range(2):
                at = window((2 - i) * 512 + (core if part == 0 else 1 - core) * ROWS, ROWS)
                rows = slice(part * ROWS, (part + 1) * ROWS)
                stage, kind = (own_sc, F32) if i == 0 else (bf_sc.at[i - 1], BF)
                stage[rows, :HEAD] = (dk_sc[at, :] * SCALE).astype(kind)
                stage[rows, HEAD:] = dv_sc[at, :].astype(kind)
            send(stage, hbm)

    factor = SCALE * LOG2E

    def base(u, t):
        return 1536 if t == 5 else (u["b"] + t) * ROWS

    units = [dict(b=u // 4, h=u % 4, slot=u % 3) for u in range(8)]

    def open_unit(u):
        rows = slice(u["b"] * ROWS, (u["b"] + 1) * ROWS)
        cols = slice(u["h"] * HEAD, (u["h"] + 1) * HEAD)
        u["q"], u["d"] = q_sc[rows, cols], d_sc[rows, cols]
        u["qt"], u["dt"] = u["q"].T, u["d"].T
        u["m"] = u["l"] = u["o"] = u["dq"] = None

    def scores(u, t):
        b, at = u["b"], slice(t * ROWS, (t + 1) * ROWS)
        s = dot(k_sc[base(u, t) : base(u, t) + ROWS, :], u["qt"])
        if t == 0:
            limit = lim_sc[b]
        elif t == 4:
            limit = lim_sc[2]
        elif t == 5:
            limit = lims_sc[b]
        else:
            limit = jnp.where(chip * 2 + b + t >= 4, BIG, NEG)
        s = jnp.minimum(s, limit)
        s_sc[u["slot"], at, :] = s
        m = fold(s, jnp.max)
        u["m"] = m if u["m"] is None else jnp.maximum(u["m"], m)

    def close_scores(u):
        u["m2"] = jnp.max(u["m"], axis=0, keepdims=True) * factor

    def weights(u, t):
        b, at = u["b"], slice(t * ROWS, (t + 1) * ROWS)
        p = jnp.exp2(s_sc[u["slot"], at, :] * factor - u["m2"])
        s_sc[u["slot"], at, :] = p
        part = fold(p, jnp.sum)
        u["l"] = part if u["l"] is None else u["l"] + part
        o = dot(vt_sc[:, base(u, t) : base(u, t) + ROWS], p.astype(BF))
        u["o"] = o if u["o"] is None else u["o"] + o

    def close_weights(u):
        u["inv"] = 1.0 / jnp.sum(u["l"], axis=0, keepdims=True)
        attended = (u["o"] * u["inv"]).astype(BF).astype(F32)
        u["delta"] = jnp.sum(u["dt"].astype(F32) * attended, axis=0, keepdims=True)

    def grads(u, t):
        b, at = u["b"], slice(t * ROWS, (t + 1) * ROWS)
        keys = slice(base(u, t), base(u, t) + ROWS)
        dp = dot(v_sc[keys, :], u["dt"])
        p = s_sc[u["slot"], at, :] * u["inv"]
        ds = (p * (dp - u["delta"])).astype(BF)
        dk_sc[keys, :] += dot(ds, u["q"])
        dv_sc[keys, :] += dot(p.astype(BF), u["d"])
        dq = dot(kt_sc[:, keys], ds)
        u["dq"] = dq if u["dq"] is None else u["dq"] + dq

    def close_grads(u):
        rows = slice(u["b"] * ROWS, (u["b"] + 1) * ROWS)
        cols = slice(u["h"] * HEAD, (u["h"] + 1) * HEAD)
        dq_sc[rows, cols] = (u["dq"] * SCALE).T.astype(BF)

    for step in range(len(units) + 2):
        now, before, earlier = step < 8, 0 <= step - 1 < 8, 0 <= step - 2 < 8
        if now:
            open_unit(units[step])
        for t in range(6):
            if earlier:
                grads(units[step - 2], t)
            if before:
                weights(units[step - 1], t)
            if now:
                scores(units[step], t)
        if now:
            close_scores(units[step])
        if before:
            close_weights(units[step - 1])
        if earlier:
            close_grads(units[step - 2])
    emit()
    for done in outs:
        done.wait()


def attend(g, *args):
    shape = jax.ShapeDtypeStruct
    return pl.pallas_call(
        functools.partial(attend_kernel, g),
        in_specs=[VM] + [ANY] * (7 + g),
        out_specs=[ANY] * 6,
        out_shape=[
            shape((ROWS, 512), BF),
            shape((ROWS, 512), BF),
            shape((1024, HEAD), F32),
            shape((512, 256), F32),
            shape((512, 256), BF),
            shape((512, 256), BF),
        ],
        scratch_shapes=[
            pltpu.VMEM((SPAN, HEAD), BF),
            pltpu.VMEM((SPAN, HEAD), BF),
            pltpu.VMEM((HEAD, SPAN), BF),
            pltpu.VMEM((HEAD, SPAN), BF),
            pltpu.VMEM((3, 1536, ROWS), F32),
            pltpu.VMEM((512, 512), BF),
            pltpu.VMEM((512, 512), BF),
            pltpu.VMEM((512, 512), BF),
            pltpu.VMEM((SPAN, HEAD), F32),
            pltpu.VMEM((SPAN, HEAD), F32),
            pltpu.VMEM((3, ROWS, ROWS), F32),
            pltpu.VMEM((2, ROWS, ROWS), F32),
            pltpu.VMEM((512, 256), F32),
            pltpu.VMEM((2, 512, 256), BF),
            pltpu.VMEM((1024, HEAD), F32),
            pltpu.SemaphoreType.DMA((22,)),
            pltpu.SemaphoreType.DMA((8,)),
        ],
        compiler_params=pltpu.CompilerParams(vmem_limit_bytes=60 << 20),
        cost_estimate=pl.CostEstimate(
            flops=5_000_000_000, bytes_accessed=4_000_000, transcendentals=3_000_000
        ),
        name="attend",
    )(*args)


def gather_kernel(*refs):
    parts = (refs[:3], refs[3:6])
    dq_parts, mine_ref, theirs, dq_ref = refs[6:10], refs[10], refs[11:13], refs[13]
    core = place()[2]
    for g, (own, back1, back2) in enumerate(parts):
        total = own[...] + back1[...].astype(F32) + back2[...].astype(F32)
        mine_ref[:, g * 256 : (g + 1) * 256] = total[:ROWS]
        theirs[g][...] = total[ROWS:].astype(BF)
    for i, ref in enumerate(dq_parts):
        which = core if i % 2 == 0 else 1 - core
        dq_ref[:, window((2 * which + i // 2) * 512, 512)] = ref[...]


def gather(*args):
    shape = jax.ShapeDtypeStruct
    return pl.pallas_call(
        gather_kernel,
        in_specs=[VM] * 10,
        out_specs=[VM] * 4,
        out_shape=[
            shape((ROWS, 512), F32),
            shape((ROWS, 256), BF),
            shape((ROWS, 256), BF),
            shape((ROWS, 2048), BF),
        ],
        compiler_params=pltpu.CompilerParams(vmem_limit_bytes=60 << 20),
        cost_estimate=pl.CostEstimate(flops=GATHER_FLOPS, bytes_accessed=6_000_000, transcendentals=0),
        name="gather",
    )(*args)


def finish_kernel(pos_ref, mine_ref, recv0_ref, recv1_ref, share_ref, dk_ref, dv_ref):
    index, _, core = place()
    row = lax.broadcasted_iota(jnp.int32, (ROWS, HEAD), 0)
    first = pos_ref[2 * index] - index * ROWS
    second = pos_ref[2 * index + 1] - index * ROWS
    shares = []
    for source in range(2):
        share = share_ref[source]
        for i in range(1, share_ref.shape[0] // 2):
            share = share + share_ref[2 * i + source]
        shares.append(share)
    for half in range(2):
        which = core if half == 0 else 1 - core
        share = jnp.where(which == 0, shares[0], shares[1])
        for g in range(2):
            for i, out in enumerate((dk_ref, dv_ref)):
                at = 4 * g + 2 * i
                if half == 0:
                    total = mine_ref[:, (2 * g + i) * HEAD : (2 * g + i + 1) * HEAD]
                else:
                    total = (recv0_ref, recv1_ref)[g][:, i * HEAD : (i + 1) * HEAD].astype(F32)
                total = total + jnp.where(row == first, share[at : at + 1], 0.0)
                total = total + jnp.where(row == second, share[at + 1 : at + 2], 0.0)
                out[:, window((2 * which + g) * HEAD, HEAD)] = total.astype(BF)


def finish(*args):
    shape = jax.ShapeDtypeStruct
    return pl.pallas_call(
        finish_kernel,
        in_specs=[SM] + [VM] * 4,
        out_specs=[VM, VM],
        out_shape=[shape((ROWS, 512), BF), shape((ROWS, 512), BF)],
        compiler_params=pltpu.CompilerParams(vmem_limit_bytes=60 << 20),
        name="finish",
    )(*args)


def to_sibling(block):
    return lax.ppermute(block, "ctx", [(i, i ^ 1) for i in range(lax.axis_size("ctx"))])


def to_chip(block, hops, flip=0):
    size = lax.axis_size("ctx")
    return lax.ppermute(block, "ctx", [(i, ((i + 2 * hops) % size) ^ flip) for i in range(size)])


def exchange(block):
    return lax.all_to_all(block, "ctx", 0, 0, tiled=True)


def body(queries, keys, values, cotangent, summary_positions):
    kv_own, kv_send, blocks, qd_send = pack(summary_positions, keys, values, queries, cotangent)
    kv_recv = to_sibling(kv_send)
    qd = to_sibling(qd_send)
    summ = exchange(blocks).reshape(1024, HEAD)
    kv0 = [jnp.concatenate([kv_own[g], kv_recv[g]], 0) for g in range(2)]
    kv1 = [to_chip(kv0[g], 1) for g in range(2)]
    kv2 = [to_chip(kv0[g], 2) for g in range(2)]
    sk0, sk1, pos = unpack(summary_positions.reshape(2, 128), summ)
    outs = attend(0, pos, queries, cotangent, qd, kv2[0], kv1[0], kv0[0], sk0)
    dq0, dqs0, summ_grad, own0, back1, back2 = outs
    back1_0, back2_0 = to_chip(back1, -1), to_chip(back2, -2)
    outs = attend(1, pos, queries, cotangent, qd, kv2[1], kv1[1], kv0[1], sk1, summ_grad)
    outs, back1_0, back2_0, dqs0 = lax.optimization_barrier((outs, back1_0, back2_0, dqs0))
    dq1, dqs1, summ_grad, own1, back1, back2 = outs
    back1_1, back2_1 = to_chip(back1, -1), to_chip(back2, -2)
    mine, theirs0, theirs1, query_grad = gather(
        own0, back1_0, back2_0, own1, back1_1, back2_1, dq0, to_sibling(dqs0), dq1, to_sibling(dqs1)
    )
    shares = exchange(summ_grad.reshape(128, 8, HEAD))
    key_grad, value_gradient = finish(
        summary_positions, mine, to_sibling(theirs0), to_sibling(theirs1), shares
    )
    return query_grad, key_grad, value_gradient


def solution(mesh):
    return jax.shard_map(
        body,
        mesh=mesh,
        in_specs=(P("ctx", None), P("ctx", None), P("ctx", None), P("ctx", None), P()),
        out_specs=(P("ctx", None), P("ctx", None), P("ctx", None)),
        check_vma=False,
    )
```

time: 390 us -> 106 us (0.27)
  waiting for transfers between devices: 165 us -> 18.6 us
  blocking collectives: 74.2 us -> 0 us
  matrix products: 43.2 us -> 0 us
  Pallas kernels: 0 us -> 40.6 us
  other arithmetic: 21.8 us -> 0.04 us
  local copies, waits for them, and re-layouts: 25.2 us -> 4.31 us
  between operations: 15.2 us -> 0.83 us
    unnamed x2 -> x0, waiting for transfers between devices: 140 us -> none
    all_gather x2 -> x0, blocking collectives: 74.2 us -> none  [the longest x1 41 us: body(): lax.all_gather(local_keys, 'ctx', axis=0, tiled=True)]
    dot_general x48 -> x0, matrix products: 43.2 us -> none  [the longest x4 6.22 us: group_pass(): jnp.einsum('gtk,kd->tgd', band_dscore, band_keys, preferred_element_type=...]
    pallas_call x0 -> x6, Pallas kernels: none -> 40.6 us  [the longest x2 29.7 us: attend(): pl.pallas_call(functools.partial(attend_kernel, g), in_specs=[VM] + [ANY]...]
    ppermute x16 -> x14, starting transfers between devices: 43.7 us -> 26.4 us  [the longest x8 15.2 us: to_chip(): lax.ppermute(block, 'ctx', [(i, (i + 2 * hops) % size ^ flip) for i in ra...]
    all_to_all x0 -> x2, starting transfers between devices: none -> 14.6 us  [exchange(): return lax.all_to_all(block, 'ctx', 0, 0, tiled=True)]
    ppermute x16 -> x14, waiting for transfers between devices: 25.5 us -> 12.4 us  [the longest x8 10.9 us: to_chip(): lax.ppermute(block, 'ctx', [(i, (i + 2 * hops) % size ^ flip) for i in ra...]
    unnamed x88 -> x38, local copies, waits for them, and re-layouts: 12.2 us -> 4.27 us
  transfers between devices with their start and end apart: 17 -> 16, of which waited for: 6 -> 7; matrix products, arithmetic and copies ran while one was open for 7% -> 0% of each run, Pallas kernels for 0% -> 33%
where the time goes in v1:
time: 106 us; the launch traced here: 105 us
  starting transfers between devices  41 us (39%)
  Pallas kernels  40.6 us (38%)
  waiting for transfers between devices  18.6 us (18%)
  local copies, waits for them, and re-layouts  4.31 us (4%)
    pallas_call x2, Pallas kernels, attend(): pl.pallas_call(functools.partial(attend_kernel, g), in_specs=[VM] + [ANY]...  29.7 us
    ppermute x8, starting transfers between devices, to_chip(): lax.ppermute(block, 'ctx', [(i, (i + 2 * hops) % size ^ flip) for i in ra...  15.2 us
    all_to_all x2, starting transfers between devices, exchange(): return lax.all_to_all(block, 'ctx', 0, 0, tiled=True)  14.6 us
    ppermute x6, starting transfers between devices, to_sibling(): lax.ppermute(block, 'ctx', [(i, i ^ 1) for i in range(lax.axis_size('ctx'...  11.3 us
    ppermute x8, waiting for transfers between devices, to_chip(): lax.ppermute(block, 'ctx', [(i, (i + 2 * hops) % size ^ flip) for i in ra...  10.9 us
    all_to_all x2, waiting for transfers between devices, exchange(): return lax.all_to_all(block, 'ctx', 0, 0, tiled=True)  6.26 us
    unnamed x38, local copies, waits for them, and re-layouts  4.27 us
    pallas_call x1, Pallas kernels, pack(): pl.pallas_call(pack_kernel, in_specs=[SM, VM, VM, ANY, ANY], out_specs=[V...  3.51 us
  transfers between devices with their start and end apart: 16, of which 7 were waited for; matrix products, arithmetic and copies ran while one was open for 0% of the time, Pallas kernels for 33%

profile of v1, /device:TPU:1, one launch (start us, length us, event | category | flops | bytes accessed | tf_op | source)
XLA Modules:
  0.0 105.4 jit_solution(4092807089213917034)
XLA Ops:
  0.6 3.5 %pack.1 = (bf16[2,256,256]{2,1,0:T(8,128)(2,1)}, bf16[2,256,256]{2,1,0:T(8,128)(2,1)}, bf16[128,8,128]{2,1,0:T(8,128)(2,1)}, bf16[256,2048]{1,0:T(8,128)(2,1)}) custom-call(s32[256]{0:T(256)} %pos_ref.3, bf16[256,512]{1,0:T(8,128)(2,1)} %k_ref.1, bf16[256,512]{1,0:T(8,128)(2,1)} %v_ref.1, bf16[256,2048]{1,0:T(8,128)(2,1)} %q_hbm.5, bf16[256,2048]{1,0:T(8,128)(2,1)} %d_hbm.5), custom_call_target="tpu_custom_call" | custom-call | tf_op jit(solution)/shard_map/pack/pallas_call | solution.py:80
  4.1 1.5 %collective-permute-start.1 = (bf16[2,256,256]{2,1,0:T(8,128)(2,1)}, bf16[2,256,256]{2,1,0:T(8,128)(2,1)S(1)}, u32[]{:S(2)}, u32[]{:S(2)}) collective-permute-start(bf16[2,256,256]{2,1,0:T(8,128)(2,1)} %get-tuple-element.41), channel_id=1, source_target_pairs={{0,1},{1,0},{2,3},{3,2},{4,5},{5,4},{6,7},{7,6},{8,9},{9,8},{10,11... | collective-permute-start | bytes 786440 | tf_op jit(solution)/shard_map/ppermute | solution.py:390
  5.6 0.0 copy-start.4
  5.6 10.2 %all-to-all-start = ((bf16[128,8,128]{2,1,0:T(8,128)(2,1)}), bf16[128,8,128]{2,1,0:T(8,128)(2,1)S(1)}, u32[]{:S(2)}, u32[]{:S(2)}) async-start(bf16[128,8,128]{2,1,0:T(8,128)(2,1)} %get-tuple-element.37), calls=%async_computation | async-start | bytes 524288 | tf_op jit(solution)/shard_map/all_to_all | solution.py:399
  15.8 1.1 %collective-permute-start = (bf16[256,2048]{1,0:T(8,128)(2,1)}, bf16[256,2048]{1,0:T(8,128)(2,1)S(1)}, u32[]{:S(2)}, u32[]{:S(2)}) collective-permute-start(bf16[256,2048]{1,0:T(8,128)(2,1)} %get-tuple-element.39), channel_id=1, source_target_pairs={{0,1},{1,0},{2,3},{3,2},{4,5},{5,4},{6,7},{7,6},{8,9},{9,8},{10,11... | collective-permute-start | bytes 3145736 | tf_op jit(solution)/shard_map/ppermute | solution.py:390
  17.0 0.0 copy-done.4
  17.0 0.0 collective-permute-done.1
  17.1 0.0 copy-start.2
  17.1 0.9 collective-permute-start.3
  18.0 2.9 %collective-permute-start.2 = (bf16[512,256]{1,0:T(8,128)(2,1)S(1)}, bf16[512,256]{1,0:T(8,128)(2,1)S(1)}, u32[]{:S(2)}, u32[]{:S(2)}) collective-permute-start(bf16[512,256]{1,0:T(8,128)(2,1)S(1)} %pad_maximum_fusion.kv0), channel_id=1, source_target_pairs={{0,4},{1,5},{2,6},{3,7},{4,8},{5,9},{6,10},{7,11},{8,12},{9,13},{1... | collective-permute-start | bytes 786440 | tf_op jit(solution)/shard_map/ppermute | solution.py:395
  20.9 6.3 %all-to-all-done = bf16[128,8,128]{2,1,0:T(8,128)(2,1)S(1)} async-done(((bf16[128,8,128]{2,1,0:T(8,128)(2,1)}), bf16[128,8,128]{2,1,0:T(8,128)(2,1)S(1)}, u32[]{:S(2)}, u32[]{:S(2)}) %all-to-all-start) | async-done | bytes 262176 | tf_op jit(solution)/shard_map/all_to_all | solution.py:399
  27.2 0.7 copy-done.3
  27.9 1.9 %unpack.1 = (bf16[256,256]{1,0:T(8,128)(2,1)}, bf16[256,256]{1,0:T(8,128)(2,1)}, f32[256,128]{1,0:T(8,128)}) custom-call(s32[2,128]{1,0:T(2,128)} %bitcast.13, bf16[1024,128]{1,0:T(8,128)(2,1)} %bitcast.12), custom_call_target="tpu_custom_call" | custom-call | flops 40000000000 | bytes 1000000 | tf_op jit(solution)/shard_map/unpack/pallas_call | solution.py:111
  29.7 0.0 copy-done.2
  29.7 0.0 copy-start.1
  29.8 0.1 collective-permute-start.5
  29.8 1.8 %collective-permute-start.4 = (bf16[512,256]{1,0:T(8,128)(2,1)S(1)}, bf16[512,256]{1,0:T(8,128)(2,1)S(1)}, u32[]{:S(2)}, u32[]{:S(2)}) collective-permute-start(bf16[512,256]{1,0:T(8,128)(2,1)S(1)} %pad_maximum_fusion.1.kv0), channel_id=1, source_target_pairs={{0,4},{1,5},{2,6},{3,7},{4,8},{5,9},{6,10},{7,11},{8,12},{9,13},{1... | collective-permute-start | bytes 786440 | tf_op jit(solution)/shard_map/ppermute | solution.py:395
  31.7 4.4 %collective-permute-done.3.kv1 = bf16[512,256]{1,0:T(8,128)(2,1)S(1)} collective-permute-done((bf16[512,256]{1,0:T(8,128)(2,1)S(1)}, bf16[512,256]{1,0:T(8,128)(2,1)S(1)}, u32[]{:S(2)}, u32[]{:S(2)}) %collective-permute-start.3) | collective-permute-done | bytes 262176 | tf_op jit(solution)/shard_map/ppermute | solution.py:395
  36.0 1.2 %collective-permute-done.2.kv2 = bf16[512,256]{1,0:T(8,128)(2,1)S(1)} collective-permute-done((bf16[512,256]{1,0:T(8,128)(2,1)S(1)}, bf16[512,256]{1,0:T(8,128)(2,1)S(1)}, u32[]{:S(2)}, u32[]{:S(2)}) %collective-permute-start.2) | collective-permute-done | bytes 262176 | tf_op jit(solution)/shard_map/ppermute | solution.py:395
  37.2 0.0 collective-permute-done.qd_hbm
  37.2 0.0 copy-done.13
  37.3 0.7 copy-done.15
  37.9 0.4 copy-done.7
  38.3 14.8 %attend.2 = (bf16[256,512]{1,0:T(8,128)(2,1)}, bf16[256,512]{1,0:T(8,128)(2,1)}, f32[1024,128]{1,0:T(8,128)}, f32[512,256]{1,0:T(8,128)}, bf16[512,256]{1,0:T(8,128)(2,1)}, /*index=5*/bf16[512,256]{1,0:T(8,128)(2,1)}) custom-call(f32[256,128]{1,0:T(8,128)} %get-tuple-element.38.pos_ref, bf16[256,2048]{1,0:T(8,128)(2,1)} %q_hbm.5, bf16[256,2048]{1,0:T(8,128)(2,1)} %d_hbm.5, ...), custom_call_target="tpu_custom_call" | custom-call | flops 5000000000 | bytes 4000000 | tf_op jit(solution)/shard_map/attend/pallas_call | solution.py:281
  53.1 0.0 copy-done.1
  53.1 2.8 %collective-permute-start.6 = (bf16[512,256]{1,0:T(8,128)(2,1)}, bf16[512,256]{1,0:T(8,128)(2,1)S(1)}, u32[]{:S(2)}, u32[]{:S(2)}) collective-permute-start(bf16[512,256]{1,0:T(8,128)(2,1)} %get-tuple-element.52), channel_id=1, source_target_pairs={{0,126},{1,127},{2,0},{3,1},{4,2},{5,3},{6,4},{7,5},{8,6},{9,7},{1... | collective-permute-start | bytes 786440 | tf_op jit(solution)/shard_map/ppermute | solution.py:395
  55.9 5.7 %collective-permute-start.7 = (bf16[512,256]{1,0:T(8,128)(2,1)}, bf16[512,256]{1,0:T(8,128)(2,1)S(1)}, u32[]{:S(2)}, u32[]{:S(2)}) collective-permute-start(bf16[512,256]{1,0:T(8,128)(2,1)} %get-tuple-element.53), channel_id=1, source_target_pairs={{0,124},{1,125},{2,126},{3,127},{4,0},{5,1},{6,2},{7,3},{8,4},{9,5... | collective-permute-start | bytes 786440 | tf_op jit(solution)/shard_map/ppermute | solution.py:395
  61.6 0.0 collective-permute-done.5.kv1
  61.6 0.0 collective-permute-done.4.kv2
  61.6 0.0 copy-start.12
  61.6 0.7 copy-done.11
  62.3 0.1 copy-done.12
  62.4 14.9 %attend.3 = (bf16[256,512]{1,0:T(8,128)(2,1)}, bf16[256,512]{1,0:T(8,128)(2,1)}, f32[1024,128]{1,0:T(8,128)}, f32[512,256]{1,0:T(8,128)}, bf16[512,256]{1,0:T(8,128)(2,1)}, /*index=5*/bf16[512,256]{1,0:T(8,128)(2,1)}) custom-call(f32[256,128]{1,0:T(8,128)} %get-tuple-element.38.pos_ref, bf16[256,2048]{1,0:T(8,128)(2,1)} %q_hbm.5, bf16[256,2048]{1,0:T(8,128)(2,1)} %d_hbm.5, ...), custom_call_target="tpu_custom_call" | custom-call | flops 5000000000 | bytes 4000000 | tf_op jit(solution)/shard_map/attend/pallas_call | solution.py:281
  77.4 0.0 collective-permute-done.6.refs_1_
  77.4 0.0 copy-start.8
  77.4 0.0 collective-permute-done.7.refs_2_
  77.4 0.0 copy-start.9
  77.4 1.0 collective-permute-start.8
  78.4 0.0 collective-permute-start.9
  78.4 0.0 copy-done.10
  78.4 2.6 %collective-permute-start.10 = (bf16[256,512]{1,0:T(8,128)(2,1)S(1)}, bf16[256,512]{1,0:T(8,128)(2,1)S(1)}, u32[]{:S(2)}, u32[]{:S(2)}) collective-permute-start(bf16[256,512]{1,0:T(8,128)(2,1)S(1)} %copy-done.10), channel_id=1, source_target_pairs={{0,1},{1,0},{2,3},{3,2},{4,5},{5,4},{6,7},{7,6},{8,9},{9,8},{10,11... | collective-permute-start | bytes 786440 | tf_op jit(solution)/shard_map/ppermute | solution.py:390
  81.0 0.0 collective-permute-start.11
  81.0 0.0 copy-done.8
  81.0 0.0 copy-done.9
  81.0 4.4 %all-to-all-start.1 = ((f32[128,8,128]{2,1,0:T(8,128)}), f32[128,8,128]{2,1,0:T(8,128)S(1)}, u32[]{:S(2)}, u32[]{:S(2)}) async-start(f32[128,8,128]{2,1,0:T(8,128)} %bitcast.11), calls=%async_computation.1 | async-start | bytes 1048576 | tf_op jit(solution)/shard_map/all_to_all | solution.py:399
  85.4 3.8 %collective-permute-done.8.refs_4_ = bf16[512,256]{1,0:T(8,128)(2,1)S(1)} collective-permute-done((bf16[512,256]{1,0:T(8,128)(2,1)}, bf16[512,256]{1,0:T(8,128)(2,1)S(1)}, u32[]{:S(2)}, u32[]{:S(2)}) %collective-permute-start.8) | collective-permute-done | bytes 262176 | tf_op jit(solution)/shard_map/ppermute | solution.py:395
  89.2 1.5 %collective-permute-done.9.refs_5_ = bf16[512,256]{1,0:T(8,128)(2,1)S(1)} collective-permute-done((bf16[512,256]{1,0:T(8,128)(2,1)}, bf16[512,256]{1,0:T(8,128)(2,1)S(1)}, u32[]{:S(2)}, u32[]{:S(2)}) %collective-permute-start.9) | collective-permute-done | bytes 262176 | tf_op jit(solution)/shard_map/ppermute | solution.py:395
  90.7 0.0 collective-permute-done.10.refs_7_
  90.7 0.0 collective-permute-done.11.refs_9_
  90.7 0.0 copy-start.18
  90.8 0.0 copy-done.14
  90.8 0.7 copy-done.16
  91.4 0.1 copy-done.17
  91.5 0.1 copy-done.18
  91.6 3.1 %gather.1 = (f32[256,512]{1,0:T(8,128)}, bf16[256,256]{1,0:T(8,128)(2,1)}, bf16[256,256]{1,0:T(8,128)(2,1)}, bf16[256,2048]{1,0:T(8,128)(2,1)}) custom-call(f32[512,256]{1,0:T(8,128)} %get-tuple-element.43.refs_0_, bf16[512,256]{1,0:T(8,128)(2,1)} %copy-done.8, bf16[512,256]{1,0:T(8,128)(2,1)} %copy-done.9, f32[512,256]{1,0:T(8,128)} %get-tuple-element.57.refs_3_, ...), custom_call_target="tpu_custom_call" | custom-call | flops 6000000000 | bytes 6000000 | tf_op jit(solution)/shard_map/gather/pallas_call | solution.py:335
  94.8 5.9 %collective-permute-start.12 = (bf16[256,256]{1,0:T(8,128)(2,1)}, bf16[256,256]{1,0:T(8,128)(2,1)S(1)}, u32[]{:S(2)}, u32[]{:S(2)}) collective-permute-start(bf16[256,256]{1,0:T(8,128)(2,1)} %get-tuple-element.66), channel_id=1, source_target_pairs={{0,1},{1,0},{2,3},{3,2},{4,5},{5,4},{6,7},{7,6},{8,9},{9,8},{10,11... | collective-permute-start | bytes 393224 | tf_op jit(solution)/shard_map/ppermute | solution.py:390
  100.6 0.1 collective-permute-start.13
  100.7 1.1 %collective-permute-done.12.recv0_ref = bf16[256,256]{1,0:T(8,128)(2,1)S(1)} collective-permute-done((bf16[256,256]{1,0:T(8,128)(2,1)}, bf16[256,256]{1,0:T(8,128)(2,1)S(1)}, u32[]{:S(2)}, u32[]{:S(2)}) %collective-permute-start.12) | collective-permute-done | bytes 131104 | tf_op jit(solution)/shard_map/ppermute | solution.py:390
  101.8 0.4 collective-permute-done.13.recv1_ref
  102.2 0.0 all-to-all-done.1.share_ref
  102.2 0.3 copy-done.5
  102.5 0.4 copy-done.6
  102.9 0.2 copy-done
  103.1 2.4 %finish.1 = (bf16[256,512]{1,0:T(8,128)(2,1)}, bf16[256,512]{1,0:T(8,128)(2,1)}) custom-call(s32[256]{0:T(256)} %pos_ref.3, f32[256,512]{1,0:T(8,128)} %get-tuple-element.65.mine_ref, bf16[256,256]{1,0:T(8,128)(2,1)} %copy-done.5, bf16[256,256]{1,0:T(8,128)(2,1)} %copy-done.6, f32[128,8,128]{2,1,0:T(8,128)} %copy-done), custom_call_target="tpu_custom_call" | custom-call | tf_op jit(solution)/shard_map/finish/pallas_call | solution.py:379
  (16 shorter events, 0.1 us)
Async XLA Ops:
  4.1 12.9 %collective-permute-start.1 = (bf16[2,256,256]{2,1,0:T(8,128)(2,1)}, bf16[2,256,256]{2,1,0:T(8,128)(2,1)S(1)}, u32[]{:S(2)}, u32[]{:S(2)}) collective-permute-start(bf16[2,256,256]{2,1,0:T(8,128)(2,1)} %get-tuple-element.41), channel_id=1, source_target_pairs={{0,1},{1,0},{2,3},{3,2},{4,5},{5,4},{6,7},{7,6},{8,9},{9,8},{10,11... | collective-permute-start | bytes 786440 | tf_op jit(solution)/shard_map/ppermute | solution.py:390
  5.6 11.3 %copy-start.4 = (bf16[2,256,256]{2,1,0:T(8,128)(2,1)S(1)}, bf16[2,256,256]{2,1,0:T(8,128)(2,1)}, u32[]{:S(2)}) copy-start(bf16[2,256,256]{2,1,0:T(8,128)(2,1)} %get-tuple-element.40) | copy-start | bytes 786436
  5.6 21.5 %all-to-all-start = ((bf16[128,8,128]{2,1,0:T(8,128)(2,1)}), bf16[128,8,128]{2,1,0:T(8,128)(2,1)S(1)}, u32[]{:S(2)}, u32[]{:S(2)}) async-start(bf16[128,8,128]{2,1,0:T(8,128)(2,1)} %get-tuple-element.37), calls=%async_computation | async-start | bytes 524288 | tf_op jit(solution)/shard_map/all_to_all | solution.py:399
  15.8 21.4 %collective-permute-start = (bf16[256,2048]{1,0:T(8,128)(2,1)}, bf16[256,2048]{1,0:T(8,128)(2,1)S(1)}, u32[]{:S(2)}, u32[]{:S(2)}) collective-permute-start(bf16[256,2048]{1,0:T(8,128)(2,1)} %get-tuple-element.39), channel_id=1, source_target_pairs={{0,1},{1,0},{2,3},{3,2},{4,5},{5,4},{6,7},{7,6},{8,9},{9,8},{10,11... | collective-permute-start | bytes 3145736 | tf_op jit(solution)/shard_map/ppermute | solution.py:390
  17.1 12.6 %copy-start.2 = (bf16[512,256]{1,0:T(8,128)(2,1)}, bf16[512,256]{1,0:T(8,128)(2,1)S(1)}, u32[]{:S(2)}) copy-start(bf16[512,256]{1,0:T(8,128)(2,1)S(1)} %pad_maximum_fusion.kv0) | copy-start | bytes 786436
  17.1 19.0 %collective-permute-start.3 = (bf16[512,256]{1,0:T(8,128)(2,1)S(1)}, bf16[512,256]{1,0:T(8,128)(2,1)S(1)}, u32[]{:S(2)}, u32[]{:S(2)}) collective-permute-start(bf16[512,256]{1,0:T(8,128)(2,1)S(1)} %pad_maximum_fusion.kv0), channel_id=1, source_target_pairs={{0,2},{1,3},{2,4},{3,5},{4,6},{5,7},{6,8},{7,9},{8,10},{9,11},{10,... | collective-permute-start | bytes 786440 | tf_op jit(solution)/shard_map/ppermute | solution.py:395
  18.0 19.3 %collective-permute-start.2 = (bf16[512,256]{1,0:T(8,128)(2,1)S(1)}, bf16[512,256]{1,0:T(8,128)(2,1)S(1)}, u32[]{:S(2)}, u32[]{:S(2)}) collective-permute-start(bf16[512,256]{1,0:T(8,128)(2,1)S(1)} %pad_maximum_fusion.kv0), channel_id=1, source_target_pairs={{0,4},{1,5},{2,6},{3,7},{4,8},{5,9},{6,10},{7,11},{8,12},{9,13},{1... | collective-permute-start | bytes 786440 | tf_op jit(solution)/shard_map/ppermute | solution.py:395
  27.2 0.7 copy-start.3
  29.7 23.3 %copy-start.1 = (bf16[512,256]{1,0:T(8,128)(2,1)}, bf16[512,256]{1,0:T(8,128)(2,1)S(1)}, u32[]{:S(2)}) copy-start(bf16[512,256]{1,0:T(8,128)(2,1)S(1)} %pad_maximum_fusion.1.kv0) | copy-start | bytes 786436
  29.8 31.9 %collective-permute-start.5 = (bf16[512,256]{1,0:T(8,128)(2,1)S(1)}, bf16[512,256]{1,0:T(8,128)(2,1)S(1)}, u32[]{:S(2)}, u32[]{:S(2)}) collective-permute-start(bf16[512,256]{1,0:T(8,128)(2,1)S(1)} %pad_maximum_fusion.1.kv0), channel_id=1, source_target_pairs={{0,2},{1,3},{2,4},{3,5},{4,6},{5,7},{6,8},{7,9},{8,10},{9,11},{10,... | collective-permute-start | bytes 786440 | tf_op jit(solution)/shard_map/ppermute | solution.py:395
  29.8 31.8 %collective-permute-start.4 = (bf16[512,256]{1,0:T(8,128)(2,1)S(1)}, bf16[512,256]{1,0:T(8,128)(2,1)S(1)}, u32[]{:S(2)}, u32[]{:S(2)}) collective-permute-start(bf16[512,256]{1,0:T(8,128)(2,1)S(1)} %pad_maximum_fusion.1.kv0), channel_id=1, source_target_pairs={{0,4},{1,5},{2,6},{3,7},{4,8},{5,9},{6,10},{7,11},{8,12},{9,13},{1... | collective-permute-start | bytes 786440 | tf_op jit(solution)/shard_map/ppermute | solution.py:395
  36.0 1.2 %copy-start.13 = (bf16[512,256]{1,0:T(8,128)(2,1)}, bf16[512,256]{1,0:T(8,128)(2,1)S(1)}, u32[]{:S(2)}) copy-start(bf16[512,256]{1,0:T(8,128)(2,1)S(1)} %collective-permute-done.3.kv1) | copy-start | bytes 786436
  37.2 0.7 copy-start.15
  37.2 1.1 copy-start.7
  53.1 24.3 %collective-permute-start.6 = (bf16[512,256]{1,0:T(8,128)(2,1)}, bf16[512,256]{1,0:T(8,128)(2,1)S(1)}, u32[]{:S(2)}, u32[]{:S(2)}) collective-permute-start(bf16[512,256]{1,0:T(8,128)(2,1)} %get-tuple-element.52), channel_id=1, source_target_pairs={{0,126},{1,127},{2,0},{3,1},{4,2},{5,3},{6,4},{7,5},{8,6},{9,7},{1... | collective-permute-start | bytes 786440 | tf_op jit(solution)/shard_map/ppermute | solution.py:395
  55.9 21.5 %collective-permute-start.7 = (bf16[512,256]{1,0:T(8,128)(2,1)}, bf16[512,256]{1,0:T(8,128)(2,1)S(1)}, u32[]{:S(2)}, u32[]{:S(2)}) collective-permute-start(bf16[512,256]{1,0:T(8,128)(2,1)} %get-tuple-element.53), channel_id=1, source_target_pairs={{0,124},{1,125},{2,126},{3,127},{4,0},{5,1},{6,2},{7,3},{8,4},{9,5... | collective-permute-start | bytes 786440 | tf_op jit(solution)/shard_map/ppermute | solution.py:395
  61.6 0.7 copy-start.11
  61.6 0.8 copy-start.12
  62.4 16.0 %copy-start.10 = (bf16[256,512]{1,0:T(8,128)(2,1)S(1)}, bf16[256,512]{1,0:T(8,128)(2,1)}, u32[]{:S(2)}) copy-start(bf16[256,512]{1,0:T(8,128)(2,1)} %get-tuple-element.61) | copy-start | bytes 786436
  77.4 3.7 %copy-start.8 = (bf16[512,256]{1,0:T(8,128)(2,1)}, bf16[512,256]{1,0:T(8,128)(2,1)S(1)}, u32[]{:S(2)}) copy-start(bf16[512,256]{1,0:T(8,128)(2,1)S(1)} %collective-permute-done.6.refs_1_) | copy-start | bytes 786436
  77.4 3.6 %copy-start.9 = (bf16[512,256]{1,0:T(8,128)(2,1)}, bf16[512,256]{1,0:T(8,128)(2,1)S(1)}, u32[]{:S(2)}) copy-start(bf16[512,256]{1,0:T(8,128)(2,1)S(1)} %collective-permute-done.7.refs_2_) | copy-start | bytes 786436
  77.4 11.8 %collective-permute-start.8 = (bf16[512,256]{1,0:T(8,128)(2,1)}, bf16[512,256]{1,0:T(8,128)(2,1)S(1)}, u32[]{:S(2)}, u32[]{:S(2)}) collective-permute-start(bf16[512,256]{1,0:T(8,128)(2,1)} %get-tuple-element.58), channel_id=1, source_target_pairs={{0,126},{1,127},{2,0},{3,1},{4,2},{5,3},{6,4},{7,5},{8,6},{9,7},{1... | collective-permute-start | bytes 786440 | tf_op jit(solution)/shard_map/ppermute | solution.py:395
  78.4 12.4 %collective-permute-start.9 = (bf16[512,256]{1,0:T(8,128)(2,1)}, bf16[512,256]{1,0:T(8,128)(2,1)S(1)}, u32[]{:S(2)}, u32[]{:S(2)}) collective-permute-start(bf16[512,256]{1,0:T(8,128)(2,1)} %get-tuple-element.59), channel_id=1, source_target_pairs={{0,124},{1,125},{2,126},{3,127},{4,0},{5,1},{6,2},{7,3},{8,4},{9,5... | collective-permute-start | bytes 786440 | tf_op jit(solution)/shard_map/ppermute | solution.py:395
  78.4 12.4 %collective-permute-start.10 = (bf16[256,512]{1,0:T(8,128)(2,1)S(1)}, bf16[256,512]{1,0:T(8,128)(2,1)S(1)}, u32[]{:S(2)}, u32[]{:S(2)}) collective-permute-start(bf16[256,512]{1,0:T(8,128)(2,1)S(1)} %copy-done.10), channel_id=1, source_target_pairs={{0,1},{1,0},{2,3},{3,2},{4,5},{5,4},{6,7},{7,6},{8,9},{9,8},{10,11... | collective-permute-start | bytes 786440 | tf_op jit(solution)/shard_map/ppermute | solution.py:390
  81.0 9.7 %collective-permute-start.11 = (bf16[256,512]{1,0:T(8,128)(2,1)}, bf16[256,512]{1,0:T(8,128)(2,1)S(1)}, u32[]{:S(2)}, u32[]{:S(2)}) collective-permute-start(bf16[256,512]{1,0:T(8,128)(2,1)} %get-tuple-element.63), channel_id=1, source_target_pairs={{0,1},{1,0},{2,3},{3,2},{4,5},{5,4},{6,7},{7,6},{8,9},{9,8},{10,11... | collective-permute-start | bytes 786440 | tf_op jit(solution)/shard_map/ppermute | solution.py:390
  81.0 21.2 %all-to-all-start.1 = ((f32[128,8,128]{2,1,0:T(8,128)}), f32[128,8,128]{2,1,0:T(8,128)S(1)}, u32[]{:S(2)}, u32[]{:S(2)}) async-start(f32[128,8,128]{2,1,0:T(8,128)} %bitcast.11), calls=%async_computation.1 | async-start | bytes 1048576 | tf_op jit(solution)/shard_map/all_to_all | solution.py:399
  89.2 1.5 %copy-start.14 = (bf16[512,256]{1,0:T(8,128)(2,1)}, bf16[512,256]{1,0:T(8,128)(2,1)S(1)}, u32[]{:S(2)}) copy-start(bf16[512,256]{1,0:T(8,128)(2,1)S(1)} %collective-permute-done.8.refs_4_) | copy-start | bytes 786436
  90.7 0.7 copy-start.16
  90.7 0.8 copy-start.17
  90.7 0.9 copy-start.18
  94.8 7.1 %collective-permute-start.12 = (bf16[256,256]{1,0:T(8,128)(2,1)}, bf16[256,256]{1,0:T(8,128)(2,1)S(1)}, u32[]{:S(2)}, u32[]{:S(2)}) collective-permute-start(bf16[256,256]{1,0:T(8,128)(2,1)} %get-tuple-element.66), channel_id=1, source_target_pairs={{0,1},{1,0},{2,3},{3,2},{4,5},{5,4},{6,7},{7,6},{8,9},{9,8},{10,11... | collective-permute-start | bytes 393224 | tf_op jit(solution)/shard_map/ppermute | solution.py:390
  100.6 1.6 %collective-permute-start.13 = (bf16[256,256]{1,0:T(8,128)(2,1)}, bf16[256,256]{1,0:T(8,128)(2,1)S(1)}, u32[]{:S(2)}, u32[]{:S(2)}) collective-permute-start(bf16[256,256]{1,0:T(8,128)(2,1)} %get-tuple-element.67), channel_id=1, source_target_pairs={{0,1},{1,0},{2,3},{3,2},{4,5},{5,4},{6,7},{7,6},{8,9},{9,8},{10,11... | collective-permute-start | bytes 393224 | tf_op jit(solution)/shard_map/ppermute | solution.py:390
  101.8 0.6 copy-start.5
  102.2 0.7 copy-start.6
  102.2 0.8 copy-start

commit v2 on v1

--- a/solution.py
+++ b/solution.py
@@ -20,7 +20,8 @@
 BF = jnp.bfloat16
 VM = pl.BlockSpec(memory_space=pltpu.VMEM)
 SM = pl.BlockSpec(memory_space=pltpu.SMEM)
-ANY = pl.BlockSpec(memory_space=pltpu.HBM)
+HBM = pl.BlockSpec(memory_space=pltpu.HBM)
+ANY = pl.BlockSpec(memory_space=pl.ANY)
 
 
 def dot(a, b):
@@ -79,7 +80,7 @@
     shape = jax.ShapeDtypeStruct
     return pl.pallas_call(
         pack_kernel,
-        in_specs=[SM, VM, VM, ANY, ANY],
+        in_specs=[SM, VM, VM, HBM, HBM],
         out_specs=[VM] * 4,
         out_shape=[
             shape((2, ROWS, 2 * HEAD), BF),
@@ -114,7 +115,7 @@
         out_specs=[VM] * 3,
         out_shape=[shape((ROWS, 256), BF), shape((ROWS, 256), BF), shape((ROWS, HEAD), F32)],
         scratch_shapes=[pltpu.VMEM((1024, HEAD), F32), pltpu.VMEM((ROWS, HEAD), F32)],
-        compiler_params=pltpu.CompilerParams(vmem_limit_bytes=60 << 20),
+        compiler_params=pltpu.CompilerParams(vmem_limit_bytes=16 << 20),
         cost_estimate=pl.CostEstimate(flops=UNPACK_FLOPS, bytes_accessed=1_000_000, transcendentals=0),
         name="unpack",
     )(pos, summ)
@@ -280,8 +281,8 @@
     shape = jax.ShapeDtypeStruct
     return pl.pallas_call(
         functools.partial(attend_kernel, g),
-        in_specs=[VM] + [ANY] * (7 + g),
-        out_specs=[ANY] * 6,
+        in_specs=[VM, HBM, HBM] + [ANY] * (5 + g),
+        out_specs=[HBM] * 6,
         out_shape=[
             shape((ROWS, 512), BF),
             shape((ROWS, 512), BF),
@@ -309,7 +310,7 @@
             pltpu.SemaphoreType.DMA((22,)),
             pltpu.SemaphoreType.DMA((8,)),
         ],
-        compiler_params=pltpu.CompilerParams(vmem_limit_bytes=60 << 20),
+        compiler_params=pltpu.CompilerParams(vmem_limit_bytes=24 << 20),
         cost_estimate=pl.CostEstimate(
             flops=5_000_000_000, bytes_accessed=4_000_000, transcendentals=3_000_000
         ),
@@ -342,7 +343,7 @@
             shape((ROWS, 256), BF),
             shape((ROWS, 2048), BF),
         ],
-        compiler_params=pltpu.CompilerParams(vmem_limit_bytes=60 << 20),
+        compiler_params=pltpu.CompilerParams(vmem_limit_bytes=16 << 20),
         cost_estimate=pl.CostEstimate(flops=GATHER_FLOPS, bytes_accessed=6_000_000, transcendentals=0),
         name="gather",
     )(*args)
@@ -381,7 +382,7 @@
         in_specs=[SM] + [VM] * 4,
         out_specs=[VM, VM],
         out_shape=[shape((ROWS, 512), BF), shape((ROWS, 512), BF)],
-        compiler_params=pltpu.CompilerParams(vmem_limit_bytes=60 << 20),
+        compiler_params=pltpu.CompilerParams(vmem_limit_bytes=16 << 20),
         name="finish",
     )(*args)
 

time: 106 us -> 96.4 us (0.909)
  Pallas kernels: 40.6 us -> 30.3 us
  starting transfers between devices: 41 us -> 42.9 us
  waiting for transfers between devices: 18.6 us -> 17.4 us
    pallas_call x3, Pallas kernels: 33.2 us -> 27.4 us  [the longest x2 23.9 us: attend(): pl.pallas_call(functools.partial(attend_kernel, g), in_specs=[VM, HBM, HB...]
    pallas_call x1, Pallas kernels: 3.15 us -> 1.13 us  [gather(): pl.pallas_call(gather_kernel, in_specs=[VM] * 10, out_specs=[VM] * 4, out...]
    pallas_call x1, Pallas kernels: 1.86 us -> 0.18 us  [unpack(): pl.pallas_call(unpack_kernel, in_specs=[VM, VM], out_specs=[VM] * 3, out_...]
    all_to_all x2, starting transfers between devices: 14.6 us -> 16 us  [exchange(): return lax.all_to_all(block, 'ctx', 0, 0, tiled=True)]
    ppermute x8, waiting for transfers between devices: 10.9 us -> 9.78 us  [to_chip(): lax.ppermute(block, 'ctx', [(i, (i + 2 * hops) % size ^ flip) for i in ra...]
    unnamed x38 -> x20, local copies, waits for them, and re-layouts: 4.27 us -> 4.54 us
  transfers between devices with their start and end apart: 16 -> 16, of which waited for: 7 -> 7; matrix products, arithmetic and copies ran while one was open for 0% -> 0% of each run, Pallas kernels for 33% -> 26%
where the time goes in v2:
time: 96.4 us; the launch traced here: 96 us
  starting transfers between devices  42.9 us (45%)
  Pallas kernels  30.3 us (31%)
  waiting for transfers between devices  17.4 us (18%)
  local copies, waits for them, and re-layouts  4.57 us (5%)
    pallas_call x2, Pallas kernels, attend(): pl.pallas_call(functools.partial(attend_kernel, g), in_specs=[VM, HBM, HB...  23.9 us
    all_to_all x2, starting transfers between devices, exchange(): return lax.all_to_all(block, 'ctx', 0, 0, tiled=True)  16 us
    ppermute x8, starting transfers between devices, to_chip(): lax.ppermute(block, 'ctx', [(i, (i + 2 * hops) % size ^ flip) for i in ra...  15.2 us
    ppermute x6, starting transfers between devices, to_sibling(): lax.ppermute(block, 'ctx', [(i, i ^ 1) for i in range(lax.axis_size('ctx'...  11.7 us
    ppermute x8, waiting for transfers between devices, to_chip(): lax.ppermute(block, 'ctx', [(i, (i + 2 * hops) % size ^ flip) for i in ra...  9.78 us
    all_to_all x2, waiting for transfers between devices, exchange(): return lax.all_to_all(block, 'ctx', 0, 0, tiled=True)  6.27 us
    unnamed x20, local copies, waits for them, and re-layouts  4.54 us
    pallas_call x1, Pallas kernels, pack(): pl.pallas_call(pack_kernel, in_specs=[SM, VM, VM, HBM, HBM], out_specs=[V...  3.51 us
  transfers between devices with their start and end apart: 16, of which 7 were waited for; matrix products, arithmetic and copies ran while one was open for 0% of the time, Pallas kernels for 26%

profile of v2, /device:TPU:1, one launch (start us, length us, event | category | flops | bytes accessed | tf_op | source)
XLA Modules:
  0.0 96.0 jit_solution(15909055818335171225)
XLA Ops:
  0.6 3.5 %pack.1 = (bf16[2,256,256]{2,1,0:T(8,128)(2,1)}, bf16[2,256,256]{2,1,0:T(8,128)(2,1)}, bf16[128,8,128]{2,1,0:T(8,128)(2,1)}, bf16[256,2048]{1,0:T(8,128)(2,1)}) custom-call(s32[256]{0:T(256)} %pos_ref.3, bf16[256,512]{1,0:T(8,128)(2,1)} %k_ref.1, bf16[256,512]{1,0:T(8,128)(2,1)} %v_ref.1, bf16[256,2048]{1,0:T(8,128)(2,1)} %q_hbm.5, bf16[256,2048]{1,0:T(8,128)(2,1)} %d_hbm.5), custom_call_target="tpu_custom_call" | custom-call | tf_op jit(solution)/shard_map/pack/pallas_call | solution.py:81
  4.1 1.5 %collective-permute-start.1 = (bf16[2,256,256]{2,1,0:T(8,128)(2,1)}, bf16[2,256,256]{2,1,0:T(8,128)(2,1)S(1)}, u32[]{:S(2)}, u32[]{:S(2)}) collective-permute-start(bf16[2,256,256]{2,1,0:T(8,128)(2,1)} %get-tuple-element.41), channel_id=1, source_target_pairs={{0,1},{1,0},{2,3},{3,2},{4,5},{5,4},{6,7},{7,6},{8,9},{9,8},{10,11... | collective-permute-start | bytes 786440 | tf_op jit(solution)/shard_map/ppermute | solution.py:391
  5.6 0.0 copy-start.9
  5.6 10.2 %all-to-all-start = ((bf16[128,8,128]{2,1,0:T(8,128)(2,1)}), bf16[128,8,128]{2,1,0:T(8,128)(2,1)S(1)}, u32[]{:S(2)}, u32[]{:S(2)}) async-start(bf16[128,8,128]{2,1,0:T(8,128)(2,1)} %get-tuple-element.37), calls=%async_computation | async-start | bytes 524288 | tf_op jit(solution)/shard_map/all_to_all | solution.py:400
  15.8 1.1 %collective-permute-start = (bf16[256,2048]{1,0:T(8,128)(2,1)}, bf16[256,2048]{1,0:T(8,128)(2,1)S(1)}, u32[]{:S(2)}, u32[]{:S(2)}) collective-permute-start(bf16[256,2048]{1,0:T(8,128)(2,1)} %get-tuple-element.39), channel_id=1, source_target_pairs={{0,1},{1,0},{2,3},{3,2},{4,5},{5,4},{6,7},{7,6},{8,9},{9,8},{10,11... | collective-permute-start | bytes 3145736 | tf_op jit(solution)/shard_map/ppermute | solution.py:391
  17.0 0.0 copy-done.9
  17.0 0.0 collective-permute-done.1
  17.1 0.9 collective-permute-start.3
  18.0 2.9 %collective-permute-start.2 = (bf16[512,256]{1,0:T(8,128)(2,1)S(1)}, bf16[512,256]{1,0:T(8,128)(2,1)S(1)}, u32[]{:S(2)}, u32[]{:S(2)}) collective-permute-start(bf16[512,256]{1,0:T(8,128)(2,1)S(1)} %pad_maximum_fusion.kv0), channel_id=1, source_target_pairs={{0,4},{1,5},{2,6},{3,7},{4,8},{5,9},{6,10},{7,11},{8,12},{9,13},{1... | collective-permute-start | bytes 786440 | tf_op jit(solution)/shard_map/ppermute | solution.py:396
  20.9 6.3 %all-to-all-done = bf16[128,8,128]{2,1,0:T(8,128)(2,1)S(1)} async-done(((bf16[128,8,128]{2,1,0:T(8,128)(2,1)}), bf16[128,8,128]{2,1,0:T(8,128)(2,1)S(1)}, u32[]{:S(2)}, u32[]{:S(2)}) %all-to-all-start) | async-done | bytes 262176 | tf_op jit(solution)/shard_map/all_to_all | solution.py:400
  27.2 0.0 copy-start.2
  27.2 0.7 copy-done.2
  27.8 0.0 copy-start
  27.8 0.0 copy-start.1
  27.8 0.2 unpack.1
  28.0 0.1 collective-permute-start.5
  28.1 1.8 %collective-permute-start.4 = (bf16[512,256]{1,0:T(8,128)(2,1)S(1)}, bf16[512,256]{1,0:T(8,128)(2,1)S(1)}, u32[]{:S(2)}, u32[]{:S(2)}) collective-permute-start(bf16[512,256]{1,0:T(8,128)(2,1)S(1)} %pad_maximum_fusion.1.kv0), channel_id=1, source_target_pairs={{0,4},{1,5},{2,6},{3,7},{4,8},{5,9},{6,10},{7,11},{8,12},{9,13},{1... | collective-permute-start | bytes 786440 | tf_op jit(solution)/shard_map/ppermute | solution.py:396
  30.0 6.1 %collective-permute-done.3.kv1 = bf16[512,256]{1,0:T(8,128)(2,1)S(1)} collective-permute-done((bf16[512,256]{1,0:T(8,128)(2,1)S(1)}, bf16[512,256]{1,0:T(8,128)(2,1)S(1)}, u32[]{:S(2)}, u32[]{:S(2)}) %collective-permute-start.3) | collective-permute-done | bytes 262176 | tf_op jit(solution)/shard_map/ppermute | solution.py:396
  36.0 1.2 %collective-permute-done.2.kv2 = bf16[512,256]{1,0:T(8,128)(2,1)S(1)} collective-permute-done((bf16[512,256]{1,0:T(8,128)(2,1)S(1)}, bf16[512,256]{1,0:T(8,128)(2,1)S(1)}, u32[]{:S(2)}, u32[]{:S(2)}) %collective-permute-start.2) | collective-permute-done | bytes 262176 | tf_op jit(solution)/shard_map/ppermute | solution.py:396
  37.3 0.0 collective-permute-done.qd_hbm
  37.3 0.0 copy-done
  37.3 0.0 copy-done.1
  37.3 11.7 %attend.2 = (bf16[256,512]{1,0:T(8,128)(2,1)S(1)}, bf16[256,512]{1,0:T(8,128)(2,1)S(1)}, f32[1024,128]{1,0:T(8,128)S(1)}, f32[512,256]{1,0:T(8,128)S(1)}, bf16[5...) custom-call(f32[256,128]{1,0:T(8,128)S(1)} %get-tuple-element.38.pos_ref, bf16[256,2048]{1,0:T(8,128)(2,1)S(1)} %copy-done, ...), custom_call_target="tpu_custom_call" | custom-call | flops 5000000000 | bytes 4000000 | tf_op jit(solution)/shard_map/attend/pallas_call | solution.py:282
  49.0 0.0 copy-start.5
  49.0 0.0 copy-start.7
  49.0 2.7 %collective-permute-start.6 = (bf16[512,256]{1,0:T(8,128)(2,1)S(1)}, bf16[512,256]{1,0:T(8,128)(2,1)S(1)}, u32[]{:S(2)}, u32[]{:S(2)}) collective-permute-start(bf16[512,256]{1,0:T(8,128)(2,1)S(1)} %get-tuple-element.52), channel_id=1, source_target_pairs={{0,126},{1,127},{2,0},{3,1},{4,2},{5,3},{6,4},{7,5},{8,6},{9,7},{1... | collective-permute-start | bytes 786440 | tf_op jit(solution)/shard_map/ppermute | solution.py:396
  51.7 5.8 %collective-permute-start.7 = (bf16[512,256]{1,0:T(8,128)(2,1)S(1)}, bf16[512,256]{1,0:T(8,128)(2,1)S(1)}, u32[]{:S(2)}, u32[]{:S(2)}) collective-permute-start(bf16[512,256]{1,0:T(8,128)(2,1)S(1)} %get-tuple-element.53), channel_id=1, source_target_pairs={{0,124},{1,125},{2,126},{3,127},{4,0},{5,1},{6,2},{7,3},{8,4},{9,5... | collective-permute-start | bytes 786440 | tf_op jit(solution)/shard_map/ppermute | solution.py:396
  57.5 0.0 collective-permute-done.5.kv1
  57.5 0.0 collective-permute-done.4.kv2
  57.5 12.2 %attend.3 = (bf16[256,512]{1,0:T(8,128)(2,1)S(1)}, bf16[256,512]{1,0:T(8,128)(2,1)S(1)}, f32[1024,128]{1,0:T(8,128)}, f32[512,256]{1,0:T(8,128)S(1)}, bf16[512,2...) custom-call(f32[256,128]{1,0:T(8,128)S(1)} %get-tuple-element.38.pos_ref, bf16[256,2048]{1,0:T(8,128)(2,1)S(1)} %copy-done, ...), custom_call_target="tpu_custom_call" | custom-call | flops 5000000000 | bytes 4000000 | tf_op jit(solution)/shard_map/attend/pallas_call | solution.py:282
  69.7 0.0 copy-done.5
  69.7 0.0 copy-done.7
  69.7 0.0 copy-start.3
  69.7 0.8 copy-done.3
  70.5 0.0 collective-permute-done.6.refs_1_
  70.5 0.0 collective-permute-done.7.refs_2_
  70.5 0.9 collective-permute-start.8
  71.5 0.1 collective-permute-start.9
  71.5 3.3 %collective-permute-start.10 = (bf16[256,512]{1,0:T(8,128)(2,1)S(1)}, bf16[256,512]{1,0:T(8,128)(2,1)S(1)}, u32[]{:S(2)}, u32[]{:S(2)}) collective-permute-start(bf16[256,512]{1,0:T(8,128)(2,1)S(1)} %get-tuple-element.61), channel_id=1, source_target_pairs={{0,1},{1,0},{2,3},{3,2},{4,5},{5,4},{6,7},{7,6},{8,9},{9,8},{10,11... | collective-permute-start | bytes 786440 | tf_op jit(solution)/shard_map/ppermute | solution.py:391
  74.8 0.0 collective-permute-start.11
  74.8 5.8 %all-to-all-start.1 = ((f32[128,8,128]{2,1,0:T(8,128)}), f32[128,8,128]{2,1,0:T(8,128)S(1)}, u32[]{:S(2)}, u32[]{:S(2)}) async-start(f32[128,8,128]{2,1,0:T(8,128)} %bitcast.6), calls=%async_computation.1 | async-start | bytes 1048576 | tf_op jit(solution)/shard_map/all_to_all | solution.py:400
  80.7 1.2 %collective-permute-done.8.refs_4_ = bf16[512,256]{1,0:T(8,128)(2,1)S(1)} collective-permute-done((bf16[512,256]{1,0:T(8,128)(2,1)S(1)}, bf16[512,256]{1,0:T(8,128)(2,1)S(1)}, u32[]{:S(2)}, u32[]{:S(2)}) %collective-permute-start.8) | collective-permute-done | bytes 262176 | tf_op jit(solution)/shard_map/ppermute | solution.py:396
  81.9 1.3 %collective-permute-done.9.refs_5_ = bf16[512,256]{1,0:T(8,128)(2,1)S(1)} collective-permute-done((bf16[512,256]{1,0:T(8,128)(2,1)S(1)}, bf16[512,256]{1,0:T(8,128)(2,1)S(1)}, u32[]{:S(2)}, u32[]{:S(2)}) %collective-permute-start.9) | collective-permute-done | bytes 262176 | tf_op jit(solution)/shard_map/ppermute | solution.py:396
  83.1 0.0 collective-permute-done.10.refs_7_
  83.1 0.0 collective-permute-done.11.refs_9_
  83.1 0.0 copy-start.4
  83.2 1.0 %copy-done.4 = f32[512,256]{1,0:T(8,128)S(1)} copy-done((f32[512,256]{1,0:T(8,128)S(1)}, f32[512,256]{1,0:T(8,128)}, u32[]{:S(2)}) %copy-start.4) | copy-done | bytes 524312
  84.2 0.0 copy-start.6
  84.2 1.0 %copy-done.6 = f32[512,256]{1,0:T(8,128)S(1)} copy-done((f32[512,256]{1,0:T(8,128)S(1)}, f32[512,256]{1,0:T(8,128)}, u32[]{:S(2)}) %copy-start.6) | copy-done | bytes 524312
  85.2 0.0 copy-start.8
  85.2 0.9 copy-done.8
  86.2 1.1 %gather.1 = (f32[256,512]{1,0:T(8,128)S(1)}, bf16[256,256]{1,0:T(8,128)(2,1)S(1)}, bf16[256,256]{1,0:T(8,128)(2,1)S(1)}, bf16[256,2048]{1,0:T(8,128)(2,1)}) custom-call(f32[512,256]{1,0:T(8,128)S(1)} %copy-done.6, bf16[512,256]{1,0:T(8,128)(2,1)S(1)} %collective-permute-done.6.refs_1_, bf16[512,256]{1,0:T(8,128)(2,1)S(1)} %collective-permute-done.7.refs_2_, ...), custom_call_target="tpu_custom_call" | custom-call | flops 6000000000 | bytes 6000000 | tf_op jit(solution)/shard_map/gather/pallas_call | solution.py:336
  87.3 5.7 %collective-permute-start.12 = (bf16[256,256]{1,0:T(8,128)(2,1)S(1)}, bf16[256,256]{1,0:T(8,128)(2,1)S(1)}, u32[]{:S(2)}, u32[]{:S(2)}) collective-permute-start(bf16[256,256]{1,0:T(8,128)(2,1)S(1)} %get-tuple-element.66), channel_id=1, source_target_pairs={{0,1},{1,0},{2,3},{3,2},{4,5},{5,4},{6,7},{7,6},{8,9},{9,8},{10,11... | collective-permute-start | bytes 393224 | tf_op jit(solution)/shard_map/ppermute | solution.py:391
  93.0 0.0 collective-permute-start.13
  93.0 1.0 %collective-permute-done.12.recv0_ref = bf16[256,256]{1,0:T(8,128)(2,1)S(1)} collective-permute-done((bf16[256,256]{1,0:T(8,128)(2,1)S(1)}, bf16[256,256]{1,0:T(8,128)(2,1)S(1)}, u32[]{:S(2)}, u32[]{:S(2)}) %collective-permute-start.12) | collective-permute-done | bytes 131104 | tf_op jit(solution)/shard_map/ppermute | solution.py:391
  94.0 0.4 collective-permute-done.13.recv1_ref
  94.4 0.0 all-to-all-done.1.share_ref
  94.4 1.6 %finish.1 = (bf16[256,512]{1,0:T(8,128)(2,1)}, bf16[256,512]{1,0:T(8,128)(2,1)}) custom-call(s32[256]{0:T(256)S(1)} %copy-done.2, f32[256,512]{1,0:T(8,128)S(1)} %get-tuple-element.65.mine_ref, bf16[256,256]{1,0:T(8,128)(2,1)S(1)} %collective-permute-done.12.recv0_ref, bf16[256,256]{1,0:T(8,128)(2,1)S(1)} %collective-permute-done.13.recv1_ref, ...), custom_call_target="tpu_custom_call" | custom-call | tf_op jit(solution)/shard_map/finish/pallas_call | solution.py:380
  (4 shorter events, 0.1 us)
Async XLA Ops:
  4.1 12.9 %collective-permute-start.1 = (bf16[2,256,256]{2,1,0:T(8,128)(2,1)}, bf16[2,256,256]{2,1,0:T(8,128)(2,1)S(1)}, u32[]{:S(2)}, u32[]{:S(2)}) collective-permute-start(bf16[2,256,256]{2,1,0:T(8,128)(2,1)} %get-tuple-element.41), channel_id=1, source_target_pairs={{0,1},{1,0},{2,3},{3,2},{4,5},{5,4},{6,7},{7,6},{8,9},{9,8},{10,11... | collective-permute-start | bytes 786440 | tf_op jit(solution)/shard_map/ppermute | solution.py:391
  5.6 11.3 %copy-start.9 = (bf16[2,256,256]{2,1,0:T(8,128)(2,1)S(1)}, bf16[2,256,256]{2,1,0:T(8,128)(2,1)}, u32[]{:S(2)}) copy-start(bf16[2,256,256]{2,1,0:T(8,128)(2,1)} %get-tuple-element.40) | copy-start | bytes 786436
  5.6 21.5 %all-to-all-start = ((bf16[128,8,128]{2,1,0:T(8,128)(2,1)}), bf16[128,8,128]{2,1,0:T(8,128)(2,1)S(1)}, u32[]{:S(2)}, u32[]{:S(2)}) async-start(bf16[128,8,128]{2,1,0:T(8,128)(2,1)} %get-tuple-element.37), calls=%async_computation | async-start | bytes 524288 | tf_op jit(solution)/shard_map/all_to_all | solution.py:400
  15.8 21.4 %collective-permute-start = (bf16[256,2048]{1,0:T(8,128)(2,1)}, bf16[256,2048]{1,0:T(8,128)(2,1)S(1)}, u32[]{:S(2)}, u32[]{:S(2)}) collective-permute-start(bf16[256,2048]{1,0:T(8,128)(2,1)} %get-tuple-element.39), channel_id=1, source_target_pairs={{0,1},{1,0},{2,3},{3,2},{4,5},{5,4},{6,7},{7,6},{8,9},{9,8},{10,11... | collective-permute-start | bytes 3145736 | tf_op jit(solution)/shard_map/ppermute | solution.py:391
  17.1 19.0 %collective-permute-start.3 = (bf16[512,256]{1,0:T(8,128)(2,1)S(1)}, bf16[512,256]{1,0:T(8,128)(2,1)S(1)}, u32[]{:S(2)}, u32[]{:S(2)}) collective-permute-start(bf16[512,256]{1,0:T(8,128)(2,1)S(1)} %pad_maximum_fusion.kv0), channel_id=1, source_target_pairs={{0,2},{1,3},{2,4},{3,5},{4,6},{5,7},{6,8},{7,9},{8,10},{9,11},{10,... | collective-permute-start | bytes 786440 | tf_op jit(solution)/shard_map/ppermute | solution.py:396
  18.0 19.3 %collective-permute-start.2 = (bf16[512,256]{1,0:T(8,128)(2,1)S(1)}, bf16[512,256]{1,0:T(8,128)(2,1)S(1)}, u32[]{:S(2)}, u32[]{:S(2)}) collective-permute-start(bf16[512,256]{1,0:T(8,128)(2,1)S(1)} %pad_maximum_fusion.kv0), channel_id=1, source_target_pairs={{0,4},{1,5},{2,6},{3,7},{4,8},{5,9},{6,10},{7,11},{8,12},{9,13},{1... | collective-permute-start | bytes 786440 | tf_op jit(solution)/shard_map/ppermute | solution.py:396
  27.2 0.7 copy-start.2
  27.8 9.4 %copy-start = (bf16[256,2048]{1,0:T(8,128)(2,1)S(1)}, bf16[256,2048]{1,0:T(8,128)(2,1)}, u32[]{:S(2)}) copy-start(bf16[256,2048]{1,0:T(8,128)(2,1)} %q_hbm.5) | copy-start | bytes 3145732
  27.8 9.4 %copy-start.1 = (bf16[256,2048]{1,0:T(8,128)(2,1)S(1)}, bf16[256,2048]{1,0:T(8,128)(2,1)}, u32[]{:S(2)}) copy-start(bf16[256,2048]{1,0:T(8,128)(2,1)} %d_hbm.5) | copy-start | bytes 3145732
  28.0 29.4 %collective-permute-start.5 = (bf16[512,256]{1,0:T(8,128)(2,1)S(1)}, bf16[512,256]{1,0:T(8,128)(2,1)S(1)}, u32[]{:S(2)}, u32[]{:S(2)}) collective-permute-start(bf16[512,256]{1,0:T(8,128)(2,1)S(1)} %pad_maximum_fusion.1.kv0), channel_id=1, source_target_pairs={{0,2},{1,3},{2,4},{3,5},{4,6},{5,7},{6,8},{7,9},{8,10},{9,11},{10,... | collective-permute-start | bytes 786440 | tf_op jit(solution)/shard_map/ppermute | solution.py:396
  28.1 29.3 %collective-permute-start.4 = (bf16[512,256]{1,0:T(8,128)(2,1)S(1)}, bf16[512,256]{1,0:T(8,128)(2,1)S(1)}, u32[]{:S(2)}, u32[]{:S(2)}) collective-permute-start(bf16[512,256]{1,0:T(8,128)(2,1)S(1)} %pad_maximum_fusion.1.kv0), channel_id=1, source_target_pairs={{0,4},{1,5},{2,6},{3,7},{4,8},{5,9},{6,10},{7,11},{8,12},{9,13},{1... | collective-permute-start | bytes 786440 | tf_op jit(solution)/shard_map/ppermute | solution.py:396
  49.0 20.8 %copy-start.5 = (f32[512,256]{1,0:T(8,128)}, f32[512,256]{1,0:T(8,128)S(1)}, u32[]{:S(2)}) copy-start(f32[512,256]{1,0:T(8,128)S(1)} %get-tuple-element.43.refs_0_) | copy-start | bytes 1572868
  49.0 20.8 %copy-start.7 = (bf16[256,512]{1,0:T(8,128)(2,1)}, bf16[256,512]{1,0:T(8,128)(2,1)S(1)}, u32[]{:S(2)}) copy-start(bf16[256,512]{1,0:T(8,128)(2,1)S(1)} %get-tuple-element.60.refs_6_) | copy-start | bytes 786436
  49.0 21.6 %collective-permute-start.6 = (bf16[512,256]{1,0:T(8,128)(2,1)S(1)}, bf16[512,256]{1,0:T(8,128)(2,1)S(1)}, u32[]{:S(2)}, u32[]{:S(2)}) collective-permute-start(bf16[512,256]{1,0:T(8,128)(2,1)S(1)} %get-tuple-element.52), channel_id=1, source_target_pairs={{0,126},{1,127},{2,0},{3,1},{4,2},{5,3},{6,4},{7,5},{8,6},{9,7},{1... | collective-permute-start | bytes 786440 | tf_op jit(solution)/shard_map/ppermute | solution.py:396
  51.7 18.9 %collective-permute-start.7 = (bf16[512,256]{1,0:T(8,128)(2,1)S(1)}, bf16[512,256]{1,0:T(8,128)(2,1)S(1)}, u32[]{:S(2)}, u32[]{:S(2)}) collective-permute-start(bf16[512,256]{1,0:T(8,128)(2,1)S(1)} %get-tuple-element.53), channel_id=1, source_target_pairs={{0,124},{1,125},{2,126},{3,127},{4,0},{5,1},{6,2},{7,3},{8,4},{9,5... | collective-permute-start | bytes 786440 | tf_op jit(solution)/shard_map/ppermute | solution.py:396
  69.7 0.8 copy-start.3
  70.5 11.3 %collective-permute-start.8 = (bf16[512,256]{1,0:T(8,128)(2,1)S(1)}, bf16[512,256]{1,0:T(8,128)(2,1)S(1)}, u32[]{:S(2)}, u32[]{:S(2)}) collective-permute-start(bf16[512,256]{1,0:T(8,128)(2,1)S(1)} %get-tuple-element.58), channel_id=1, source_target_pairs={{0,126},{1,127},{2,0},{3,1},{4,2},{5,3},{6,4},{7,5},{8,6},{9,7},{1... | collective-permute-start | bytes 786440 | tf_op jit(solution)/shard_map/ppermute | solution.py:396
  71.5 11.7 %collective-permute-start.9 = (bf16[512,256]{1,0:T(8,128)(2,1)S(1)}, bf16[512,256]{1,0:T(8,128)(2,1)S(1)}, u32[]{:S(2)}, u32[]{:S(2)}) collective-permute-start(bf16[512,256]{1,0:T(8,128)(2,1)S(1)} %get-tuple-element.59), channel_id=1, source_target_pairs={{0,124},{1,125},{2,126},{3,127},{4,0},{5,1},{6,2},{7,3},{8,4},{9,5... | collective-permute-start | bytes 786440 | tf_op jit(solution)/shard_map/ppermute | solution.py:396
  71.5 11.6 %collective-permute-start.10 = (bf16[256,512]{1,0:T(8,128)(2,1)S(1)}, bf16[256,512]{1,0:T(8,128)(2,1)S(1)}, u32[]{:S(2)}, u32[]{:S(2)}) collective-permute-start(bf16[256,512]{1,0:T(8,128)(2,1)S(1)} %get-tuple-element.61), channel_id=1, source_target_pairs={{0,1},{1,0},{2,3},{3,2},{4,5},{5,4},{6,7},{7,6},{8,9},{9,8},{10,11... | collective-permute-start | bytes 786440 | tf_op jit(solution)/shard_map/ppermute | solution.py:391
  74.8 8.3 %collective-permute-start.11 = (bf16[256,512]{1,0:T(8,128)(2,1)S(1)}, bf16[256,512]{1,0:T(8,128)(2,1)S(1)}, u32[]{:S(2)}, u32[]{:S(2)}) collective-permute-start(bf16[256,512]{1,0:T(8,128)(2,1)S(1)} %get-tuple-element.63), channel_id=1, source_target_pairs={{0,1},{1,0},{2,3},{3,2},{4,5},{5,4},{6,7},{7,6},{8,9},{9,8},{10,11... | collective-permute-start | bytes 786440 | tf_op jit(solution)/shard_map/ppermute | solution.py:391
  74.8 19.5 %all-to-all-start.1 = ((f32[128,8,128]{2,1,0:T(8,128)}), f32[128,8,128]{2,1,0:T(8,128)S(1)}, u32[]{:S(2)}, u32[]{:S(2)}) async-start(f32[128,8,128]{2,1,0:T(8,128)} %bitcast.6), calls=%async_computation.1 | async-start | bytes 1048576 | tf_op jit(solution)/shard_map/all_to_all | solution.py:400
  83.1 1.0 %copy-start.4 = (f32[512,256]{1,0:T(8,128)S(1)}, f32[512,256]{1,0:T(8,128)}, u32[]{:S(2)}) copy-start(f32[512,256]{1,0:T(8,128)} %copy-done.3) | copy-start | bytes 1572868
  84.2 1.0 %copy-start.6 = (f32[512,256]{1,0:T(8,128)S(1)}, f32[512,256]{1,0:T(8,128)}, u32[]{:S(2)}) copy-start(f32[512,256]{1,0:T(8,128)} %copy-done.5) | copy-start | bytes 1572868
  85.2 0.9 copy-start.8
  87.3 6.7 %collective-permute-start.12 = (bf16[256,256]{1,0:T(8,128)(2,1)S(1)}, bf16[256,256]{1,0:T(8,128)(2,1)S(1)}, u32[]{:S(2)}, u32[]{:S(2)}) collective-permute-start(bf16[256,256]{1,0:T(8,128)(2,1)S(1)} %get-tuple-element.66), channel_id=1, source_target_pairs={{0,1},{1,0},{2,3},{3,2},{4,5},{5,4},{6,7},{7,6},{8,9},{9,8},{10,11... | collective-permute-start | bytes 393224 | tf_op jit(solution)/shard_map/ppermute | solution.py:391
  93.0 1.3 %collective-permute-start.13 = (bf16[256,256]{1,0:T(8,128)(2,1)S(1)}, bf16[256,256]{1,0:T(8,128)(2,1)S(1)}, u32[]{:S(2)}, u32[]{:S(2)}) collective-permute-start(bf16[256,256]{1,0:T(8,128)(2,1)S(1)} %get-tuple-element.67), channel_id=1, source_target_pairs={{0,1},{1,0},{2,3},{3,2},{4,5},{5,4},{6,7},{7,6},{8,9},{9,8},{10,11... | collective-permute-start | bytes 393224 | tf_op jit(solution)/shard_map/ppermute | solution.py:391

commit v3 on v2

--- a/solution.py
+++ b/solution.py
@@ -44,18 +44,31 @@
         copy.wait()
 
 
-def pack_kernel(pos_ref, k_ref, v_ref, q_hbm, d_hbm, own_ref, send_ref, block_ref, qd_ref, sem):
+def pack_kernel(
+    pos_ref, k_hbm, v_hbm, q_hbm, d_hbm, own_hbm, send_hbm, block_hbm, qd_hbm,
+    k_ref, v_ref, own_ref, send_ref, block_ref, qd_ref, sem, out_sem,
+):
     index, _, core = place()
-    copies = []
+    outs = []
+
+    def send(src, dst):
+        outs.append(pltpu.make_async_copy(src, dst, out_sem.at[len(outs)]))
+        outs[-1].start()
+
+    loads = [pltpu.make_async_copy(k_hbm, k_ref, sem.at[0]), pltpu.make_async_copy(v_hbm, v_ref, sem.at[1])]
     for i, ref in enumerate((q_hbm, d_hbm)):
         src = ref.at[:, window((1 - core) * 1024, 1024)]
-        copies.append(pltpu.make_async_copy(src, qd_ref.at[:, i * 1024 : (i + 1) * 1024], sem.at[i]))
-        copies[-1].start()
-    for out, which in ((own_ref, core), (send_ref, 1 - core)):
+        loads.append(pltpu.make_async_copy(src, qd_ref.at[i], sem.at[2 + i]))
+    for load in loads:
+        load.start()
+    loads[0].wait()
+    loads[1].wait()
+    for out, hbm, which in ((send_ref, send_hbm, 1 - core), (own_ref, own_hbm, core)):
         for g in range(2):
             cols = window((2 * which + g) * HEAD, HEAD)
             out[g, :, :HEAD] = k_ref[:, cols]
             out[g, :, HEAD:] = v_ref[:, cols]
+        send(out, hbm)
     slot = lax.broadcasted_iota(jnp.int32, (8, ROWS), 0)
     row = lax.broadcasted_iota(jnp.int32, (8, ROWS), 1)
     first = pos_ref[2 * index] - index * ROWS
@@ -72,23 +85,36 @@
         tiles.append(tile.astype(BF))
     for device in range(block_ref.shape[0]):
         block_ref[device] = tiles[device % 2]
-    for copy in copies:
-        copy.wait()
+    send(block_ref, block_hbm)
+    for i in range(2):
+        loads[2 + i].wait()
+        send(qd_ref.at[i], qd_hbm.at[:, i * 1024 : (i + 1) * 1024])
+    for done in outs:
+        done.wait()
 
 
 def pack(pos, keys, values, queries, cotangent):
     shape = jax.ShapeDtypeStruct
     return pl.pallas_call(
         pack_kernel,
-        in_specs=[SM, VM, VM, HBM, HBM],
-        out_specs=[VM] * 4,
+        in_specs=[SM, HBM, HBM, HBM, HBM],
+        out_specs=[HBM] * 4,
         out_shape=[
             shape((2, ROWS, 2 * HEAD), BF),
             shape((2, ROWS, 2 * HEAD), BF),
             shape((128, 8, HEAD), BF),
             shape((ROWS, 2048), BF),
         ],
-        scratch_shapes=[pltpu.SemaphoreType.DMA((2,))],
+        scratch_shapes=[
+            pltpu.VMEM((ROWS, 512), BF),
+            pltpu.VMEM((ROWS, 512), BF),
+            pltpu.VMEM((2, ROWS, 256), BF),
+            pltpu.VMEM((2, ROWS, 256), BF),
+            pltpu.VMEM((128, 8, HEAD), BF),
+            pltpu.VMEM((2, ROWS, 1024), BF),
+            pltpu.SemaphoreType.DMA((4,)),
+            pltpu.SemaphoreType.DMA((5,)),
+        ],
         compiler_params=pltpu.CompilerParams(vmem_limit_bytes=60 << 20),
         name="pack",
     )(pos, keys, values, queries, cotangent)
@@ -126,10 +152,10 @@
 
 
 def attend_kernel(g, pos_ref, q_hbm, d_hbm, qd_hbm, kv2, kv1, kv0, summ, *rest):
-    before, rest = (rest[0], rest[1:]) if g else (None, rest)
+    before, rest = (rest[:3], rest[3:]) if g else (None, rest)
     dqo_hbm, dqs_hbm, gs_hbm, grad_hbm = rest[0], rest[1], rest[2], rest[3:6]
     (k_sc, v_sc, kt_sc, vt_sc, s_sc, q_sc, d_sc, dq_sc, dk_sc, dv_sc, lim_sc, lims_sc) = rest[6:18]
-    own_sc, bf_sc, gs_sc, sem, out_sem = rest[18:]
+    own_sc, bf_sc, gs_sc, gsb_sc, dq_before, sem, out_sem = rest[18:]
     _, chip, core = place()
     mine = window(core * ROWS, ROWS)
     theirs = window((1 - core) * ROWS, ROWS)
@@ -140,7 +166,9 @@
         copies[-1].start()
 
     if g:
-        copy(before, gs_sc)
+        copy(before[0], gs_sc)
+        copy(before[1], own_sc.at[:, :256])
+        copy(before[2], dq_before)
     copy(q_hbm.at[:, window(core * 1024 + g * 512, 512)], q_sc.at[mine])
     copy(d_hbm.at[:, window(core * 1024 + g * 512, 512)], d_sc.at[mine])
     copy(qd_hbm.at[:, g * 512 : (g + 1) * 512], q_sc.at[theirs])
@@ -175,22 +203,28 @@
         outs[-1].start()
 
     def emit():
-        send(dq_sc.at[mine], dqo_hbm)
+        if g:
+            send(dq_before, dqo_hbm.at[:, :512])
+            send(dq_sc.at[mine], dqo_hbm.at[:, 512:])
+        else:
+            send(dq_sc.at[mine], dqo_hbm)
         send(dq_sc.at[theirs], dqs_hbm)
         dk_sc[1536:, :] = dk_sc[1536:, :] * SCALE
         for i, acc in enumerate((dk_sc, dv_sc)):
             for r in range(2):
                 slots = pl.ds(4 * g + 2 * i + r, 128, stride=8)
                 gs_sc[slots, :] = acc[pl.ds(1536 + r, 128, stride=2), :]
-        send(gs_sc, gs_hbm)
+        if g:
+            gsb_sc[...] = gs_sc[...].astype(BF)
+        send(gsb_sc if g else gs_sc, gs_hbm)
         for i, hbm in enumerate(grad_hbm):
             for part in range(2):
                 at = window((2 - i) * 512 + (core if part == 0 else 1 - core) * ROWS, ROWS)
                 rows = slice(part * ROWS, (part + 1) * ROWS)
-                stage, kind = (own_sc, F32) if i == 0 else (bf_sc.at[i - 1], BF)
+                stage, kind = (own_sc.at[:, g * 256 :], F32) if i == 0 else (bf_sc.at[i - 1], BF)
                 stage[rows, :HEAD] = (dk_sc[at, :] * SCALE).astype(kind)
                 stage[rows, HEAD:] = dv_sc[at, :].astype(kind)
-            send(stage, hbm)
+            send(own_sc if i == 0 else stage, hbm)
 
     factor = SCALE * LOG2E
 
@@ -281,13 +315,13 @@
     shape = jax.ShapeDtypeStruct
     return pl.pallas_call(
         functools.partial(attend_kernel, g),
-        in_specs=[VM, HBM, HBM] + [ANY] * (5 + g),
+        in_specs=[VM, HBM, HBM] + [ANY] * (5 + 3 * g),
         out_specs=[HBM] * 6,
         out_shape=[
+            shape((ROWS, 512 + 512 * g), BF),
             shape((ROWS, 512), BF),
-            shape((ROWS, 512), BF),
-            shape((1024, HEAD), F32),
-            shape((512, 256), F32),
+            shape((1024, HEAD), BF if g else F32),
+            shape((512, 256 + 256 * g), F32),
             shape((512, 256), BF),
             shape((512, 256), BF),
         ],
@@ -304,10 +338,12 @@
             pltpu.VMEM((SPAN, HEAD), F32),
             pltpu.VMEM((3, ROWS, ROWS), F32),
             pltpu.VMEM((2, ROWS, ROWS), F32),
-            pltpu.VMEM((512, 256), F32),
+            pltpu.VMEM((512, 256 + 256 * g), F32),
             pltpu.VMEM((2, 512, 256), BF),
             pltpu.VMEM((1024, HEAD), F32),
-            pltpu.SemaphoreType.DMA((22,)),
+            pltpu.VMEM((1024, HEAD), BF),
+            pltpu.VMEM((ROWS, 512), BF),
+            pltpu.SemaphoreType.DMA((24,)),
             pltpu.SemaphoreType.DMA((8,)),
         ],
         compiler_params=pltpu.CompilerParams(vmem_limit_bytes=24 << 20),
@@ -318,24 +354,22 @@
     )(*args)
 
 
-def gather_kernel(*refs):
-    parts = (refs[:3], refs[3:6])
-    dq_parts, mine_ref, theirs, dq_ref = refs[6:10], refs[10], refs[11:13], refs[13]
+def gather_kernel(own, b10, b20, b11, b21, dq_own, dqr0, dqr1, mine_ref, their0, their1, dq_ref):
     core = place()[2]
-    for g, (own, back1, back2) in enumerate(parts):
-        total = own[...] + back1[...].astype(F32) + back2[...].astype(F32)
-        mine_ref[:, g * 256 : (g + 1) * 256] = total[:ROWS]
-        theirs[g][...] = total[ROWS:].astype(BF)
-    for i, ref in enumerate(dq_parts):
-        which = core if i % 2 == 0 else 1 - core
-        dq_ref[:, window((2 * which + i // 2) * 512, 512)] = ref[...]
+    for g, (back1, back2, their) in enumerate(((b10, b20, their0), (b11, b21, their1))):
+        cols = slice(g * 256, (g + 1) * 256)
+        total = own[:, cols] + back1[...].astype(F32) + back2[...].astype(F32)
+        mine_ref[:, cols] = total[:ROWS]
+        their[...] = total[ROWS:].astype(BF)
+        dq_ref[:, window(((1 - core) * 2 + g) * 512, 512)] = (dqr0, dqr1)[g][...]
+    dq_ref[:, window(core * 1024, 1024)] = dq_own[...]
 
 
 def gather(*args):
     shape = jax.ShapeDtypeStruct
     return pl.pallas_call(
         gather_kernel,
-        in_specs=[VM] * 10,
+        in_specs=[VM] * 8,
         out_specs=[VM] * 4,
         out_shape=[
             shape((ROWS, 512), F32),
@@ -356,9 +390,9 @@
     second = pos_ref[2 * index + 1] - index * ROWS
     shares = []
     for source in range(2):
-        share = share_ref[source]
+        share = share_ref[source].astype(F32)
         for i in range(1, share_ref.shape[0] // 2):
-            share = share + share_ref[2 * i + source]
+            share = share + share_ref[2 * i + source].astype(F32)
         shares.append(share)
     for half in range(2):
         which = core if half == 0 else 1 - core
@@ -412,12 +446,12 @@
     outs = attend(0, pos, queries, cotangent, qd, kv2[0], kv1[0], kv0[0], sk0)
     dq0, dqs0, summ_grad, own0, back1, back2 = outs
     back1_0, back2_0 = to_chip(back1, -1), to_chip(back2, -2)
-    outs = attend(1, pos, queries, cotangent, qd, kv2[1], kv1[1], kv0[1], sk1, summ_grad)
+    outs = attend(1, pos, queries, cotangent, qd, kv2[1], kv1[1], kv0[1], sk1, summ_grad, own0, dq0)
     outs, back1_0, back2_0, dqs0 = lax.optimization_barrier((outs, back1_0, back2_0, dqs0))
-    dq1, dqs1, summ_grad, own1, back1, back2 = outs
+    dq_own, dqs1, summ_grad, own, back1, back2 = outs
     back1_1, back2_1 = to_chip(back1, -1), to_chip(back2, -2)
     mine, theirs0, theirs1, query_grad = gather(
-        own0, back1_0, back2_0, own1, back1_1, back2_1, dq0, to_sibling(dqs0), dq1, to_sibling(dqs1)
+        own, back1_0, back2_0, back1_1, back2_1, dq_own, to_sibling(dqs0), to_sibling(dqs1)
     )
     shares = exchange(summ_grad.reshape(128, 8, HEAD))
     key_grad, value_gradient = finish(

time: 96.4 us -> 93.2 us (0.967)
  starting transfers between devices: 42.9 us -> 40.4 us
  local copies, waits for them, and re-layouts: 4.57 us -> 2.92 us
  waiting for transfers between devices: 17.4 us -> 18.7 us
    ppermute x6, starting transfers between devices: 11.7 us -> 9.29 us  [to_sibling(): lax.ppermute(block, 'ctx', [(i, i ^ 1) for i in range(lax.axis_size('ctx'...]
    all_to_all x2, waiting for transfers between devices: 6.27 us -> 8.55 us  [exchange(): return lax.all_to_all(block, 'ctx', 0, 0, tiled=True)]
    unnamed x20 -> x12, local copies, waits for them, and re-layouts: 4.54 us -> 2.88 us
    ppermute x6, waiting for transfers between devices: 1.36 us -> 0.02 us  [to_sibling(): lax.ppermute(block, 'ctx', [(i, i ^ 1) for i in range(lax.axis_size('ctx'...]
  transfers between devices with their start and end apart: 16 -> 16, of which waited for: 7 -> 6; matrix products, arithmetic and copies ran while one was open for 0% -> 0% of each run, Pallas kernels for 26% -> 27%
where the time goes in v3:
time: 93.2 us; the launch traced here: 92.9 us
  starting transfers between devices  40.4 us (43%)
  Pallas kernels  30.1 us (32%)
  waiting for transfers between devices  18.7 us (20%)
  local copies, waits for them, and re-layouts  2.92 us (3%)
    pallas_call x2, Pallas kernels, attend(): pl.pallas_call(functools.partial(attend_kernel, g), in_specs=[VM, HBM, HB...  24 us
    all_to_all x2, starting transfers between devices, exchange(): return lax.all_to_all(block, 'ctx', 0, 0, tiled=True)  16 us
    ppermute x8, starting transfers between devices, to_chip(): lax.ppermute(block, 'ctx', [(i, (i + 2 * hops) % size ^ flip) for i in ra...  15.1 us
    ppermute x8, waiting for transfers between devices, to_chip(): lax.ppermute(block, 'ctx', [(i, (i + 2 * hops) % size ^ flip) for i in ra...  10.1 us
    ppermute x6, starting transfers between devices, to_sibling(): lax.ppermute(block, 'ctx', [(i, i ^ 1) for i in range(lax.axis_size('ctx'...  9.29 us
    all_to_all x2, waiting for transfers between devices, exchange(): return lax.all_to_all(block, 'ctx', 0, 0, tiled=True)  8.55 us
    pallas_call x1, Pallas kernels, pack(): pl.pallas_call(pack_kernel, in_specs=[SM, HBM, HBM, HBM, HBM], out_specs=...  3.15 us
    unnamed x12, local copies, waits for them, and re-layouts  2.88 us
  transfers between devices with their start and end apart: 16, of which 6 were waited for; matrix products, arithmetic and copies ran while one was open for 0% of the time, Pallas kernels for 27%

profile of v3, /device:TPU:1, one launch (start us, length us, event | category | flops | bytes accessed | tf_op | source)
XLA Modules:
  0.0 92.9 jit_solution(5704104280258100540)
XLA Ops:
  0.6 3.2 %pack.1 = (bf16[2,256,256]{2,1,0:T(8,128)(2,1)}, bf16[2,256,256]{2,1,0:T(8,128)(2,1)}, bf16[128,8,128]{2,1,0:T(8,128)(2,1)}, bf16[256,2048]{1,0:T(8,128)(2,1)}) custom-call(s32[256]{0:T(256)} %pos_ref.3, bf16[256,512]{1,0:T(8,128)(2,1)} %k_hbm.1, bf16[256,512]{1,0:T(8,128)(2,1)} %v_hbm.1, bf16[256,2048]{1,0:T(8,128)(2,1)} %q_hbm.5, bf16[256,2048]{1,0:T(8,128)(2,1)} %d_hbm.5), custom_call_target="tpu_custom_call" | custom-call | tf_op jit(solution)/shard_map/pack/pallas_call | solution.py:98
  3.8 1.5 %collective-permute-start.1 = (bf16[2,256,256]{2,1,0:T(8,128)(2,1)}, bf16[2,256,256]{2,1,0:T(8,128)(2,1)S(1)}, u32[]{:S(2)}, u32[]{:S(2)}) collective-permute-start(bf16[2,256,256]{2,1,0:T(8,128)(2,1)} %get-tuple-element.41), channel_id=1, source_target_pairs={{0,1},{1,0},{2,3},{3,2},{4,5},{5,4},{6,7},{7,6},{8,9},{9,8},{10,11... | collective-permute-start | bytes 786440 | tf_op jit(solution)/shard_map/ppermute | solution.py:425
  5.3 0.0 copy-start.5
  5.3 10.2 %all-to-all-start = ((bf16[128,8,128]{2,1,0:T(8,128)(2,1)}), bf16[128,8,128]{2,1,0:T(8,128)(2,1)S(1)}, u32[]{:S(2)}, u32[]{:S(2)}) async-start(bf16[128,8,128]{2,1,0:T(8,128)(2,1)} %get-tuple-element.37), calls=%async_computation | async-start | bytes 524288 | tf_op jit(solution)/shard_map/all_to_all | solution.py:434
  15.5 1.1 %collective-permute-start = (bf16[256,2048]{1,0:T(8,128)(2,1)}, bf16[256,2048]{1,0:T(8,128)(2,1)S(1)}, u32[]{:S(2)}, u32[]{:S(2)}) collective-permute-start(bf16[256,2048]{1,0:T(8,128)(2,1)} %get-tuple-element.39), channel_id=1, source_target_pairs={{0,1},{1,0},{2,3},{3,2},{4,5},{5,4},{6,7},{7,6},{8,9},{9,8},{10,11... | collective-permute-start | bytes 3145736 | tf_op jit(solution)/shard_map/ppermute | solution.py:425
  16.6 0.0 copy-done.5
  16.7 0.0 collective-permute-done.1
  16.7 0.9 collective-permute-start.5
  17.6 2.9 %collective-permute-start.4 = (bf16[512,256]{1,0:T(8,128)(2,1)S(1)}, bf16[512,256]{1,0:T(8,128)(2,1)S(1)}, u32[]{:S(2)}, u32[]{:S(2)}) collective-permute-start(bf16[512,256]{1,0:T(8,128)(2,1)S(1)} %pad_maximum_fusion.1.kv0), channel_id=1, source_target_pairs={{0,4},{1,5},{2,6},{3,7},{4,8},{5,9},{6,10},{7,11},{8,12},{9,13},{1... | collective-permute-start | bytes 786440 | tf_op jit(solution)/shard_map/ppermute | solution.py:430
  20.5 6.3 %all-to-all-done = bf16[128,8,128]{2,1,0:T(8,128)(2,1)S(1)} async-done(((bf16[128,8,128]{2,1,0:T(8,128)(2,1)}), bf16[128,8,128]{2,1,0:T(8,128)(2,1)S(1)}, u32[]{:S(2)}, u32[]{:S(2)}) %all-to-all-start) | async-done | bytes 262176 | tf_op jit(solution)/shard_map/all_to_all | solution.py:434
  26.8 0.0 copy-start.2
  26.8 0.7 copy-done.2
  27.5 0.0 copy-start
  27.5 0.0 copy-start.1
  27.5 0.2 unpack.1
  27.7 0.1 collective-permute-start.3
  27.8 1.8 %collective-permute-start.2 = (bf16[512,256]{1,0:T(8,128)(2,1)S(1)}, bf16[512,256]{1,0:T(8,128)(2,1)S(1)}, u32[]{:S(2)}, u32[]{:S(2)}) collective-permute-start(bf16[512,256]{1,0:T(8,128)(2,1)S(1)} %pad_maximum_fusion.kv0), channel_id=1, source_target_pairs={{0,4},{1,5},{2,6},{3,7},{4,8},{5,9},{6,10},{7,11},{8,12},{9,13},{1... | collective-permute-start | bytes 786440 | tf_op jit(solution)/shard_map/ppermute | solution.py:430
  29.6 6.1 %collective-permute-done.5.kv1 = bf16[512,256]{1,0:T(8,128)(2,1)S(1)} collective-permute-done((bf16[512,256]{1,0:T(8,128)(2,1)S(1)}, bf16[512,256]{1,0:T(8,128)(2,1)S(1)}, u32[]{:S(2)}, u32[]{:S(2)}) %collective-permute-start.5) | collective-permute-done | bytes 262176 | tf_op jit(solution)/shard_map/ppermute | solution.py:430
  35.7 1.2 %collective-permute-done.4.kv2 = bf16[512,256]{1,0:T(8,128)(2,1)S(1)} collective-permute-done((bf16[512,256]{1,0:T(8,128)(2,1)S(1)}, bf16[512,256]{1,0:T(8,128)(2,1)S(1)}, u32[]{:S(2)}, u32[]{:S(2)}) %collective-permute-start.4) | collective-permute-done | bytes 262176 | tf_op jit(solution)/shard_map/ppermute | solution.py:430
  36.9 0.0 collective-permute-done.qd_hbm
  36.9 0.0 copy-done
  36.9 0.0 copy-done.1
  36.9 11.7 %attend.2 = (bf16[256,512]{1,0:T(8,128)(2,1)S(1)}, bf16[256,512]{1,0:T(8,128)(2,1)S(1)}, f32[1024,128]{1,0:T(8,128)S(1)}, f32[512,256]{1,0:T(8,128)S(1)}, bf16[5...) custom-call(f32[256,128]{1,0:T(8,128)S(1)} %get-tuple-element.38.pos_ref, bf16[256,2048]{1,0:T(8,128)(2,1)S(1)} %copy-done, ...), custom_call_target="tpu_custom_call" | custom-call | flops 5000000000 | bytes 4000000 | tf_op jit(solution)/shard_map/attend/pallas_call | solution.py:316
  48.6 2.7 %collective-permute-start.6 = (bf16[512,256]{1,0:T(8,128)(2,1)S(1)}, bf16[512,256]{1,0:T(8,128)(2,1)S(1)}, u32[]{:S(2)}, u32[]{:S(2)}) collective-permute-start(bf16[512,256]{1,0:T(8,128)(2,1)S(1)} %get-tuple-element.53), channel_id=1, source_target_pairs={{0,126},{1,127},{2,0},{3,1},{4,2},{5,3},{6,4},{7,5},{8,6},{9,7},{1... | collective-permute-start | bytes 786440 | tf_op jit(solution)/shard_map/ppermute | solution.py:430
  51.3 5.8 %collective-permute-start.7 = (bf16[512,256]{1,0:T(8,128)(2,1)S(1)}, bf16[512,256]{1,0:T(8,128)(2,1)S(1)}, u32[]{:S(2)}, u32[]{:S(2)}) collective-permute-start(bf16[512,256]{1,0:T(8,128)(2,1)S(1)} %get-tuple-element.54), channel_id=1, source_target_pairs={{0,124},{1,125},{2,126},{3,127},{4,0},{5,1},{6,2},{7,3},{8,4},{9,5... | collective-permute-start | bytes 786440 | tf_op jit(solution)/shard_map/ppermute | solution.py:430
  57.1 0.0 collective-permute-done.3.kv1
  57.1 0.0 collective-permute-done.2.kv2
  57.1 12.3 %attend.3 = (bf16[256,1024]{1,0:T(8,128)(2,1)S(1)}, bf16[256,512]{1,0:T(8,128)(2,1)S(1)}, bf16[1024,128]{1,0:T(8,128)(2,1)}, f32[512,512]{1,0:T(8,128)S(1)}, bf1...) custom-call(f32[256,128]{1,0:T(8,128)S(1)} %get-tuple-element.38.pos_ref, bf16[256,2048]{1,0:T(8,128)(2,1)S(1)} %copy-done, ...), custom_call_target="tpu_custom_call" | custom-call | flops 5000000000 | bytes 4000000 | tf_op jit(solution)/shard_map/attend/pallas_call | solution.py:316
  69.4 0.0 copy-start.3
  69.4 1.0 %copy-done.3 = f32[512,512]{1,0:T(8,128)} copy-done((f32[512,512]{1,0:T(8,128)}, f32[512,512]{1,0:T(8,128)S(1)}, u32[]{:S(2)}) %copy-start.3) | copy-done | bytes 1048600
  70.4 0.0 collective-permute-done.6.b10
  70.4 0.0 collective-permute-done.7.b20
  70.4 0.9 collective-permute-start.8
  71.3 0.0 collective-permute-start.9
  71.3 3.1 %collective-permute-start.10 = (bf16[256,512]{1,0:T(8,128)(2,1)S(1)}, bf16[256,512]{1,0:T(8,128)(2,1)S(1)}, u32[]{:S(2)}, u32[]{:S(2)}) collective-permute-start(bf16[256,512]{1,0:T(8,128)(2,1)S(1)} %get-tuple-element.62), channel_id=1, source_target_pairs={{0,1},{1,0},{2,3},{3,2},{4,5},{5,4},{6,7},{7,6},{8,9},{9,8},{10,11... | collective-permute-start | bytes 786440 | tf_op jit(solution)/shard_map/ppermute | solution.py:425
  74.5 0.0 collective-permute-start.11
  74.5 5.8 %all-to-all-start.1 = ((bf16[128,8,128]{2,1,0:T(8,128)(2,1)}), bf16[128,8,128]{2,1,0:T(8,128)(2,1)S(1)}, u32[]{:S(2)}, u32[]{:S(2)}) async-start(bf16[128,8,128]{2,1,0:T(8,128)(2,1)} %bitcast.6), calls=%async_computation.1 | async-start | bytes 524288 | tf_op jit(solution)/shard_map/all_to_all | solution.py:434
  80.3 1.5 %collective-permute-done.8.b11 = bf16[512,256]{1,0:T(8,128)(2,1)S(1)} collective-permute-done((bf16[512,256]{1,0:T(8,128)(2,1)S(1)}, bf16[512,256]{1,0:T(8,128)(2,1)S(1)}, u32[]{:S(2)}, u32[]{:S(2)}) %collective-permute-start.8) | collective-permute-done | bytes 262176 | tf_op jit(solution)/shard_map/ppermute | solution.py:430
  81.9 1.2 %collective-permute-done.9.b21 = bf16[512,256]{1,0:T(8,128)(2,1)S(1)} collective-permute-done((bf16[512,256]{1,0:T(8,128)(2,1)S(1)}, bf16[512,256]{1,0:T(8,128)(2,1)S(1)}, u32[]{:S(2)}, u32[]{:S(2)}) %collective-permute-start.9) | collective-permute-done | bytes 262176 | tf_op jit(solution)/shard_map/ppermute | solution.py:430
  83.1 0.0 collective-permute-done.10.dqr0
  83.1 0.0 collective-permute-done.11.dqr1
  83.1 0.0 copy-start.4
  83.1 1.2 %copy-done.4 = f32[512,512]{1,0:T(8,128)S(1)} copy-done((f32[512,512]{1,0:T(8,128)S(1)}, f32[512,512]{1,0:T(8,128)}, u32[]{:S(2)}) %copy-start.4) | copy-done | bytes 1048600
  84.3 1.1 %gather.1 = (f32[256,512]{1,0:T(8,128)S(1)}, bf16[256,256]{1,0:T(8,128)(2,1)S(1)}, bf16[256,256]{1,0:T(8,128)(2,1)S(1)}, bf16[256,2048]{1,0:T(8,128)(2,1)}) custom-call(f32[512,512]{1,0:T(8,128)S(1)} %copy-done.4, bf16[512,256]{1,0:T(8,128)(2,1)S(1)} %collective-permute-done.6.b10, bf16[512,256]{1,0:T(8,128)(2,1)S(1)} %collective-permute-done.7.b20, ...), custom_call_target="tpu_custom_call" | custom-call | flops 6000000000 | bytes 6000000 | tf_op jit(solution)/shard_map/gather/pallas_call | solution.py:370
  85.5 3.5 %collective-permute-start.12 = (bf16[256,256]{1,0:T(8,128)(2,1)S(1)}, bf16[256,256]{1,0:T(8,128)(2,1)S(1)}, u32[]{:S(2)}, u32[]{:S(2)}) collective-permute-start(bf16[256,256]{1,0:T(8,128)(2,1)S(1)} %get-tuple-element.66), channel_id=1, source_target_pairs={{0,1},{1,0},{2,3},{3,2},{4,5},{5,4},{6,7},{7,6},{8,9},{9,8},{10,11... | collective-permute-start | bytes 393224 | tf_op jit(solution)/shard_map/ppermute | solution.py:425
  88.9 0.0 collective-permute-start.13
  89.0 2.3 %all-to-all-done.1.share_ref = bf16[128,8,128]{2,1,0:T(8,128)(2,1)S(1)} async-done(((bf16[128,8,128]{2,1,0:T(8,128)(2,1)}), bf16[128,8,128]{2,1,0:T(8,128)(2,1)S(1)}, u32[]{:S(2)}, u32[]{:S(2)}) %all-to-all-start.1) | async-done | bytes 262176 | tf_op jit(solution)/shard_map/all_to_all | solution.py:434
  91.2 0.0 collective-permute-done.12.recv0_ref
  91.2 0.0 collective-permute-done.13.recv1_ref
  91.2 1.6 %finish.1 = (bf16[256,512]{1,0:T(8,128)(2,1)}, bf16[256,512]{1,0:T(8,128)(2,1)}) custom-call(s32[256]{0:T(256)S(1)} %copy-done.2, f32[256,512]{1,0:T(8,128)S(1)} %get-tuple-element.65.mine_ref, bf16[256,256]{1,0:T(8,128)(2,1)S(1)} %collective-permute-done.12.recv0_ref, bf16[256,256]{1,0:T(8,128)(2,1)S(1)} %collective-permute-done.13.recv1_ref, ...), custom_call_target="tpu_custom_call" | custom-call | tf_op jit(solution)/shard_map/finish/pallas_call | solution.py:414
  (4 shorter events, 0.1 us)
Async XLA Ops:
  3.8 12.9 %collective-permute-start.1 = (bf16[2,256,256]{2,1,0:T(8,128)(2,1)}, bf16[2,256,256]{2,1,0:T(8,128)(2,1)S(1)}, u32[]{:S(2)}, u32[]{:S(2)}) collective-permute-start(bf16[2,256,256]{2,1,0:T(8,128)(2,1)} %get-tuple-element.41), channel_id=1, source_target_pairs={{0,1},{1,0},{2,3},{3,2},{4,5},{5,4},{6,7},{7,6},{8,9},{9,8},{10,11... | collective-permute-start | bytes 786440 | tf_op jit(solution)/shard_map/ppermute | solution.py:425
  5.3 11.3 %copy-start.5 = (bf16[2,256,256]{2,1,0:T(8,128)(2,1)S(1)}, bf16[2,256,256]{2,1,0:T(8,128)(2,1)}, u32[]{:S(2)}) copy-start(bf16[2,256,256]{2,1,0:T(8,128)(2,1)} %get-tuple-element.40) | copy-start | bytes 786436
  5.3 21.5 %all-to-all-start = ((bf16[128,8,128]{2,1,0:T(8,128)(2,1)}), bf16[128,8,128]{2,1,0:T(8,128)(2,1)S(1)}, u32[]{:S(2)}, u32[]{:S(2)}) async-start(bf16[128,8,128]{2,1,0:T(8,128)(2,1)} %get-tuple-element.37), calls=%async_computation | async-start | bytes 524288 | tf_op jit(solution)/shard_map/all_to_all | solution.py:434
  15.5 21.4 %collective-permute-start = (bf16[256,2048]{1,0:T(8,128)(2,1)}, bf16[256,2048]{1,0:T(8,128)(2,1)S(1)}, u32[]{:S(2)}, u32[]{:S(2)}) collective-permute-start(bf16[256,2048]{1,0:T(8,128)(2,1)} %get-tuple-element.39), channel_id=1, source_target_pairs={{0,1},{1,0},{2,3},{3,2},{4,5},{5,4},{6,7},{7,6},{8,9},{9,8},{10,11... | collective-permute-start | bytes 3145736 | tf_op jit(solution)/shard_map/ppermute | solution.py:425
  16.7 19.0 %collective-permute-start.5 = (bf16[512,256]{1,0:T(8,128)(2,1)S(1)}, bf16[512,256]{1,0:T(8,128)(2,1)S(1)}, u32[]{:S(2)}, u32[]{:S(2)}) collective-permute-start(bf16[512,256]{1,0:T(8,128)(2,1)S(1)} %pad_maximum_fusion.1.kv0), channel_id=1, source_target_pairs={{0,2},{1,3},{2,4},{3,5},{4,6},{5,7},{6,8},{7,9},{8,10},{9,11},{10,... | collective-permute-start | bytes 786440 | tf_op jit(solution)/shard_map/ppermute | solution.py:430
  17.6 19.3 %collective-permute-start.4 = (bf16[512,256]{1,0:T(8,128)(2,1)S(1)}, bf16[512,256]{1,0:T(8,128)(2,1)S(1)}, u32[]{:S(2)}, u32[]{:S(2)}) collective-permute-start(bf16[512,256]{1,0:T(8,128)(2,1)S(1)} %pad_maximum_fusion.1.kv0), channel_id=1, source_target_pairs={{0,4},{1,5},{2,6},{3,7},{4,8},{5,9},{6,10},{7,11},{8,12},{9,13},{1... | collective-permute-start | bytes 786440 | tf_op jit(solution)/shard_map/ppermute | solution.py:430
  26.8 0.7 copy-start.2
  27.5 9.4 %copy-start = (bf16[256,2048]{1,0:T(8,128)(2,1)S(1)}, bf16[256,2048]{1,0:T(8,128)(2,1)}, u32[]{:S(2)}) copy-start(bf16[256,2048]{1,0:T(8,128)(2,1)} %q_hbm.5) | copy-start | bytes 3145732
  27.5 9.4 %copy-start.1 = (bf16[256,2048]{1,0:T(8,128)(2,1)S(1)}, bf16[256,2048]{1,0:T(8,128)(2,1)}, u32[]{:S(2)}) copy-start(bf16[256,2048]{1,0:T(8,128)(2,1)} %d_hbm.5) | copy-start | bytes 3145732
  27.7 29.4 %collective-permute-start.3 = (bf16[512,256]{1,0:T(8,128)(2,1)S(1)}, bf16[512,256]{1,0:T(8,128)(2,1)S(1)}, u32[]{:S(2)}, u32[]{:S(2)}) collective-permute-start(bf16[512,256]{1,0:T(8,128)(2,1)S(1)} %pad_maximum_fusion.kv0), channel_id=1, source_target_pairs={{0,2},{1,3},{2,4},{3,5},{4,6},{5,7},{6,8},{7,9},{8,10},{9,11},{10,... | collective-permute-start | bytes 786440 | tf_op jit(solution)/shard_map/ppermute | solution.py:430
  27.8 29.3 %collective-permute-start.2 = (bf16[512,256]{1,0:T(8,128)(2,1)S(1)}, bf16[512,256]{1,0:T(8,128)(2,1)S(1)}, u32[]{:S(2)}, u32[]{:S(2)}) collective-permute-start(bf16[512,256]{1,0:T(8,128)(2,1)S(1)} %pad_maximum_fusion.kv0), channel_id=1, source_target_pairs={{0,4},{1,5},{2,6},{3,7},{4,8},{5,9},{6,10},{7,11},{8,12},{9,13},{1... | collective-permute-start | bytes 786440 | tf_op jit(solution)/shard_map/ppermute | solution.py:430
  48.6 21.8 %collective-permute-start.6 = (bf16[512,256]{1,0:T(8,128)(2,1)S(1)}, bf16[512,256]{1,0:T(8,128)(2,1)S(1)}, u32[]{:S(2)}, u32[]{:S(2)}) collective-permute-start(bf16[512,256]{1,0:T(8,128)(2,1)S(1)} %get-tuple-element.53), channel_id=1, source_target_pairs={{0,126},{1,127},{2,0},{3,1},{4,2},{5,3},{6,4},{7,5},{8,6},{9,7},{1... | collective-permute-start | bytes 786440 | tf_op jit(solution)/shard_map/ppermute | solution.py:430
  51.3 19.1 %collective-permute-start.7 = (bf16[512,256]{1,0:T(8,128)(2,1)S(1)}, bf16[512,256]{1,0:T(8,128)(2,1)S(1)}, u32[]{:S(2)}, u32[]{:S(2)}) collective-permute-start(bf16[512,256]{1,0:T(8,128)(2,1)S(1)} %get-tuple-element.54), channel_id=1, source_target_pairs={{0,124},{1,125},{2,126},{3,127},{4,0},{5,1},{6,2},{7,3},{8,4},{9,5... | collective-permute-start | bytes 786440 | tf_op jit(solution)/shard_map/ppermute | solution.py:430
  69.4 1.0 %copy-start.3 = (f32[512,512]{1,0:T(8,128)}, f32[512,512]{1,0:T(8,128)S(1)}, u32[]{:S(2)}) copy-start(f32[512,512]{1,0:T(8,128)S(1)} %get-tuple-element.56.own) | copy-start | bytes 3145732
  70.4 11.4 %collective-permute-start.8 = (bf16[512,256]{1,0:T(8,128)(2,1)S(1)}, bf16[512,256]{1,0:T(8,128)(2,1)S(1)}, u32[]{:S(2)}, u32[]{:S(2)}) collective-permute-start(bf16[512,256]{1,0:T(8,128)(2,1)S(1)} %get-tuple-element.59), channel_id=1, source_target_pairs={{0,126},{1,127},{2,0},{3,1},{4,2},{5,3},{6,4},{7,5},{8,6},{9,7},{1... | collective-permute-start | bytes 786440 | tf_op jit(solution)/shard_map/ppermute | solution.py:430
  71.3 11.8 %collective-permute-start.9 = (bf16[512,256]{1,0:T(8,128)(2,1)S(1)}, bf16[512,256]{1,0:T(8,128)(2,1)S(1)}, u32[]{:S(2)}, u32[]{:S(2)}) collective-permute-start(bf16[512,256]{1,0:T(8,128)(2,1)S(1)} %get-tuple-element.60), channel_id=1, source_target_pairs={{0,124},{1,125},{2,126},{3,127},{4,0},{5,1},{6,2},{7,3},{8,4},{9,5... | collective-permute-start | bytes 786440 | tf_op jit(solution)/shard_map/ppermute | solution.py:430
  71.3 11.8 %collective-permute-start.10 = (bf16[256,512]{1,0:T(8,128)(2,1)S(1)}, bf16[256,512]{1,0:T(8,128)(2,1)S(1)}, u32[]{:S(2)}, u32[]{:S(2)}) collective-permute-start(bf16[256,512]{1,0:T(8,128)(2,1)S(1)} %get-tuple-element.62), channel_id=1, source_target_pairs={{0,1},{1,0},{2,3},{3,2},{4,5},{5,4},{6,7},{7,6},{8,9},{9,8},{10,11... | collective-permute-start | bytes 786440 | tf_op jit(solution)/shard_map/ppermute | solution.py:425
  74.5 8.6 %collective-permute-start.11 = (bf16[256,512]{1,0:T(8,128)(2,1)S(1)}, bf16[256,512]{1,0:T(8,128)(2,1)S(1)}, u32[]{:S(2)}, u32[]{:S(2)}) collective-permute-start(bf16[256,512]{1,0:T(8,128)(2,1)S(1)} %get-tuple-element.63), channel_id=1, source_target_pairs={{0,1},{1,0},{2,3},{3,2},{4,5},{5,4},{6,7},{7,6},{8,9},{9,8},{10,11... | collective-permute-start | bytes 786440 | tf_op jit(solution)/shard_map/ppermute | solution.py:425
  74.5 16.8 %all-to-all-start.1 = ((bf16[128,8,128]{2,1,0:T(8,128)(2,1)}), bf16[128,8,128]{2,1,0:T(8,128)(2,1)S(1)}, u32[]{:S(2)}, u32[]{:S(2)}) async-start(bf16[128,8,128]{2,1,0:T(8,128)(2,1)} %bitcast.6), calls=%async_computation.1 | async-start | bytes 524288 | tf_op jit(solution)/shard_map/all_to_all | solution.py:434
  83.1 1.2 %copy-start.4 = (f32[512,512]{1,0:T(8,128)S(1)}, f32[512,512]{1,0:T(8,128)}, u32[]{:S(2)}) copy-start(f32[512,512]{1,0:T(8,128)} %copy-done.3) | copy-start | bytes 3145732
  85.5 5.8 %collective-permute-start.12 = (bf16[256,256]{1,0:T(8,128)(2,1)S(1)}, bf16[256,256]{1,0:T(8,128)(2,1)S(1)}, u32[]{:S(2)}, u32[]{:S(2)}) collective-permute-start(bf16[256,256]{1,0:T(8,128)(2,1)S(1)} %get-tuple-element.66), channel_id=1, source_target_pairs={{0,1},{1,0},{2,3},{3,2},{4,5},{5,4},{6,7},{7,6},{8,9},{9,8},{10,11... | collective-permute-start | bytes 393224 | tf_op jit(solution)/shard_map/ppermute | solution.py:425
  88.9 2.3 %collective-permute-start.13 = (bf16[256,256]{1,0:T(8,128)(2,1)S(1)}, bf16[256,256]{1,0:T(8,128)(2,1)S(1)}, u32[]{:S(2)}, u32[]{:S(2)}) collective-permute-start(bf16[256,256]{1,0:T(8,128)(2,1)S(1)} %get-tuple-element.67), channel_id=1, source_target_pairs={{0,1},{1,0},{2,3},{3,2},{4,5},{5,4},{6,7},{7,6},{8,9},{9,8},{10,11... | collective-permute-start | bytes 393224 | tf_op jit(solution)/shard_map/ppermute | solution.py:425

commit v4 on v3

--- a/solution.py
+++ b/solution.py
@@ -188,8 +188,6 @@
         lim_sc[b] = jnp.where((ki > qi) & (chip * 2 + b >= 4), BIG, NEG)
         lims_sc[b] = jnp.where(pos <= ((chip * 2 + b) * ROWS + qi).astype(F32), BIG, NEG)
     lim_sc[2] = jnp.where(ki <= qi, BIG, NEG)
-    dk_sc[...] = jnp.zeros_like(dk_sc)
-    dv_sc[...] = jnp.zeros_like(dv_sc)
     for done in copies:
         done.wait()
     for i in range(7):
@@ -279,8 +277,13 @@
         dp = dot(v_sc[keys, :], u["dt"])
         p = s_sc[u["slot"], at, :] * u["inv"]
         ds = (p * (dp - u["delta"])).astype(BF)
-        dk_sc[keys, :] += dot(ds, u["q"])
-        dv_sc[keys, :] += dot(p.astype(BF), u["d"])
+        dk, dv = dot(ds, u["q"]), dot(p.astype(BF), u["d"])
+        if u["h"] == 0 and (u["b"] == 0 or t == 4):
+            dk_sc[keys, :] = dk
+            dv_sc[keys, :] = dv
+        else:
+            dk_sc[keys, :] += dk
+            dv_sc[keys, :] += dv
         dq = dot(kt_sc[:, keys], ds)
         u["dq"] = dq if u["dq"] is None else u["dq"] + dq
 

time: 93.2 us -> 93 us (level)
  no operation moved by 1% of the time
where the time goes in v4:
time: 93 us; the launch traced here: 92.7 us
  starting transfers between devices  40.6 us (44%)
  Pallas kernels  29.8 us (32%)
  waiting for transfers between devices  18.6 us (20%)
  local copies, waits for them, and re-layouts  2.92 us (3%)
    pallas_call x2, Pallas kernels, attend(): pl.pallas_call(functools.partial(attend_kernel, g), in_specs=[VM, HBM, HB...  23.8 us
    all_to_all x2, starting transfers between devices, exchange(): return lax.all_to_all(block, 'ctx', 0, 0, tiled=True)  16 us
    ppermute x8, starting transfers between devices, to_chip(): lax.ppermute(block, 'ctx', [(i, (i + 2 * hops) % size ^ flip) for i in ra...  15.1 us
    ppermute x8, waiting for transfers between devices, to_chip(): lax.ppermute(block, 'ctx', [(i, (i + 2 * hops) % size ^ flip) for i in ra...  10 us
    ppermute x6, starting transfers between devices, to_sibling(): lax.ppermute(block, 'ctx', [(i, i ^ 1) for i in range(lax.axis_size('ctx'...  9.45 us
    all_to_all x2, waiting for transfers between devices, exchange(): return lax.all_to_all(block, 'ctx', 0, 0, tiled=True)  8.6 us
    pallas_call x1, Pallas kernels, pack(): pl.pallas_call(pack_kernel, in_specs=[SM, HBM, HBM, HBM, HBM], out_specs=...  3.15 us
    unnamed x12, local copies, waits for them, and re-layouts  2.88 us
  transfers between devices with their start and end apart: 16, of which 6 were waited for; matrix products, arithmetic and copies ran while one was open for 0% of the time, Pallas kernels for 27%

profile of v4, /device:TPU:1, one launch (start us, length us, event | category | flops | bytes accessed | tf_op | source)
XLA Modules:
  0.0 92.7 jit_solution(5953350406309105900)
XLA Ops:
  0.6 3.2 %pack.1 = (bf16[2,256,256]{2,1,0:T(8,128)(2,1)}, bf16[2,256,256]{2,1,0:T(8,128)(2,1)}, bf16[128,8,128]{2,1,0:T(8,128)(2,1)}, bf16[256,2048]{1,0:T(8,128)(2,1)}) custom-call(s32[256]{0:T(256)} %pos_ref.3, bf16[256,512]{1,0:T(8,128)(2,1)} %k_hbm.1, bf16[256,512]{1,0:T(8,128)(2,1)} %v_hbm.1, bf16[256,2048]{1,0:T(8,128)(2,1)} %q_hbm.5, bf16[256,2048]{1,0:T(8,128)(2,1)} %d_hbm.5), custom_call_target="tpu_custom_call" | custom-call | tf_op jit(solution)/shard_map/pack/pallas_call | solution.py:98
  3.8 1.5 %collective-permute-start.1 = (bf16[2,256,256]{2,1,0:T(8,128)(2,1)}, bf16[2,256,256]{2,1,0:T(8,128)(2,1)S(1)}, u32[]{:S(2)}, u32[]{:S(2)}) collective-permute-start(bf16[2,256,256]{2,1,0:T(8,128)(2,1)} %get-tuple-element.41), channel_id=1, source_target_pairs={{0,1},{1,0},{2,3},{3,2},{4,5},{5,4},{6,7},{7,6},{8,9},{9,8},{10,11... | collective-permute-start | bytes 786440 | tf_op jit(solution)/shard_map/ppermute | solution.py:428
  5.3 0.0 copy-start.5
  5.3 10.2 %all-to-all-start = ((bf16[128,8,128]{2,1,0:T(8,128)(2,1)}), bf16[128,8,128]{2,1,0:T(8,128)(2,1)S(1)}, u32[]{:S(2)}, u32[]{:S(2)}) async-start(bf16[128,8,128]{2,1,0:T(8,128)(2,1)} %get-tuple-element.37), calls=%async_computation | async-start | bytes 524288 | tf_op jit(solution)/shard_map/all_to_all | solution.py:437
  15.5 1.1 %collective-permute-start = (bf16[256,2048]{1,0:T(8,128)(2,1)}, bf16[256,2048]{1,0:T(8,128)(2,1)S(1)}, u32[]{:S(2)}, u32[]{:S(2)}) collective-permute-start(bf16[256,2048]{1,0:T(8,128)(2,1)} %get-tuple-element.39), channel_id=1, source_target_pairs={{0,1},{1,0},{2,3},{3,2},{4,5},{5,4},{6,7},{7,6},{8,9},{9,8},{10,11... | collective-permute-start | bytes 3145736 | tf_op jit(solution)/shard_map/ppermute | solution.py:428
  16.6 0.0 copy-done.5
  16.7 0.0 collective-permute-done.1
  16.7 0.9 collective-permute-start.5
  17.6 2.9 %collective-permute-start.4 = (bf16[512,256]{1,0:T(8,128)(2,1)S(1)}, bf16[512,256]{1,0:T(8,128)(2,1)S(1)}, u32[]{:S(2)}, u32[]{:S(2)}) collective-permute-start(bf16[512,256]{1,0:T(8,128)(2,1)S(1)} %pad_maximum_fusion.1.kv0), channel_id=1, source_target_pairs={{0,4},{1,5},{2,6},{3,7},{4,8},{5,9},{6,10},{7,11},{8,12},{9,13},{1... | collective-permute-start | bytes 786440 | tf_op jit(solution)/shard_map/ppermute | solution.py:433
  20.5 6.3 %all-to-all-done = bf16[128,8,128]{2,1,0:T(8,128)(2,1)S(1)} async-done(((bf16[128,8,128]{2,1,0:T(8,128)(2,1)}), bf16[128,8,128]{2,1,0:T(8,128)(2,1)S(1)}, u32[]{:S(2)}, u32[]{:S(2)}) %all-to-all-start) | async-done | bytes 262176 | tf_op jit(solution)/shard_map/all_to_all | solution.py:437
  26.8 0.0 copy-start.2
  26.8 0.7 copy-done.2
  27.5 0.0 copy-start
  27.5 0.0 copy-start.1
  27.5 0.2 unpack.1
  27.7 0.1 collective-permute-start.3
  27.8 1.8 %collective-permute-start.2 = (bf16[512,256]{1,0:T(8,128)(2,1)S(1)}, bf16[512,256]{1,0:T(8,128)(2,1)S(1)}, u32[]{:S(2)}, u32[]{:S(2)}) collective-permute-start(bf16[512,256]{1,0:T(8,128)(2,1)S(1)} %pad_maximum_fusion.kv0), channel_id=1, source_target_pairs={{0,4},{1,5},{2,6},{3,7},{4,8},{5,9},{6,10},{7,11},{8,12},{9,13},{1... | collective-permute-start | bytes 786440 | tf_op jit(solution)/shard_map/ppermute | solution.py:433
  29.6 6.1 %collective-permute-done.5.kv1 = bf16[512,256]{1,0:T(8,128)(2,1)S(1)} collective-permute-done((bf16[512,256]{1,0:T(8,128)(2,1)S(1)}, bf16[512,256]{1,0:T(8,128)(2,1)S(1)}, u32[]{:S(2)}, u32[]{:S(2)}) %collective-permute-start.5) | collective-permute-done | bytes 262176 | tf_op jit(solution)/shard_map/ppermute | solution.py:433
  35.7 1.2 %collective-permute-done.4.kv2 = bf16[512,256]{1,0:T(8,128)(2,1)S(1)} collective-permute-done((bf16[512,256]{1,0:T(8,128)(2,1)S(1)}, bf16[512,256]{1,0:T(8,128)(2,1)S(1)}, u32[]{:S(2)}, u32[]{:S(2)}) %collective-permute-start.4) | collective-permute-done | bytes 262176 | tf_op jit(solution)/shard_map/ppermute | solution.py:433
  36.9 0.0 collective-permute-done.qd_hbm
  36.9 0.0 copy-done
  36.9 0.0 copy-done.1
  36.9 11.6 %attend.2 = (bf16[256,512]{1,0:T(8,128)(2,1)S(1)}, bf16[256,512]{1,0:T(8,128)(2,1)S(1)}, f32[1024,128]{1,0:T(8,128)S(1)}, f32[512,256]{1,0:T(8,128)S(1)}, bf16[5...) custom-call(f32[256,128]{1,0:T(8,128)S(1)} %get-tuple-element.38.pos_ref, bf16[256,2048]{1,0:T(8,128)(2,1)S(1)} %copy-done, ...), custom_call_target="tpu_custom_call" | custom-call | flops 5000000000 | bytes 4000000 | tf_op jit(solution)/shard_map/attend/pallas_call | solution.py:319
  48.5 2.7 %collective-permute-start.6 = (bf16[512,256]{1,0:T(8,128)(2,1)S(1)}, bf16[512,256]{1,0:T(8,128)(2,1)S(1)}, u32[]{:S(2)}, u32[]{:S(2)}) collective-permute-start(bf16[512,256]{1,0:T(8,128)(2,1)S(1)} %get-tuple-element.53), channel_id=1, source_target_pairs={{0,126},{1,127},{2,0},{3,1},{4,2},{5,3},{6,4},{7,5},{8,6},{9,7},{1... | collective-permute-start | bytes 786440 | tf_op jit(solution)/shard_map/ppermute | solution.py:433
  51.2 5.8 %collective-permute-start.7 = (bf16[512,256]{1,0:T(8,128)(2,1)S(1)}, bf16[512,256]{1,0:T(8,128)(2,1)S(1)}, u32[]{:S(2)}, u32[]{:S(2)}) collective-permute-start(bf16[512,256]{1,0:T(8,128)(2,1)S(1)} %get-tuple-element.54), channel_id=1, source_target_pairs={{0,124},{1,125},{2,126},{3,127},{4,0},{5,1},{6,2},{7,3},{8,4},{9,5... | collective-permute-start | bytes 786440 | tf_op jit(solution)/shard_map/ppermute | solution.py:433
  57.0 0.0 collective-permute-done.3.kv1
  57.0 0.0 collective-permute-done.2.kv2
  57.0 12.2 %attend.3 = (bf16[256,1024]{1,0:T(8,128)(2,1)S(1)}, bf16[256,512]{1,0:T(8,128)(2,1)S(1)}, bf16[1024,128]{1,0:T(8,128)(2,1)}, f32[512,512]{1,0:T(8,128)S(1)}, bf1...) custom-call(f32[256,128]{1,0:T(8,128)S(1)} %get-tuple-element.38.pos_ref, bf16[256,2048]{1,0:T(8,128)(2,1)S(1)} %copy-done, ...), custom_call_target="tpu_custom_call" | custom-call | flops 5000000000 | bytes 4000000 | tf_op jit(solution)/shard_map/attend/pallas_call | solution.py:319
  69.2 0.0 copy-start.3
  69.2 1.0 %copy-done.3 = f32[512,512]{1,0:T(8,128)} copy-done((f32[512,512]{1,0:T(8,128)}, f32[512,512]{1,0:T(8,128)S(1)}, u32[]{:S(2)}) %copy-start.3) | copy-done | bytes 1048600
  70.2 0.0 collective-permute-done.6.b10
  70.2 0.0 collective-permute-done.7.b20
  70.2 0.9 collective-permute-start.8
  71.1 0.0 collective-permute-start.9
  71.1 3.3 %collective-permute-start.10 = (bf16[256,512]{1,0:T(8,128)(2,1)S(1)}, bf16[256,512]{1,0:T(8,128)(2,1)S(1)}, u32[]{:S(2)}, u32[]{:S(2)}) collective-permute-start(bf16[256,512]{1,0:T(8,128)(2,1)S(1)} %get-tuple-element.62), channel_id=1, source_target_pairs={{0,1},{1,0},{2,3},{3,2},{4,5},{5,4},{6,7},{7,6},{8,9},{9,8},{10,11... | collective-permute-start | bytes 786440 | tf_op jit(solution)/shard_map/ppermute | solution.py:428
  74.4 0.0 collective-permute-start.11
  74.4 5.8 %all-to-all-start.1 = ((bf16[128,8,128]{2,1,0:T(8,128)(2,1)}), bf16[128,8,128]{2,1,0:T(8,128)(2,1)S(1)}, u32[]{:S(2)}, u32[]{:S(2)}) async-start(bf16[128,8,128]{2,1,0:T(8,128)(2,1)} %bitcast.6), calls=%async_computation.1 | async-start | bytes 524288 | tf_op jit(solution)/shard_map/all_to_all | solution.py:437
  80.2 1.3 %collective-permute-done.8.b11 = bf16[512,256]{1,0:T(8,128)(2,1)S(1)} collective-permute-done((bf16[512,256]{1,0:T(8,128)(2,1)S(1)}, bf16[512,256]{1,0:T(8,128)(2,1)S(1)}, u32[]{:S(2)}, u32[]{:S(2)}) %collective-permute-start.8) | collective-permute-done | bytes 262176 | tf_op jit(solution)/shard_map/ppermute | solution.py:433
  81.5 1.4 %collective-permute-done.9.b21 = bf16[512,256]{1,0:T(8,128)(2,1)S(1)} collective-permute-done((bf16[512,256]{1,0:T(8,128)(2,1)S(1)}, bf16[512,256]{1,0:T(8,128)(2,1)S(1)}, u32[]{:S(2)}, u32[]{:S(2)}) %collective-permute-start.9) | collective-permute-done | bytes 262176 | tf_op jit(solution)/shard_map/ppermute | solution.py:433
  82.9 0.0 collective-permute-done.10.dqr0
  82.9 0.0 collective-permute-done.11.dqr1
  82.9 0.0 copy-start.4
  82.9 1.2 %copy-done.4 = f32[512,512]{1,0:T(8,128)S(1)} copy-done((f32[512,512]{1,0:T(8,128)S(1)}, f32[512,512]{1,0:T(8,128)}, u32[]{:S(2)}) %copy-start.4) | copy-done | bytes 1048600
  84.1 1.1 %gather.1 = (f32[256,512]{1,0:T(8,128)S(1)}, bf16[256,256]{1,0:T(8,128)(2,1)S(1)}, bf16[256,256]{1,0:T(8,128)(2,1)S(1)}, bf16[256,2048]{1,0:T(8,128)(2,1)}) custom-call(f32[512,512]{1,0:T(8,128)S(1)} %copy-done.4, bf16[512,256]{1,0:T(8,128)(2,1)S(1)} %collective-permute-done.6.b10, bf16[512,256]{1,0:T(8,128)(2,1)S(1)} %collective-permute-done.7.b20, ...), custom_call_target="tpu_custom_call" | custom-call | flops 6000000000 | bytes 6000000 | tf_op jit(solution)/shard_map/gather/pallas_call | solution.py:373
  85.2 3.5 %collective-permute-start.12 = (bf16[256,256]{1,0:T(8,128)(2,1)S(1)}, bf16[256,256]{1,0:T(8,128)(2,1)S(1)}, u32[]{:S(2)}, u32[]{:S(2)}) collective-permute-start(bf16[256,256]{1,0:T(8,128)(2,1)S(1)} %get-tuple-element.66), channel_id=1, source_target_pairs={{0,1},{1,0},{2,3},{3,2},{4,5},{5,4},{6,7},{7,6},{8,9},{9,8},{10,11... | collective-permute-start | bytes 393224 | tf_op jit(solution)/shard_map/ppermute | solution.py:428
  88.8 0.0 collective-permute-start.13
  88.8 2.3 %all-to-all-done.1.share_ref = bf16[128,8,128]{2,1,0:T(8,128)(2,1)S(1)} async-done(((bf16[128,8,128]{2,1,0:T(8,128)(2,1)}), bf16[128,8,128]{2,1,0:T(8,128)(2,1)S(1)}, u32[]{:S(2)}, u32[]{:S(2)}) %all-to-all-start.1) | async-done | bytes 262176 | tf_op jit(solution)/shard_map/all_to_all | solution.py:437
  91.1 0.0 collective-permute-done.12.recv0_ref
  91.1 0.0 collective-permute-done.13.recv1_ref
  91.1 1.6 %finish.1 = (bf16[256,512]{1,0:T(8,128)(2,1)}, bf16[256,512]{1,0:T(8,128)(2,1)}) custom-call(s32[256]{0:T(256)S(1)} %copy-done.2, f32[256,512]{1,0:T(8,128)S(1)} %get-tuple-element.65.mine_ref, bf16[256,256]{1,0:T(8,128)(2,1)S(1)} %collective-permute-done.12.recv0_ref, bf16[256,256]{1,0:T(8,128)(2,1)S(1)} %collective-permute-done.13.recv1_ref, ...), custom_call_target="tpu_custom_call" | custom-call | tf_op jit(solution)/shard_map/finish/pallas_call | solution.py:417
  (4 shorter events, 0.1 us)
Async XLA Ops:
  3.8 12.9 %collective-permute-start.1 = (bf16[2,256,256]{2,1,0:T(8,128)(2,1)}, bf16[2,256,256]{2,1,0:T(8,128)(2,1)S(1)}, u32[]{:S(2)}, u32[]{:S(2)}) collective-permute-start(bf16[2,256,256]{2,1,0:T(8,128)(2,1)} %get-tuple-element.41), channel_id=1, source_target_pairs={{0,1},{1,0},{2,3},{3,2},{4,5},{5,4},{6,7},{7,6},{8,9},{9,8},{10,11... | collective-permute-start | bytes 786440 | tf_op jit(solution)/shard_map/ppermute | solution.py:428
  5.3 11.3 %copy-start.5 = (bf16[2,256,256]{2,1,0:T(8,128)(2,1)S(1)}, bf16[2,256,256]{2,1,0:T(8,128)(2,1)}, u32[]{:S(2)}) copy-start(bf16[2,256,256]{2,1,0:T(8,128)(2,1)} %get-tuple-element.40) | copy-start | bytes 786436
  5.3 21.5 %all-to-all-start = ((bf16[128,8,128]{2,1,0:T(8,128)(2,1)}), bf16[128,8,128]{2,1,0:T(8,128)(2,1)S(1)}, u32[]{:S(2)}, u32[]{:S(2)}) async-start(bf16[128,8,128]{2,1,0:T(8,128)(2,1)} %get-tuple-element.37), calls=%async_computation | async-start | bytes 524288 | tf_op jit(solution)/shard_map/all_to_all | solution.py:437
  15.5 21.4 %collective-permute-start = (bf16[256,2048]{1,0:T(8,128)(2,1)}, bf16[256,2048]{1,0:T(8,128)(2,1)S(1)}, u32[]{:S(2)}, u32[]{:S(2)}) collective-permute-start(bf16[256,2048]{1,0:T(8,128)(2,1)} %get-tuple-element.39), channel_id=1, source_target_pairs={{0,1},{1,0},{2,3},{3,2},{4,5},{5,4},{6,7},{7,6},{8,9},{9,8},{10,11... | collective-permute-start | bytes 3145736 | tf_op jit(solution)/shard_map/ppermute | solution.py:428
  16.7 19.0 %collective-permute-start.5 = (bf16[512,256]{1,0:T(8,128)(2,1)S(1)}, bf16[512,256]{1,0:T(8,128)(2,1)S(1)}, u32[]{:S(2)}, u32[]{:S(2)}) collective-permute-start(bf16[512,256]{1,0:T(8,128)(2,1)S(1)} %pad_maximum_fusion.1.kv0), channel_id=1, source_target_pairs={{0,2},{1,3},{2,4},{3,5},{4,6},{5,7},{6,8},{7,9},{8,10},{9,11},{10,... | collective-permute-start | bytes 786440 | tf_op jit(solution)/shard_map/ppermute | solution.py:433
  17.6 19.3 %collective-permute-start.4 = (bf16[512,256]{1,0:T(8,128)(2,1)S(1)}, bf16[512,256]{1,0:T(8,128)(2,1)S(1)}, u32[]{:S(2)}, u32[]{:S(2)}) collective-permute-start(bf16[512,256]{1,0:T(8,128)(2,1)S(1)} %pad_maximum_fusion.1.kv0), channel_id=1, source_target_pairs={{0,4},{1,5},{2,6},{3,7},{4,8},{5,9},{6,10},{7,11},{8,12},{9,13},{1... | collective-permute-start | bytes 786440 | tf_op jit(solution)/shard_map/ppermute | solution.py:433
  26.8 0.7 copy-start.2
  27.5 9.4 %copy-start = (bf16[256,2048]{1,0:T(8,128)(2,1)S(1)}, bf16[256,2048]{1,0:T(8,128)(2,1)}, u32[]{:S(2)}) copy-start(bf16[256,2048]{1,0:T(8,128)(2,1)} %q_hbm.5) | copy-start | bytes 3145732
  27.5 9.4 %copy-start.1 = (bf16[256,2048]{1,0:T(8,128)(2,1)S(1)}, bf16[256,2048]{1,0:T(8,128)(2,1)}, u32[]{:S(2)}) copy-start(bf16[256,2048]{1,0:T(8,128)(2,1)} %d_hbm.5) | copy-start | bytes 3145732
  27.7 29.3 %collective-permute-start.3 = (bf16[512,256]{1,0:T(8,128)(2,1)S(1)}, bf16[512,256]{1,0:T(8,128)(2,1)S(1)}, u32[]{:S(2)}, u32[]{:S(2)}) collective-permute-start(bf16[512,256]{1,0:T(8,128)(2,1)S(1)} %pad_maximum_fusion.kv0), channel_id=1, source_target_pairs={{0,2},{1,3},{2,4},{3,5},{4,6},{5,7},{6,8},{7,9},{8,10},{9,11},{10,... | collective-permute-start | bytes 786440 | tf_op jit(solution)/shard_map/ppermute | solution.py:433
  27.8 29.2 %collective-permute-start.2 = (bf16[512,256]{1,0:T(8,128)(2,1)S(1)}, bf16[512,256]{1,0:T(8,128)(2,1)S(1)}, u32[]{:S(2)}, u32[]{:S(2)}) collective-permute-start(bf16[512,256]{1,0:T(8,128)(2,1)S(1)} %pad_maximum_fusion.kv0), channel_id=1, source_target_pairs={{0,4},{1,5},{2,6},{3,7},{4,8},{5,9},{6,10},{7,11},{8,12},{9,13},{1... | collective-permute-start | bytes 786440 | tf_op jit(solution)/shard_map/ppermute | solution.py:433
  48.5 21.7 %collective-permute-start.6 = (bf16[512,256]{1,0:T(8,128)(2,1)S(1)}, bf16[512,256]{1,0:T(8,128)(2,1)S(1)}, u32[]{:S(2)}, u32[]{:S(2)}) collective-permute-start(bf16[512,256]{1,0:T(8,128)(2,1)S(1)} %get-tuple-element.53), channel_id=1, source_target_pairs={{0,126},{1,127},{2,0},{3,1},{4,2},{5,3},{6,4},{7,5},{8,6},{9,7},{1... | collective-permute-start | bytes 786440 | tf_op jit(solution)/shard_map/ppermute | solution.py:433
  51.2 19.0 %collective-permute-start.7 = (bf16[512,256]{1,0:T(8,128)(2,1)S(1)}, bf16[512,256]{1,0:T(8,128)(2,1)S(1)}, u32[]{:S(2)}, u32[]{:S(2)}) collective-permute-start(bf16[512,256]{1,0:T(8,128)(2,1)S(1)} %get-tuple-element.54), channel_id=1, source_target_pairs={{0,124},{1,125},{2,126},{3,127},{4,0},{5,1},{6,2},{7,3},{8,4},{9,5... | collective-permute-start | bytes 786440 | tf_op jit(solution)/shard_map/ppermute | solution.py:433
  69.2 1.0 %copy-start.3 = (f32[512,512]{1,0:T(8,128)}, f32[512,512]{1,0:T(8,128)S(1)}, u32[]{:S(2)}) copy-start(f32[512,512]{1,0:T(8,128)S(1)} %get-tuple-element.56.own) | copy-start | bytes 3145732
  70.2 11.3 %collective-permute-start.8 = (bf16[512,256]{1,0:T(8,128)(2,1)S(1)}, bf16[512,256]{1,0:T(8,128)(2,1)S(1)}, u32[]{:S(2)}, u32[]{:S(2)}) collective-permute-start(bf16[512,256]{1,0:T(8,128)(2,1)S(1)} %get-tuple-element.59), channel_id=1, source_target_pairs={{0,126},{1,127},{2,0},{3,1},{4,2},{5,3},{6,4},{7,5},{8,6},{9,7},{1... | collective-permute-start | bytes 786440 | tf_op jit(solution)/shard_map/ppermute | solution.py:433
  71.1 11.8 %collective-permute-start.9 = (bf16[512,256]{1,0:T(8,128)(2,1)S(1)}, bf16[512,256]{1,0:T(8,128)(2,1)S(1)}, u32[]{:S(2)}, u32[]{:S(2)}) collective-permute-start(bf16[512,256]{1,0:T(8,128)(2,1)S(1)} %get-tuple-element.60), channel_id=1, source_target_pairs={{0,124},{1,125},{2,126},{3,127},{4,0},{5,1},{6,2},{7,3},{8,4},{9,5... | collective-permute-start | bytes 786440 | tf_op jit(solution)/shard_map/ppermute | solution.py:433
  71.1 11.8 %collective-permute-start.10 = (bf16[256,512]{1,0:T(8,128)(2,1)S(1)}, bf16[256,512]{1,0:T(8,128)(2,1)S(1)}, u32[]{:S(2)}, u32[]{:S(2)}) collective-permute-start(bf16[256,512]{1,0:T(8,128)(2,1)S(1)} %get-tuple-element.62), channel_id=1, source_target_pairs={{0,1},{1,0},{2,3},{3,2},{4,5},{5,4},{6,7},{7,6},{8,9},{9,8},{10,11... | collective-permute-start | bytes 786440 | tf_op jit(solution)/shard_map/ppermute | solution.py:428
  74.4 8.5 %collective-permute-start.11 = (bf16[256,512]{1,0:T(8,128)(2,1)S(1)}, bf16[256,512]{1,0:T(8,128)(2,1)S(1)}, u32[]{:S(2)}, u32[]{:S(2)}) collective-permute-start(bf16[256,512]{1,0:T(8,128)(2,1)S(1)} %get-tuple-element.63), channel_id=1, source_target_pairs={{0,1},{1,0},{2,3},{3,2},{4,5},{5,4},{6,7},{7,6},{8,9},{9,8},{10,11... | collective-permute-start | bytes 786440 | tf_op jit(solution)/shard_map/ppermute | solution.py:428
  74.4 16.8 %all-to-all-start.1 = ((bf16[128,8,128]{2,1,0:T(8,128)(2,1)}), bf16[128,8,128]{2,1,0:T(8,128)(2,1)S(1)}, u32[]{:S(2)}, u32[]{:S(2)}) async-start(bf16[128,8,128]{2,1,0:T(8,128)(2,1)} %bitcast.6), calls=%async_computation.1 | async-start | bytes 524288 | tf_op jit(solution)/shard_map/all_to_all | solution.py:437
  82.9 1.2 %copy-start.4 = (f32[512,512]{1,0:T(8,128)S(1)}, f32[512,512]{1,0:T(8,128)}, u32[]{:S(2)}) copy-start(f32[512,512]{1,0:T(8,128)} %copy-done.3) | copy-start | bytes 3145732
  85.2 5.9 %collective-permute-start.12 = (bf16[256,256]{1,0:T(8,128)(2,1)S(1)}, bf16[256,256]{1,0:T(8,128)(2,1)S(1)}, u32[]{:S(2)}, u32[]{:S(2)}) collective-permute-start(bf16[256,256]{1,0:T(8,128)(2,1)S(1)} %get-tuple-element.66), channel_id=1, source_target_pairs={{0,1},{1,0},{2,3},{3,2},{4,5},{5,4},{6,7},{7,6},{8,9},{9,8},{10,11... | collective-permute-start | bytes 393224 | tf_op jit(solution)/shard_map/ppermute | solution.py:428
  88.8 2.3 %collective-permute-start.13 = (bf16[256,256]{1,0:T(8,128)(2,1)S(1)}, bf16[256,256]{1,0:T(8,128)(2,1)S(1)}, u32[]{:S(2)}, u32[]{:S(2)}) collective-permute-start(bf16[256,256]{1,0:T(8,128)(2,1)S(1)} %get-tuple-element.67), channel_id=1, source_target_pairs={{0,1},{1,0},{2,3},{3,2},{4,5},{5,4},{6,7},{7,6},{8,9},{9,8},{10,11... | collective-permute-start | bytes 393224 | tf_op jit(solution)/shard_map/ppermute | solution.py:428

commit v5 on v4

--- a/solution.py
+++ b/solution.py
@@ -362,7 +362,7 @@
     for g, (back1, back2, their) in enumerate(((b10, b20, their0), (b11, b21, their1))):
         cols = slice(g * 256, (g + 1) * 256)
         total = own[:, cols] + back1[...].astype(F32) + back2[...].astype(F32)
-        mine_ref[:, cols] = total[:ROWS]
+        mine_ref[:, cols] = total[:ROWS].astype(BF)
         their[...] = total[ROWS:].astype(BF)
         dq_ref[:, window(((1 - core) * 2 + g) * 512, 512)] = (dqr0, dqr1)[g][...]
     dq_ref[:, window(core * 1024, 1024)] = dq_own[...]
@@ -375,7 +375,7 @@
         in_specs=[VM] * 8,
         out_specs=[VM] * 4,
         out_shape=[
-            shape((ROWS, 512), F32),
+            shape((ROWS, 512), BF),
             shape((ROWS, 256), BF),
             shape((ROWS, 256), BF),
             shape((ROWS, 2048), BF),
@@ -404,7 +404,7 @@
             for i, out in enumerate((dk_ref, dv_ref)):
                 at = 4 * g + 2 * i
                 if half == 0:
-                    total = mine_ref[:, (2 * g + i) * HEAD : (2 * g + i + 1) * HEAD]
+                    total = mine_ref[:, (2 * g + i) * HEAD : (2 * g + i + 1) * HEAD].astype(F32)
                 else:
                     total = (recv0_ref, recv1_ref)[g][:, i * HEAD : (i + 1) * HEAD].astype(F32)
                 total = total + jnp.where(row == first, share[at : at + 1], 0.0)

time: 93 us -> 93.1 us (level)
  no operation moved by 1% of the time
where the time goes in v5:
time: 93.1 us; the launch traced here: 92.8 us
  starting transfers between devices  40.6 us (44%)
  Pallas kernels  29.9 us (32%)
  waiting for transfers between devices  18.6 us (20%)
  local copies, waits for them, and re-layouts  2.92 us (3%)
    pallas_call x2, Pallas kernels, attend(): pl.pallas_call(functools.partial(attend_kernel, g), in_specs=[VM, HBM, HB...  23.8 us
    all_to_all x2, starting transfers between devices, exchange(): return lax.all_to_all(block, 'ctx', 0, 0, tiled=True)  16 us
    ppermute x8, starting transfers between devices, to_chip(): lax.ppermute(block, 'ctx', [(i, (i + 2 * hops) % size ^ flip) for i in ra...  15.1 us
    ppermute x8, waiting for transfers between devices, to_chip(): lax.ppermute(block, 'ctx', [(i, (i + 2 * hops) % size ^ flip) for i in ra...  10 us
    ppermute x6, starting transfers between devices, to_sibling(): lax.ppermute(block, 'ctx', [(i, i ^ 1) for i in range(lax.axis_size('ctx'...  9.45 us
    all_to_all x2, waiting for transfers between devices, exchange(): return lax.all_to_all(block, 'ctx', 0, 0, tiled=True)  8.6 us
    pallas_call x1, Pallas kernels, pack(): pl.pallas_call(pack_kernel, in_specs=[SM, HBM, HBM, HBM, HBM], out_specs=...  3.15 us
    unnamed x12, local copies, waits for them, and re-layouts  2.88 us
  transfers between devices with their start and end apart: 16, of which 6 were waited for; matrix products, arithmetic and copies ran while one was open for 0% of the time, Pallas kernels for 27%

profile of v5, /device:TPU:1, one launch (start us, length us, event | category | flops | bytes accessed | tf_op | source)
XLA Modules:
  0.0 92.8 jit_solution(4658364739560362621)
XLA Ops:
  0.6 3.2 %pack.1 = (bf16[2,256,256]{2,1,0:T(8,128)(2,1)}, bf16[2,256,256]{2,1,0:T(8,128)(2,1)}, bf16[128,8,128]{2,1,0:T(8,128)(2,1)}, bf16[256,2048]{1,0:T(8,128)(2,1)}) custom-call(s32[256]{0:T(256)} %pos_ref.3, bf16[256,512]{1,0:T(8,128)(2,1)} %k_hbm.1, bf16[256,512]{1,0:T(8,128)(2,1)} %v_hbm.1, bf16[256,2048]{1,0:T(8,128)(2,1)} %q_hbm.5, bf16[256,2048]{1,0:T(8,128)(2,1)} %d_hbm.5), custom_call_target="tpu_custom_call" | custom-call | tf_op jit(solution)/shard_map/pack/pallas_call | solution.py:98
  3.8 1.5 %collective-permute-start.1 = (bf16[2,256,256]{2,1,0:T(8,128)(2,1)}, bf16[2,256,256]{2,1,0:T(8,128)(2,1)S(1)}, u32[]{:S(2)}, u32[]{:S(2)}) collective-permute-start(bf16[2,256,256]{2,1,0:T(8,128)(2,1)} %get-tuple-element.41), channel_id=1, source_target_pairs={{0,1},{1,0},{2,3},{3,2},{4,5},{5,4},{6,7},{7,6},{8,9},{9,8},{10,11... | collective-permute-start | bytes 786440 | tf_op jit(solution)/shard_map/ppermute | solution.py:428
  5.3 0.0 copy-start.5
  5.3 10.2 %all-to-all-start = ((bf16[128,8,128]{2,1,0:T(8,128)(2,1)}), bf16[128,8,128]{2,1,0:T(8,128)(2,1)S(1)}, u32[]{:S(2)}, u32[]{:S(2)}) async-start(bf16[128,8,128]{2,1,0:T(8,128)(2,1)} %get-tuple-element.37), calls=%async_computation | async-start | bytes 524288 | tf_op jit(solution)/shard_map/all_to_all | solution.py:437
  15.5 1.1 %collective-permute-start = (bf16[256,2048]{1,0:T(8,128)(2,1)}, bf16[256,2048]{1,0:T(8,128)(2,1)S(1)}, u32[]{:S(2)}, u32[]{:S(2)}) collective-permute-start(bf16[256,2048]{1,0:T(8,128)(2,1)} %get-tuple-element.39), channel_id=1, source_target_pairs={{0,1},{1,0},{2,3},{3,2},{4,5},{5,4},{6,7},{7,6},{8,9},{9,8},{10,11... | collective-permute-start | bytes 3145736 | tf_op jit(solution)/shard_map/ppermute | solution.py:428
  16.6 0.0 copy-done.5
  16.7 0.0 collective-permute-done.1
  16.7 0.9 collective-permute-start.5
  17.6 2.9 %collective-permute-start.4 = (bf16[512,256]{1,0:T(8,128)(2,1)S(1)}, bf16[512,256]{1,0:T(8,128)(2,1)S(1)}, u32[]{:S(2)}, u32[]{:S(2)}) collective-permute-start(bf16[512,256]{1,0:T(8,128)(2,1)S(1)} %pad_maximum_fusion.1.kv0), channel_id=1, source_target_pairs={{0,4},{1,5},{2,6},{3,7},{4,8},{5,9},{6,10},{7,11},{8,12},{9,13},{1... | collective-permute-start | bytes 786440 | tf_op jit(solution)/shard_map/ppermute | solution.py:433
  20.5 6.3 %all-to-all-done = bf16[128,8,128]{2,1,0:T(8,128)(2,1)S(1)} async-done(((bf16[128,8,128]{2,1,0:T(8,128)(2,1)}), bf16[128,8,128]{2,1,0:T(8,128)(2,1)S(1)}, u32[]{:S(2)}, u32[]{:S(2)}) %all-to-all-start) | async-done | bytes 262176 | tf_op jit(solution)/shard_map/all_to_all | solution.py:437
  26.8 0.0 copy-start.2
  26.8 0.7 copy-done.2
  27.5 0.0 copy-start
  27.5 0.0 copy-start.1
  27.5 0.2 unpack.1
  27.7 0.1 collective-permute-start.3
  27.8 1.8 %collective-permute-start.2 = (bf16[512,256]{1,0:T(8,128)(2,1)S(1)}, bf16[512,256]{1,0:T(8,128)(2,1)S(1)}, u32[]{:S(2)}, u32[]{:S(2)}) collective-permute-start(bf16[512,256]{1,0:T(8,128)(2,1)S(1)} %pad_maximum_fusion.kv0), channel_id=1, source_target_pairs={{0,4},{1,5},{2,6},{3,7},{4,8},{5,9},{6,10},{7,11},{8,12},{9,13},{1... | collective-permute-start | bytes 786440 | tf_op jit(solution)/shard_map/ppermute | solution.py:433
  29.6 6.1 %collective-permute-done.5.kv1 = bf16[512,256]{1,0:T(8,128)(2,1)S(1)} collective-permute-done((bf16[512,256]{1,0:T(8,128)(2,1)S(1)}, bf16[512,256]{1,0:T(8,128)(2,1)S(1)}, u32[]{:S(2)}, u32[]{:S(2)}) %collective-permute-start.5) | collective-permute-done | bytes 262176 | tf_op jit(solution)/shard_map/ppermute | solution.py:433
  35.7 1.2 %collective-permute-done.4.kv2 = bf16[512,256]{1,0:T(8,128)(2,1)S(1)} collective-permute-done((bf16[512,256]{1,0:T(8,128)(2,1)S(1)}, bf16[512,256]{1,0:T(8,128)(2,1)S(1)}, u32[]{:S(2)}, u32[]{:S(2)}) %collective-permute-start.4) | collective-permute-done | bytes 262176 | tf_op jit(solution)/shard_map/ppermute | solution.py:433
  36.9 0.0 collective-permute-done.qd_hbm
  36.9 0.0 copy-done
  36.9 0.0 copy-done.1
  36.9 11.6 %attend.2 = (bf16[256,512]{1,0:T(8,128)(2,1)S(1)}, bf16[256,512]{1,0:T(8,128)(2,1)S(1)}, f32[1024,128]{1,0:T(8,128)S(1)}, f32[512,256]{1,0:T(8,128)S(1)}, bf16[5...) custom-call(f32[256,128]{1,0:T(8,128)S(1)} %get-tuple-element.38.pos_ref, bf16[256,2048]{1,0:T(8,128)(2,1)S(1)} %copy-done, ...), custom_call_target="tpu_custom_call" | custom-call | flops 5000000000 | bytes 4000000 | tf_op jit(solution)/shard_map/attend/pallas_call | solution.py:319
  48.5 2.7 %collective-permute-start.6 = (bf16[512,256]{1,0:T(8,128)(2,1)S(1)}, bf16[512,256]{1,0:T(8,128)(2,1)S(1)}, u32[]{:S(2)}, u32[]{:S(2)}) collective-permute-start(bf16[512,256]{1,0:T(8,128)(2,1)S(1)} %get-tuple-element.53), channel_id=1, source_target_pairs={{0,126},{1,127},{2,0},{3,1},{4,2},{5,3},{6,4},{7,5},{8,6},{9,7},{1... | collective-permute-start | bytes 786440 | tf_op jit(solution)/shard_map/ppermute | solution.py:433
  51.2 5.8 %collective-permute-start.7 = (bf16[512,256]{1,0:T(8,128)(2,1)S(1)}, bf16[512,256]{1,0:T(8,128)(2,1)S(1)}, u32[]{:S(2)}, u32[]{:S(2)}) collective-permute-start(bf16[512,256]{1,0:T(8,128)(2,1)S(1)} %get-tuple-element.54), channel_id=1, source_target_pairs={{0,124},{1,125},{2,126},{3,127},{4,0},{5,1},{6,2},{7,3},{8,4},{9,5... | collective-permute-start | bytes 786440 | tf_op jit(solution)/shard_map/ppermute | solution.py:433
  57.0 0.0 collective-permute-done.3.kv1
  57.0 0.0 collective-permute-done.2.kv2
  57.0 12.2 %attend.3 = (bf16[256,1024]{1,0:T(8,128)(2,1)S(1)}, bf16[256,512]{1,0:T(8,128)(2,1)S(1)}, bf16[1024,128]{1,0:T(8,128)(2,1)}, f32[512,512]{1,0:T(8,128)S(1)}, bf1...) custom-call(f32[256,128]{1,0:T(8,128)S(1)} %get-tuple-element.38.pos_ref, bf16[256,2048]{1,0:T(8,128)(2,1)S(1)} %copy-done, ...), custom_call_target="tpu_custom_call" | custom-call | flops 5000000000 | bytes 4000000 | tf_op jit(solution)/shard_map/attend/pallas_call | solution.py:319
  69.2 0.0 copy-start.3
  69.2 1.0 %copy-done.3 = f32[512,512]{1,0:T(8,128)} copy-done((f32[512,512]{1,0:T(8,128)}, f32[512,512]{1,0:T(8,128)S(1)}, u32[]{:S(2)}) %copy-start.3) | copy-done | bytes 1048600
  70.2 0.0 collective-permute-done.6.b10
  70.2 0.0 collective-permute-done.7.b20
  70.2 0.9 collective-permute-start.8
  71.1 0.0 collective-permute-start.9
  71.1 3.3 %collective-permute-start.10 = (bf16[256,512]{1,0:T(8,128)(2,1)S(1)}, bf16[256,512]{1,0:T(8,128)(2,1)S(1)}, u32[]{:S(2)}, u32[]{:S(2)}) collective-permute-start(bf16[256,512]{1,0:T(8,128)(2,1)S(1)} %get-tuple-element.62), channel_id=1, source_target_pairs={{0,1},{1,0},{2,3},{3,2},{4,5},{5,4},{6,7},{7,6},{8,9},{9,8},{10,11... | collective-permute-start | bytes 786440 | tf_op jit(solution)/shard_map/ppermute | solution.py:428
  74.4 0.0 collective-permute-start.11
  74.4 5.8 %all-to-all-start.1 = ((bf16[128,8,128]{2,1,0:T(8,128)(2,1)}), bf16[128,8,128]{2,1,0:T(8,128)(2,1)S(1)}, u32[]{:S(2)}, u32[]{:S(2)}) async-start(bf16[128,8,128]{2,1,0:T(8,128)(2,1)} %bitcast.6), calls=%async_computation.1 | async-start | bytes 524288 | tf_op jit(solution)/shard_map/all_to_all | solution.py:437
  80.2 1.3 %collective-permute-done.8.b11 = bf16[512,256]{1,0:T(8,128)(2,1)S(1)} collective-permute-done((bf16[512,256]{1,0:T(8,128)(2,1)S(1)}, bf16[512,256]{1,0:T(8,128)(2,1)S(1)}, u32[]{:S(2)}, u32[]{:S(2)}) %collective-permute-start.8) | collective-permute-done | bytes 262176 | tf_op jit(solution)/shard_map/ppermute | solution.py:433
  81.5 1.4 %collective-permute-done.9.b21 = bf16[512,256]{1,0:T(8,128)(2,1)S(1)} collective-permute-done((bf16[512,256]{1,0:T(8,128)(2,1)S(1)}, bf16[512,256]{1,0:T(8,128)(2,1)S(1)}, u32[]{:S(2)}, u32[]{:S(2)}) %collective-permute-start.9) | collective-permute-done | bytes 262176 | tf_op jit(solution)/shard_map/ppermute | solution.py:433
  82.9 0.0 collective-permute-done.10.dqr0
  82.9 0.0 collective-permute-done.11.dqr1
  82.9 0.0 copy-start.4
  82.9 1.2 %copy-done.4 = f32[512,512]{1,0:T(8,128)S(1)} copy-done((f32[512,512]{1,0:T(8,128)S(1)}, f32[512,512]{1,0:T(8,128)}, u32[]{:S(2)}) %copy-start.4) | copy-done | bytes 1048600
  84.1 1.1 %gather.1 = (bf16[256,512]{1,0:T(8,128)(2,1)S(1)}, bf16[256,256]{1,0:T(8,128)(2,1)S(1)}, bf16[256,256]{1,0:T(8,128)(2,1)S(1)}, bf16[256,2048]{1,0:T(8,128)(2,1)}) custom-call(f32[512,512]{1,0:T(8,128)S(1)} %copy-done.4, bf16[512,256]{1,0:T(8,128)(2,1)S(1)} %collective-permute-done.6.b10, bf16[512,256]{1,0:T(8,128)(2,1)S(1)} %collective-permute-done.7.b20, ...), custom_call_target="tpu_custom_call" | custom-call | flops 6000000000 | bytes 6000000 | tf_op jit(solution)/shard_map/gather/pallas_call | solution.py:373
  85.2 3.5 %collective-permute-start.12 = (bf16[256,256]{1,0:T(8,128)(2,1)S(1)}, bf16[256,256]{1,0:T(8,128)(2,1)S(1)}, u32[]{:S(2)}, u32[]{:S(2)}) collective-permute-start(bf16[256,256]{1,0:T(8,128)(2,1)S(1)} %get-tuple-element.66), channel_id=1, source_target_pairs={{0,1},{1,0},{2,3},{3,2},{4,5},{5,4},{6,7},{7,6},{8,9},{9,8},{10,11... | collective-permute-start | bytes 393224 | tf_op jit(solution)/shard_map/ppermute | solution.py:428
  88.8 0.0 collective-permute-start.13
  88.8 2.3 %all-to-all-done.1.share_ref = bf16[128,8,128]{2,1,0:T(8,128)(2,1)S(1)} async-done(((bf16[128,8,128]{2,1,0:T(8,128)(2,1)}), bf16[128,8,128]{2,1,0:T(8,128)(2,1)S(1)}, u32[]{:S(2)}, u32[]{:S(2)}) %all-to-all-start.1) | async-done | bytes 262176 | tf_op jit(solution)/shard_map/all_to_all | solution.py:437
  91.1 0.0 collective-permute-done.12.recv0_ref
  91.1 0.0 collective-permute-done.13.recv1_ref
  91.1 1.6 %finish.1 = (bf16[256,512]{1,0:T(8,128)(2,1)}, bf16[256,512]{1,0:T(8,128)(2,1)}) custom-call(s32[256]{0:T(256)S(1)} %copy-done.2, bf16[256,512]{1,0:T(8,128)(2,1)S(1)} %get-tuple-element.65.mine_ref, bf16[256,256]{1,0:T(8,128)(2,1)S(1)} %collective-permute-done.12.recv0_ref, bf16[256,256]{1,0:T(8,128)(2,1)S(1)} %collective-permute-done.13.recv1_ref, ...), custom_call_target="tpu_custom_call" | custom-call | tf_op jit(solution)/shard_map/finish/pallas_call | solution.py:417
  (4 shorter events, 0.1 us)
Async XLA Ops:
  3.8 12.9 %collective-permute-start.1 = (bf16[2,256,256]{2,1,0:T(8,128)(2,1)}, bf16[2,256,256]{2,1,0:T(8,128)(2,1)S(1)}, u32[]{:S(2)}, u32[]{:S(2)}) collective-permute-start(bf16[2,256,256]{2,1,0:T(8,128)(2,1)} %get-tuple-element.41), channel_id=1, source_target_pairs={{0,1},{1,0},{2,3},{3,2},{4,5},{5,4},{6,7},{7,6},{8,9},{9,8},{10,11... | collective-permute-start | bytes 786440 | tf_op jit(solution)/shard_map/ppermute | solution.py:428
  5.3 11.3 %copy-start.5 = (bf16[2,256,256]{2,1,0:T(8,128)(2,1)S(1)}, bf16[2,256,256]{2,1,0:T(8,128)(2,1)}, u32[]{:S(2)}) copy-start(bf16[2,256,256]{2,1,0:T(8,128)(2,1)} %get-tuple-element.40) | copy-start | bytes 786436
  5.3 21.5 %all-to-all-start = ((bf16[128,8,128]{2,1,0:T(8,128)(2,1)}), bf16[128,8,128]{2,1,0:T(8,128)(2,1)S(1)}, u32[]{:S(2)}, u32[]{:S(2)}) async-start(bf16[128,8,128]{2,1,0:T(8,128)(2,1)} %get-tuple-element.37), calls=%async_computation | async-start | bytes 524288 | tf_op jit(solution)/shard_map/all_to_all | solution.py:437
  15.5 21.4 %collective-permute-start = (bf16[256,2048]{1,0:T(8,128)(2,1)}, bf16[256,2048]{1,0:T(8,128)(2,1)S(1)}, u32[]{:S(2)}, u32[]{:S(2)}) collective-permute-start(bf16[256,2048]{1,0:T(8,128)(2,1)} %get-tuple-element.39), channel_id=1, source_target_pairs={{0,1},{1,0},{2,3},{3,2},{4,5},{5,4},{6,7},{7,6},{8,9},{9,8},{10,11... | collective-permute-start | bytes 3145736 | tf_op jit(solution)/shard_map/ppermute | solution.py:428
  16.7 19.0 %collective-permute-start.5 = (bf16[512,256]{1,0:T(8,128)(2,1)S(1)}, bf16[512,256]{1,0:T(8,128)(2,1)S(1)}, u32[]{:S(2)}, u32[]{:S(2)}) collective-permute-start(bf16[512,256]{1,0:T(8,128)(2,1)S(1)} %pad_maximum_fusion.1.kv0), channel_id=1, source_target_pairs={{0,2},{1,3},{2,4},{3,5},{4,6},{5,7},{6,8},{7,9},{8,10},{9,11},{10,... | collective-permute-start | bytes 786440 | tf_op jit(solution)/shard_map/ppermute | solution.py:433
  17.6 19.3 %collective-permute-start.4 = (bf16[512,256]{1,0:T(8,128)(2,1)S(1)}, bf16[512,256]{1,0:T(8,128)(2,1)S(1)}, u32[]{:S(2)}, u32[]{:S(2)}) collective-permute-start(bf16[512,256]{1,0:T(8,128)(2,1)S(1)} %pad_maximum_fusion.1.kv0), channel_id=1, source_target_pairs={{0,4},{1,5},{2,6},{3,7},{4,8},{5,9},{6,10},{7,11},{8,12},{9,13},{1... | collective-permute-start | bytes 786440 | tf_op jit(solution)/shard_map/ppermute | solution.py:433
  26.8 0.7 copy-start.2
  27.5 9.4 %copy-start = (bf16[256,2048]{1,0:T(8,128)(2,1)S(1)}, bf16[256,2048]{1,0:T(8,128)(2,1)}, u32[]{:S(2)}) copy-start(bf16[256,2048]{1,0:T(8,128)(2,1)} %q_hbm.5) | copy-start | bytes 3145732
  27.5 9.4 %copy-start.1 = (bf16[256,2048]{1,0:T(8,128)(2,1)S(1)}, bf16[256,2048]{1,0:T(8,128)(2,1)}, u32[]{:S(2)}) copy-start(bf16[256,2048]{1,0:T(8,128)(2,1)} %d_hbm.5) | copy-start | bytes 3145732
  27.7 29.3 %collective-permute-start.3 = (bf16[512,256]{1,0:T(8,128)(2,1)S(1)}, bf16[512,256]{1,0:T(8,128)(2,1)S(1)}, u32[]{:S(2)}, u32[]{:S(2)}) collective-permute-start(bf16[512,256]{1,0:T(8,128)(2,1)S(1)} %pad_maximum_fusion.kv0), channel_id=1, source_target_pairs={{0,2},{1,3},{2,4},{3,5},{4,6},{5,7},{6,8},{7,9},{8,10},{9,11},{10,... | collective-permute-start | bytes 786440 | tf_op jit(solution)/shard_map/ppermute | solution.py:433
  27.8 29.2 %collective-permute-start.2 = (bf16[512,256]{1,0:T(8,128)(2,1)S(1)}, bf16[512,256]{1,0:T(8,128)(2,1)S(1)}, u32[]{:S(2)}, u32[]{:S(2)}) collective-permute-start(bf16[512,256]{1,0:T(8,128)(2,1)S(1)} %pad_maximum_fusion.kv0), channel_id=1, source_target_pairs={{0,4},{1,5},{2,6},{3,7},{4,8},{5,9},{6,10},{7,11},{8,12},{9,13},{1... | collective-permute-start | bytes 786440 | tf_op jit(solution)/shard_map/ppermute | solution.py:433
  48.5 21.7 %collective-permute-start.6 = (bf16[512,256]{1,0:T(8,128)(2,1)S(1)}, bf16[512,256]{1,0:T(8,128)(2,1)S(1)}, u32[]{:S(2)}, u32[]{:S(2)}) collective-permute-start(bf16[512,256]{1,0:T(8,128)(2,1)S(1)} %get-tuple-element.53), channel_id=1, source_target_pairs={{0,126},{1,127},{2,0},{3,1},{4,2},{5,3},{6,4},{7,5},{8,6},{9,7},{1... | collective-permute-start | bytes 786440 | tf_op jit(solution)/shard_map/ppermute | solution.py:433
  51.2 19.0 %collective-permute-start.7 = (bf16[512,256]{1,0:T(8,128)(2,1)S(1)}, bf16[512,256]{1,0:T(8,128)(2,1)S(1)}, u32[]{:S(2)}, u32[]{:S(2)}) collective-permute-start(bf16[512,256]{1,0:T(8,128)(2,1)S(1)} %get-tuple-element.54), channel_id=1, source_target_pairs={{0,124},{1,125},{2,126},{3,127},{4,0},{5,1},{6,2},{7,3},{8,4},{9,5... | collective-permute-start | bytes 786440 | tf_op jit(solution)/shard_map/ppermute | solution.py:433
  69.2 1.0 %copy-start.3 = (f32[512,512]{1,0:T(8,128)}, f32[512,512]{1,0:T(8,128)S(1)}, u32[]{:S(2)}) copy-start(f32[512,512]{1,0:T(8,128)S(1)} %get-tuple-element.56.own) | copy-start | bytes 3145732
  70.2 11.3 %collective-permute-start.8 = (bf16[512,256]{1,0:T(8,128)(2,1)S(1)}, bf16[512,256]{1,0:T(8,128)(2,1)S(1)}, u32[]{:S(2)}, u32[]{:S(2)}) collective-permute-start(bf16[512,256]{1,0:T(8,128)(2,1)S(1)} %get-tuple-element.59), channel_id=1, source_target_pairs={{0,126},{1,127},{2,0},{3,1},{4,2},{5,3},{6,4},{7,5},{8,6},{9,7},{1... | collective-permute-start | bytes 786440 | tf_op jit(solution)/shard_map/ppermute | solution.py:433
  71.1 11.8 %collective-permute-start.9 = (bf16[512,256]{1,0:T(8,128)(2,1)S(1)}, bf16[512,256]{1,0:T(8,128)(2,1)S(1)}, u32[]{:S(2)}, u32[]{:S(2)}) collective-permute-start(bf16[512,256]{1,0:T(8,128)(2,1)S(1)} %get-tuple-element.60), channel_id=1, source_target_pairs={{0,124},{1,125},{2,126},{3,127},{4,0},{5,1},{6,2},{7,3},{8,4},{9,5... | collective-permute-start | bytes 786440 | tf_op jit(solution)/shard_map/ppermute | solution.py:433
  71.1 11.8 %collective-permute-start.10 = (bf16[256,512]{1,0:T(8,128)(2,1)S(1)}, bf16[256,512]{1,0:T(8,128)(2,1)S(1)}, u32[]{:S(2)}, u32[]{:S(2)}) collective-permute-start(bf16[256,512]{1,0:T(8,128)(2,1)S(1)} %get-tuple-element.62), channel_id=1, source_target_pairs={{0,1},{1,0},{2,3},{3,2},{4,5},{5,4},{6,7},{7,6},{8,9},{9,8},{10,11... | collective-permute-start | bytes 786440 | tf_op jit(solution)/shard_map/ppermute | solution.py:428
  74.4 8.5 %collective-permute-start.11 = (bf16[256,512]{1,0:T(8,128)(2,1)S(1)}, bf16[256,512]{1,0:T(8,128)(2,1)S(1)}, u32[]{:S(2)}, u32[]{:S(2)}) collective-permute-start(bf16[256,512]{1,0:T(8,128)(2,1)S(1)} %get-tuple-element.63), channel_id=1, source_target_pairs={{0,1},{1,0},{2,3},{3,2},{4,5},{5,4},{6,7},{7,6},{8,9},{9,8},{10,11... | collective-permute-start | bytes 786440 | tf_op jit(solution)/shard_map/ppermute | solution.py:428
  74.4 16.8 %all-to-all-start.1 = ((bf16[128,8,128]{2,1,0:T(8,128)(2,1)}), bf16[128,8,128]{2,1,0:T(8,128)(2,1)S(1)}, u32[]{:S(2)}, u32[]{:S(2)}) async-start(bf16[128,8,128]{2,1,0:T(8,128)(2,1)} %bitcast.6), calls=%async_computation.1 | async-start | bytes 524288 | tf_op jit(solution)/shard_map/all_to_all | solution.py:437
  82.9 1.2 %copy-start.4 = (f32[512,512]{1,0:T(8,128)S(1)}, f32[512,512]{1,0:T(8,128)}, u32[]{:S(2)}) copy-start(f32[512,512]{1,0:T(8,128)} %copy-done.3) | copy-start | bytes 3145732
  85.2 5.9 %collective-permute-start.12 = (bf16[256,256]{1,0:T(8,128)(2,1)S(1)}, bf16[256,256]{1,0:T(8,128)(2,1)S(1)}, u32[]{:S(2)}, u32[]{:S(2)}) collective-permute-start(bf16[256,256]{1,0:T(8,128)(2,1)S(1)} %get-tuple-element.66), channel_id=1, source_target_pairs={{0,1},{1,0},{2,3},{3,2},{4,5},{5,4},{6,7},{7,6},{8,9},{9,8},{10,11... | collective-permute-start | bytes 393224 | tf_op jit(solution)/shard_map/ppermute | solution.py:428
  88.8 2.3 %collective-permute-start.13 = (bf16[256,256]{1,0:T(8,128)(2,1)S(1)}, bf16[256,256]{1,0:T(8,128)(2,1)S(1)}, u32[]{:S(2)}, u32[]{:S(2)}) collective-permute-start(bf16[256,256]{1,0:T(8,128)(2,1)S(1)} %get-tuple-element.67), channel_id=1, source_target_pairs={{0,1},{1,0},{2,3},{3,2},{4,5},{5,4},{6,7},{7,6},{8,9},{9,8},{10,11... | collective-permute-start | bytes 393224 | tf_op jit(solution)/shard_map/ppermute | solution.py:428
